TPU v7x, 128 devices: a whole 4x4x4 slice. The times are simulated.
128 devices in a mesh: req: 16 (over z, x_hi, core), head: 8 (over y, x_lo).
Axes of the slice: x: 4 (x_hi: 2, x_lo: 2; x = x_hi * 2 + x_lo), y: 4, z: 4, core: 2. Of those that a mesh axis runs over, the one named last changes fastest.
Arguments:
- hidden_in: bfloat16 [128, 8192], P('head', 'req'), may hold values from -40 to 40
- attn_gain: bfloat16 [8192], P('req'), may hold values from 0.5 to 1.5
- w_qkv: bfloat16 [8192, 10240], P('req', 'head'), may hold values from -0.0625 to 0.0625
- w_out: bfloat16 [8192, 8192], P('head', 'req'), may hold values from -0.0625 to 0.0625
- k_cache: bfloat16 [128, 4096, 1024], P('req', None, 'head'), may hold values from -400 to 400
- v_cache: bfloat16 [128, 4096, 1024], P('req', None, 'head'), may hold values from -6 to 6
- lengths: int32 [128], P('req'), may hold values from 1 to 4096, 135168 in all
Outputs:
- hidden_out: bfloat16 [128, 8192], P('head', 'req')
Inputs may be any that keep to these rules, and one draw needn't show every extreme that they name: One request holds exactly 4096 tokens; the lengths add up to 135168.
All inputs are finite; a program needn't handle non-finite values. No bound on the sum of `lengths` on one device may be relied on, other than what follows from the above.
Results may differ from a plain program's by a relative error of at most 0.0055.
Values may be sent and summed in bfloat16 or wider, within the bound.
A program may use at most 64 MiB of HBM per device.

v0:
```python
import jax
import jax.numpy as jnp
from jax import lax
from jax.sharding import PartitionSpec as P

D = 8192
GROUP = 8
HD = 128


epsilon = 1e-05
rope_base = 500000.0


def rotate(vectors, positions):
    halfway = vectors.shape[-1] // 2
    frequency = jnp.exp(
        -jnp.log(rope_base) * 2.0 * jnp.arange(halfway, dtype=jnp.float32) / vectors.shape[-1]
    )
    angles = positions.astype(jnp.float32)[:, None] * frequency[None, :]
    target_shape = (angles.shape[0],) + (1,) * (vectors.ndim - 2) + (halfway,)
    cosine = jnp.cos(angles).reshape(target_shape)
    sine_part = jnp.sin(angles).reshape(target_shape)
    first = vectors[..., :halfway]
    second = vectors[..., halfway:]
    return jnp.concatenate(
        [first * cosine - second * sine_part, second * cosine + first * sine_part], axis=-1
    )


def own_part(own_score, running, totals, new_values):
    own_prob = lax.optimization_barrier(
        (jnp.exp(own_score - running) / totals).astype(jnp.bfloat16)
    )
    return own_prob.astype(jnp.float32)[..., None] * new_values.astype(jnp.float32)[:, :, None, :]


def attend_padded(queries, new_keys, new_values, cached_keys, cached_values, lengths, factor):
    slots = cached_keys.shape[1]
    inside = jnp.arange(slots, dtype=jnp.int32)[None, :] < lengths[:, None]
    scores = (
        jnp.einsum("rkgd,rpkd->rkgp", queries, cached_keys, preferred_element_type=jnp.float32)
        * factor
    )
    scores = jnp.where(inside[:, None, None, :], scores, -1e30)
    own_score = (
        jnp.einsum("rkgd,rkd->rkg", queries, new_keys, preferred_element_type=jnp.float32) * factor
    )
    running = jnp.maximum(jnp.max(scores, axis=3), own_score)
    weights = jnp.where(inside[:, None, None, :], jnp.exp(scores - running[..., None]), 0.0)
    totals = jnp.sum(weights, axis=3) + jnp.exp(own_score - running)
    probs = (weights / totals[..., None]).astype(jnp.bfloat16)
    mixed = jnp.einsum("rkgp,rpkd->rkgd", probs, cached_values, preferred_element_type=jnp.float32)
    mixed = mixed + own_part(own_score, running, totals, new_values)
    return mixed.astype(jnp.bfloat16)


def local(hidden_in, attn_gain, w_qkv, w_out, k_cache, v_cache, lengths):
    states = hidden_in.astype(jnp.float32)
    local_square = jnp.sum(states * states, axis=1)
    summed_square = lax.psum(local_square, "req")
    mean_square = summed_square / D
    normed = (
        states * lax.rsqrt(mean_square + epsilon)[:, None] * attn_gain.astype(jnp.float32)[None, :]
    ).astype(jnp.bfloat16)
    every_row = lax.all_gather(normed, "head", axis=0, tiled=True)
    own_count = k_cache.shape[0]
    slots = k_cache.shape[1]
    local_heads = k_cache.shape[2] // HD
    whole_sum = lax.psum(jnp.dot(every_row, w_qkv, preferred_element_type=jnp.float32), "req")
    projected = lax.dynamic_slice_in_dim(whole_sum, lax.axis_index("req") * own_count, own_count, 0)
    projected = projected.reshape(own_count, local_heads, GROUP + 2, HD)
    queries = rotate(projected[:, :, :GROUP], lengths).astype(jnp.bfloat16)
    new_keys = rotate(projected[:, :, GROUP], lengths).astype(jnp.bfloat16)
    new_values = projected[:, :, GROUP + 1].astype(jnp.bfloat16)
    cached_keys = k_cache.reshape(own_count, slots, local_heads, HD)
    cached_values = v_cache.reshape(own_count, slots, local_heads, HD)
    factor = HD ** (-0.5)
    attended = attend_padded(
        queries, new_keys, new_values, cached_keys, cached_values, lengths, factor
    )
    flat_rows = attended.reshape(own_count, local_heads * GROUP * HD)
    gathered = lax.all_gather(flat_rows, "req", axis=0, tiled=True)
    output = lax.psum_scatter(
        jnp.dot(gathered, w_out, preferred_element_type=jnp.float32),
        "head",
        scatter_dimension=0,
        tiled=True,
    )
    return (states + output).astype(jnp.bfloat16)


def solution(mesh):
    return jax.shard_map(
        local,
        mesh=mesh,
        in_specs=(
            P("head", "req"),
            P("req"),
            P("req", "head"),
            P("head", "req"),
            P("req", None, "head"),
            P("req", None, "head"),
            P("req"),
        ),
        out_specs=P("head", "req"),
        check_vma=False,
    )
```

profile of v0, /device:TPU:1, one launch (start us, length us, event | category | flops | bytes accessed | tf_op | source)
XLA Modules:
  0.0 284.6 jit_solution(3580849539838638522)
XLA Ops:
  6.5 0.0 copy-start
  6.5 0.0 all-reduce.2.cloned.1.call-start
  6.5 0.8 convert_element_type.49
  7.3 0.8 fusion.8
  8.2 35.3 %psum.14 = f32[16]{0:T(128)S(1)} all-reduce(f32[16]{0:T(128)S(1)} %fusion.8), channel_id=1, replica_groups=mesh['req'=16,'head'=8] {'req'}, use_global_device_ids=true, to_apply=%region_1.0 | all-reduce | flops 16 | bytes 128 | tf_op jit(solution)/shard_map/psum | solution.py:61
  43.4 0.8 fusion.10
  44.2 22.6 %all_gather.6 = bf16[128,512]{1,0:T(8,128)(2,1)S(1)} all-gather(bf16[16,512]{1,0:T(8,128)(2,1)S(1)} %fusion.10), channel_id=1, replica_groups=mesh['req'=16,'head'=8] {'head'}, dimensions={0}, use_global_device_ids=true | all-gather | bytes 147456 | tf_op jit(solution)/shard_map/all_gather | solution.py:66
  66.8 0.0 copy-done
  66.8 1.2 fusion.35
  68.0 0.0 all-reduce.2.cloned.1.call-update
  68.0 0.0 reduce-scatter.2.cloned.1.call-start
  68.1 0.7 convert_element_type.51
  68.8 0.1 multiply_cosine_fusion.1
  68.9 0.7 iota_compare_fusion
  69.6 144.3 %all-reduce.2.cloned.1.call-done = f32[128,1280]{1,0:T(8,128)} async-done(((f32[128,1280]{1,0:T(8,128)}), f32[128,1280]{1,0:T(8,128)}) %all-reduce.2.cloned.1.call-update) | async-done | bytes 655376 | tf_op jit(solution)/shard_map/psum | solution.py:70
  213.9 0.0 copy-start.1
  213.9 0.9 dynamic-slice_bitcast_fusion
  214.8 0.1 fusion.33
  214.9 0.1 fusion.28
  215.0 0.1 maximum_bitcast_fusion
  215.1 0.2 fusion.22
  215.3 6.1 %fusion.34 = (f32[8,8]{1,0:T(8,128)S(1)}, f32[8,8,4096]{2,1,0:T(8,128)S(1)}) fusion(bf16[8,4096,128]{2,1,0:T(8,128)(2,1)} %param.11, bf16[8,8,64]{2,1,0:T(8,128)(2,1)S(1)} %get-tuple-element.6, bf16[8,8,64]{2,1,0:T(8,128)(2,1)S(1)} %get-tuple-element.5, pred[8,4096]{1,0:T(8,128)(4,1)S(1)} %iota_compare_fusion), kind=kOutput, calls=%fused_computation.60 | convolution fusion | flops 67928000 | bytes 9486592 | tf_op jit(solution)/shard_map/rkgd,rpkd->rkgp/dot_general | solution.py:42
  221.5 0.4 fusion.3
  221.9 0.0 copy-done.1
  221.9 0.0 copy-start.2
  221.9 0.0 copy-start.3
  222.0 1.3 fusion.2
  223.3 22.1 %all_gather.7 = bf16[128,1024]{1,0:T(8,128)(2,1)S(1)} all-gather(bf16[8,1024]{1,0:T(8,128)(2,1)S(1)} %bitcast.37), channel_id=1, replica_groups=mesh['req'=16,'head'=8] {'req'}, dimensions={0}, use_global_device_ids=true | all-gather | bytes 278528 | tf_op jit(solution)/shard_map/all_gather | solution.py:83
  245.4 0.0 copy-done.2
  245.4 1.0 fusion.36
  246.4 0.0 reduce-scatter.2.cloned.1.call-update
  246.5 29.9 %reduce-scatter.2.cloned.1.call-done = f32[16,512]{1,0:T(8,128)} async-done(((f32[128,512]{1,0:T(8,128)}), f32[16,512]{1,0:T(8,128)}) %reduce-scatter.2.cloned.1.call-update) | async-done | bytes 32784 | tf_op jit(solution)/shard_map/reduce_scatter | solution.py:84
  276.4 0.0 copy-done.3
  276.4 1.4 fusion.11
  (9 shorter events, 0.1 us)
Async XLA Ops:
  6.5 60.3 %copy-start = (bf16[512,1280]{1,0:T(8,128)(2,1)S(1)}, bf16[512,1280]{1,0:T(8,128)(2,1)}, u32[]{:S(2)}) copy-start(bf16[512,1280]{1,0:T(8,128)(2,1)} %param.9) | copy-start | bytes 3932164
  6.5 207.4 %all-reduce.2.cloned.1.call-start = ((), (), s32[]{:S(2)}) async-start(), calls=%async_computation.1 | async-start | bytes 1310720 | tf_op jit(solution)/shard_map/psum | solution.py:70
  68.0 208.3 %reduce-scatter.2.cloned.1.call-start = ((), (), s32[]{:S(2)}) async-start(), calls=%async_computation.2 | async-start | bytes 294912 | tf_op jit(solution)/shard_map/reduce_scatter | solution.py:84
  213.9 8.0 %copy-start.1 = (bf16[8,4096,128]{2,1,0:T(8,128)(2,1)S(1)}, bf16[8,4096,128]{2,1,0:T(8,128)(2,1)}, u32[]{:S(2)}) copy-start(bf16[8,4096,128]{2,1,0:T(8,128)(2,1)} %param.12) | copy-start | bytes 25165828
  221.9 23.5 %copy-start.2 = (bf16[1024,512]{1,0:T(8,128)(2,1)S(1)}, bf16[1024,512]{1,0:T(8,128)(2,1)}, u32[]{:S(2)}) copy-start(bf16[1024,512]{1,0:T(8,128)(2,1)} %param.10) | copy-start | bytes 3145732
  221.9 54.4 %copy-start.3 = (bf16[16,512]{1,0:T(8,128)(2,1)S(1)}, bf16[16,512]{1,0:T(8,128)(2,1)}, u32[]{:S(2)}) copy-start(bf16[16,512]{1,0:T(8,128)(2,1)} %param.7) | copy-start | bytes 49156
Sparse Core Ops, SparseCore 0:
  68.2 145.7 all-reduce.1
  246.6 29.7 reduce-scatter.1
where the time goes:
time: 289 us; the launch traced here: 285 us
  waiting for transfers between devices  174 us (60%)
  blocking collectives  79.9 us (28%)
  between operations  13.5 us (5%)
  matrix products  9.89 us (3%)
  other arithmetic  5.97 us (2%)
    psum x1, waiting for transfers between devices, local(): lax.psum(jnp.dot(every_row, w_qkv, preferred_element_type=jnp.float32), '...  144 us
    psum x1, blocking collectives, local(): summed_square = lax.psum(local_square, 'req')  35.3 us
    reduce_scatter x1, waiting for transfers between devices, local(): lax.psum_scatter(jnp.dot(gathered, w_out, preferred_element_type=jnp.floa...  29.9 us
    all_gather x1, blocking collectives, local(): every_row = lax.all_gather(normed, 'head', axis=0, tiled=True)  22.6 us
    all_gather x1, blocking collectives, local(): gathered = lax.all_gather(flat_rows, 'req', axis=0, tiled=True)  22.1 us
    dot_general x1, matrix products, attend_padded(): jnp.einsum('rkgd,rpkd->rkgp', queries, cached_keys, preferred_element_typ...  6.13 us
  transfers between devices with their start and end apart: 2, of which 2 were waited for; matrix products, arithmetic and copies ran while one was open for 1% of the time, Pallas kernels for 0%

commit v1 on v0

--- a/solution.py
+++ b/solution.py
@@ -57,18 +57,20 @@
 
 def local(hidden_in, attn_gain, w_qkv, w_out, k_cache, v_cache, lengths):
     states = hidden_in.astype(jnp.float32)
-    local_square = jnp.sum(states * states, axis=1)
-    summed_square = lax.psum(local_square, "req")
-    mean_square = summed_square / D
-    normed = (
-        states * lax.rsqrt(mean_square + epsilon)[:, None] * attn_gain.astype(jnp.float32)[None, :]
-    ).astype(jnp.bfloat16)
-    every_row = lax.all_gather(normed, "head", axis=0, tiled=True)
+    every_row = lax.all_gather(hidden_in, "head", axis=0, tiled=True).astype(jnp.float32)
+    scaled = (every_row * attn_gain.astype(jnp.float32)[None, :]).astype(jnp.bfloat16)
+    partial_square = jnp.sum(every_row * every_row, axis=1)
+    partial = jnp.dot(scaled, w_qkv, preferred_element_type=jnp.float32)
+    columns = partial.shape[1]
+    packed = jnp.concatenate(
+        [partial, jnp.broadcast_to(partial_square[:, None], (partial.shape[0], 128))], axis=1
+    )
+    summed = lax.psum_scatter(packed, "req", scatter_dimension=0, tiled=True)
+    mean_square = summed[:, columns] / D
     own_count = k_cache.shape[0]
     slots = k_cache.shape[1]
     local_heads = k_cache.shape[2] // HD
-    whole_sum = lax.psum(jnp.dot(every_row, w_qkv, preferred_element_type=jnp.float32), "req")
-    projected = lax.dynamic_slice_in_dim(whole_sum, lax.axis_index("req") * own_count, own_count, 0)
+    projected = summed[:, :columns] * lax.rsqrt(mean_square + epsilon)[:, None]
     projected = projected.reshape(own_count, local_heads, GROUP + 2, HD)
     queries = rotate(projected[:, :, :GROUP], lengths).astype(jnp.bfloat16)
     new_keys = rotate(projected[:, :, GROUP], lengths).astype(jnp.bfloat16)

time: 289 us -> 256 us (0.89)
  blocking collectives: 79.9 us -> 48.3 us
  waiting for transfers between devices: 174 us -> 171 us
    psum x1 -> x0, waiting for transfers between devices: 144 us -> none  [local(): lax.psum(jnp.dot(every_row, w_qkv, preferred_element_type=jnp.float32), '...]
    unnamed x2 -> x3, waiting for transfers between devices: 0.03 us -> 141 us
    psum x1 -> x0, blocking collectives: 35.3 us -> none  [local(): summed_square = lax.psum(local_square, 'req')]
where the time goes in v1:
time: 256 us; the launch traced here: 251 us
  waiting for transfers between devices  171 us (67%)
  blocking collectives  48.3 us (19%)
  between operations  14.1 us (6%)
  matrix products  8.66 us (3%)
  other arithmetic  7.35 us (3%)
    unnamed x3, waiting for transfers between devices  141 us
    reduce_scatter x1, waiting for transfers between devices, local(): lax.psum_scatter(jnp.dot(gathered, w_out, preferred_element_type=jnp.floa...  30.7 us
    all_gather x1, blocking collectives, local(): gathered = lax.all_gather(flat_rows, 'req', axis=0, tiled=True)  24.5 us
    all_gather x1, blocking collectives, local(): lax.all_gather(hidden_in, 'head', axis=0, tiled=True).astype(jnp.float32)  23.8 us
    dot_general x1, matrix products, attend_padded(): jnp.einsum('rkgd,rpkd->rkgp', queries, cached_keys, preferred_element_typ...  5.77 us
  transfers between devices with their start and end apart: 2, of which 2 were waited for; matrix products, arithmetic and copies ran while one was open for 1% of the time, Pallas kernels for 0%

profile of v1, /device:TPU:1, one launch (start us, length us, event | category | flops | bytes accessed | tf_op | source)
XLA Modules:
  0.0 251.1 jit_solution(280369030877171777)
XLA Ops:
  6.5 0.0 copy-start
  6.5 0.0 all-reduce.3.cloned.1.call-start
  6.5 23.8 %all_gather.6 = bf16[128,512]{1,0:T(8,128)(2,1)S(1)} all-gather(bf16[16,512]{1,0:T(8,128)(2,1)} %param.7), channel_id=1, replica_groups=mesh['req'=16,'head'=8] {'head'}, dimensions={0}, use_global_device_ids=true | all-gather | bytes 147456 | tf_op jit(solution)/shard_map/all_gather | solution.py:60
  30.3 0.7 convert_element_type.53
  31.0 0.1 fusion.9
  31.1 0.0 copy-done
  31.2 0.3 fusion.10
  31.5 0.1 broadcast_in_dim.21
  31.6 0.9 pad_maximum_fusion
  32.5 0.0 all-reduce.3.cloned.1.call-update
  32.5 0.0 reduce-scatter.2.cloned.1.call-start
  32.6 0.7 convert_element_type.55
  33.2 1.2 dynamic-slice
  35.1 0.1 multiply_cosine_fusion.1
  35.2 0.7 iota_compare_fusion
  36.0 140.5 %all-reduce.3.cloned.1.call-done = f32[128,1408]{1,0:T(8,128)} async-done(((f32[128,1408]{1,0:T(8,128)}), f32[128,1408]{1,0:T(8,128)}) %all-reduce.3.cloned.1.call-update) | async-done | bytes 720912
  176.5 0.0 copy-start.1
  176.5 1.0 fusion.26
  177.5 1.1 fusion.13
  178.6 0.1 fusion.38
  178.6 0.1 fusion.33
  178.8 0.1 maximum_bitcast_fusion
  178.9 0.2 fusion.27
  179.1 5.8 %fusion.39 = (f32[8,8]{1,0:T(8,128)S(1)}, f32[8,8,4096]{2,1,0:T(8,128)S(1)}) fusion(bf16[8,4096,128]{2,1,0:T(8,128)(2,1)} %param.11, bf16[8,8,64]{2,1,0:T(8,128)(2,1)S(1)} %get-tuple-element.6, bf16[8,8,64]{2,1,0:T(8,128)(2,1)S(1)} %get-tuple-element.5, pred[8,4096]{1,0:T(8,128)(4,1)S(1)} %iota_compare_fusion), kind=kOutput, calls=%fused_computation.65 | convolution fusion | flops 67928000 | bytes 9486592 | tf_op jit(solution)/shard_map/rkgd,rpkd->rkgp/dot_general | solution.py:42
  184.8 0.4 fusion.3
  185.3 0.0 copy-done.1
  185.3 0.0 copy-start.2
  185.3 0.0 copy-start.3
  185.3 1.3 fusion.2
  186.7 24.5 %all_gather.7 = bf16[128,1024]{1,0:T(8,128)(2,1)S(1)} all-gather(bf16[8,1024]{1,0:T(8,128)(2,1)S(1)} %bitcast.37), channel_id=1, replica_groups=mesh['req'=16,'head'=8] {'req'}, dimensions={0}, use_global_device_ids=true | all-gather | bytes 278528 | tf_op jit(solution)/shard_map/all_gather | solution.py:85
  211.2 0.0 copy-done.2
  211.2 1.0 fusion.40
  212.2 0.0 reduce-scatter.2.cloned.1.call-update
  212.2 30.7 %reduce-scatter.2.cloned.1.call-done = f32[16,512]{1,0:T(8,128)} async-done(((f32[128,512]{1,0:T(8,128)}), f32[16,512]{1,0:T(8,128)}) %reduce-scatter.2.cloned.1.call-update) | async-done | bytes 32784 | tf_op jit(solution)/shard_map/reduce_scatter | solution.py:86
  242.9 0.0 copy-done.3
  242.9 1.4 add_convert_fusion
  (8 shorter events, 0.1 us)
Async XLA Ops:
  6.5 24.6 %copy-start = (bf16[512,1280]{1,0:T(8,128)(2,1)S(1)}, bf16[512,1280]{1,0:T(8,128)(2,1)}, u32[]{:S(2)}) copy-start(bf16[512,1280]{1,0:T(8,128)(2,1)} %param.9) | copy-start | bytes 3932164
  6.5 169.9 %all-reduce.3.cloned.1.call-start = ((), (), s32[]{:S(2)}) async-start(), calls=%async_computation.2 | async-start | bytes 1441792
  32.5 210.4 %reduce-scatter.2.cloned.1.call-start = ((), (), s32[]{:S(2)}) async-start(), calls=%async_computation.1 | async-start | bytes 294912 | tf_op jit(solution)/shard_map/reduce_scatter | solution.py:86
  176.5 8.8 %copy-start.1 = (bf16[8,4096,128]{2,1,0:T(8,128)(2,1)S(1)}, bf16[8,4096,128]{2,1,0:T(8,128)(2,1)}, u32[]{:S(2)}) copy-start(bf16[8,4096,128]{2,1,0:T(8,128)(2,1)} %param.12) | copy-start | bytes 25165828
  185.3 25.9 %copy-start.2 = (bf16[1024,512]{1,0:T(8,128)(2,1)S(1)}, bf16[1024,512]{1,0:T(8,128)(2,1)}, u32[]{:S(2)}) copy-start(bf16[1024,512]{1,0:T(8,128)(2,1)} %param.10) | copy-start | bytes 3145732
  185.3 57.6 %copy-start.3 = (bf16[16,512]{1,0:T(8,128)(2,1)S(1)}, bf16[16,512]{1,0:T(8,128)(2,1)}, u32[]{:S(2)}) copy-start(bf16[16,512]{1,0:T(8,128)(2,1)} %param.7) | copy-start | bytes 49156
Sparse Core Ops, SparseCore 0:
  32.6 143.7 all-reduce.2
  212.3 30.5 reduce-scatter.1

commit v2 on v1

--- a/solution.py
+++ b/solution.py
@@ -1,6 +1,10 @@
+import functools
+
 import jax
 import jax.numpy as jnp
 from jax import lax
+from jax.experimental import pallas as pl
+from jax.experimental.pallas import tpu as pltpu
 from jax.sharding import PartitionSpec as P
 
 D = 8192
@@ -55,9 +59,75 @@
     return mixed.astype(jnp.bfloat16)
 
 
-def local(hidden_in, attn_gain, w_qkv, w_out, k_cache, v_cache, lengths):
+def exchange_kernel(axis, n, reduce, x_ref, o_ref, buf, send_sems, recv_sems):
+    me = lax.axis_index(axis)
+    barrier = pltpu.get_barrier_semaphore()
+    for k in range(1, n):
+        pl.semaphore_signal(
+            barrier, inc=1, device_id={axis: lax.rem(me + k, n)},
+            device_id_type=pl.DeviceIdType.MESH,
+        )
+    pl.semaphore_wait(barrier, n - 1)
+    sends = []
+    for k in range(1, n):
+        peer = lax.rem(me + k, n)
+        copy = pltpu.make_async_remote_copy(
+            src_ref=x_ref.at[peer],
+            dst_ref=buf.at[me],
+            send_sem=send_sems.at[k],
+            recv_sem=recv_sems.at[k],
+            device_id={axis: peer},
+            device_id_type=pl.DeviceIdType.MESH,
+        )
+        copy.start()
+        sends.append(copy)
+    for k in range(1, n):
+        source = lax.rem(me + n - k, n)
+        arrival = pltpu.make_async_remote_copy(
+            src_ref=x_ref.at[source],
+            dst_ref=buf.at[source],
+            send_sem=send_sems.at[k],
+            recv_sem=recv_sems.at[k],
+            device_id={axis: source},
+            device_id_type=pl.DeviceIdType.MESH,
+        )
+        arrival.wait_recv()
+    for copy in sends:
+        copy.wait_send()
+    if reduce:
+        total = x_ref[me].astype(jnp.float32)
+        for k in range(1, n):
+            total = total + buf[lax.rem(me + n - k, n)].astype(jnp.float32)
+        o_ref[...] = total.astype(o_ref.dtype)
+    else:
+        for k in range(1, n):
+            source = lax.rem(me + n - k, n)
+            o_ref[source] = buf[source]
+        o_ref[me] = x_ref[me]
+
+
+def exchange(x, axis, n, reduce, collective_id):
+    out_shape = x.shape[1:] if reduce else x.shape
+    return pl.pallas_call(
+        functools.partial(exchange_kernel, axis, n, reduce),
+        out_shape=jax.ShapeDtypeStruct(out_shape, x.dtype),
+        in_specs=[pl.BlockSpec(memory_space=pltpu.VMEM)],
+        out_specs=pl.BlockSpec(memory_space=pltpu.VMEM),
+        scratch_shapes=[
+            pltpu.VMEM(x.shape, x.dtype),
+            pltpu.SemaphoreType.DMA((n,)),
+            pltpu.SemaphoreType.DMA((n,)),
+        ],
+        compiler_params=pltpu.CompilerParams(collective_id=collective_id, has_side_effects=True),
+    )(x)
+
+
+def local(req_n, head_n, hidden_in, attn_gain, w_qkv, w_out, k_cache, v_cache, lengths):
     states = hidden_in.astype(jnp.float32)
-    every_row = lax.all_gather(hidden_in, "head", axis=0, tiled=True).astype(jnp.float32)
+    rows = hidden_in.shape[0]
+    copies = jnp.broadcast_to(hidden_in[None], (head_n,) + hidden_in.shape)
+    every_row = exchange(copies, "head", head_n, False, 0)
+    every_row = every_row.reshape(head_n * rows, hidden_in.shape[1]).astype(jnp.float32)
     scaled = (every_row * attn_gain.astype(jnp.float32)[None, :]).astype(jnp.bfloat16)
     partial_square = jnp.sum(every_row * every_row, axis=1)
     partial = jnp.dot(scaled, w_qkv, preferred_element_type=jnp.float32)
@@ -65,9 +135,9 @@
     packed = jnp.concatenate(
         [partial, jnp.broadcast_to(partial_square[:, None], (partial.shape[0], 128))], axis=1
     )
-    summed = lax.psum_scatter(packed, "req", scatter_dimension=0, tiled=True)
+    own_count = k_cache.shape[0]
+    summed = exchange(packed.reshape(req_n, own_count, columns + 128), "req", req_n, True, 1)
     mean_square = summed[:, columns] / D
-    own_count = k_cache.shape[0]
     slots = k_cache.shape[1]
     local_heads = k_cache.shape[2] // HD
     projected = summed[:, :columns] * lax.rsqrt(mean_square + epsilon)[:, None]
@@ -82,19 +152,18 @@
         queries, new_keys, new_values, cached_keys, cached_values, lengths, factor
     )
     flat_rows = attended.reshape(own_count, local_heads * GROUP * HD)
-    gathered = lax.all_gather(flat_rows, "req", axis=0, tiled=True)
-    output = lax.psum_scatter(
-        jnp.dot(gathered, w_out, preferred_element_type=jnp.float32),
-        "head",
-        scatter_dimension=0,
-        tiled=True,
+    gathered = exchange(
+        jnp.broadcast_to(flat_rows[None], (req_n,) + flat_rows.shape), "req", req_n, False, 2
     )
+    gathered = gathered.reshape(req_n * own_count, flat_rows.shape[1])
+    product = jnp.dot(gathered, w_out, preferred_element_type=jnp.float32)
+    output = exchange(product.reshape(head_n, rows, product.shape[1]), "head", head_n, True, 3)
     return (states + output).astype(jnp.bfloat16)
 
 
 def solution(mesh):
     return jax.shard_map(
-        local,
+        functools.partial(local, mesh.shape["req"], mesh.shape["head"]),
         mesh=mesh,
         in_specs=(
             P("head", "req"),

time: 256 us -> 70.3 us (0.27); the launches traced: 251 us -> 69.9 us
  waiting for transfers between devices: 171 us -> 0 us
  blocking collectives: 48.3 us -> 0 us
  Pallas kernels: 0 us -> 48.2 us
  between operations: 14.1 us -> 0.16 us
    unnamed x3 -> x0, waiting for transfers between devices: 141 us -> none
    all_gather x2 -> x0, blocking collectives: 48.3 us -> none  [the longest x1 24.5 us: local(): gathered = lax.all_gather(flat_rows, 'req', axis=0, tiled=True)]
    pallas_call x0 -> x4, Pallas kernels: none -> 48.2 us  [exchange(): pl.pallas_call(functools.partial(exchange_kernel, axis, n, reduce), out_s...]
    reduce_scatter x1 -> x0, waiting for transfers between devices: 30.7 us -> none  [local(): lax.psum_scatter(jnp.dot(gathered, w_out, preferred_element_type=jnp.floa...]
  transfers between devices with their start and end apart: 2 -> 0, of which waited for: 2 -> 0; matrix products, arithmetic and copies ran while one was open for 1% -> 0% of each run, Pallas kernels for 0% -> 0%
where the time goes in v2:
time: 70.3 us; the launch traced here: 69.9 us
  Pallas kernels  48.2 us (69%)
  matrix products  9.63 us (14%)
  other arithmetic  9.41 us (13%)
  local copies, waits for them, and re-layouts  2.46 us (3%)
    pallas_call x4, Pallas kernels, exchange(): pl.pallas_call(functools.partial(exchange_kernel, axis, n, reduce), out_s...  48.2 us
    dot_general x1, matrix products, attend_padded(): jnp.einsum('rkgd,rpkd->rkgp', queries, cached_keys, preferred_element_typ...  5.77 us
    dot_general x1, matrix products, local(): product = jnp.dot(gathered, w_out, preferred_element_type=jnp.float32)  1.96 us
    broadcast_in_dim x1, local copies, waits for them, and re-layouts, local(): copies = jnp.broadcast_to(hidden_in[None], (head_n,) + hidden_in.shape)  1.47 us

profile of v2, /device:TPU:1, one launch (start us, length us, event | category | flops | bytes accessed | tf_op | source)
XLA Modules:
  0.0 69.9 jit_solution(2676178630567494587)
XLA Ops:
  0.0 0.0 copy-start
  0.0 1.5 %broadcast_in_dim.29.x_ref = bf16[8,16,512]{2,1,0:T(8,128)(2,1)} broadcast(bf16[16,512]{1,0:T(8,128)(2,1)} %param.7), dimensions={1,2} | broadcast | bytes 147456 | tf_op jit(solution)/shard_map/broadcast_in_dim | solution.py:128
  1.5 9.0 %shard_map.73 = bf16[8,16,512]{2,1,0:T(8,128)(2,1)} custom-call(bf16[8,16,512]{2,1,0:T(8,128)(2,1)} %broadcast_in_dim.29.x_ref), custom_call_target="tpu_custom_call" | custom-call | tf_op jit(solution)/shard_map/pallas_call | solution.py:111
  10.5 0.7 convert_element_type.60
  11.2 0.9 %fusion.10 = bf16[128,512]{1,0:T(8,128)(2,1)S(1)} fusion(f32[512]{0:T(512)S(1)} %convert_element_type.60, bf16[8,16,512]{2,1,0:T(8,128)(2,1)} %shard_map.73), kind=kLoop, calls=%fused_computation.16 | loop fusion | flops 196608 | bytes 264192 | tf_op jit(solution)/shard_map/convert_element_type | solution.py:131
  12.1 0.0 copy-done
  12.2 0.3 fusion.34
  12.5 1.0 %multiply_reduce_fusion = f32[8,16]{1,0:T(8,128)S(1)} fusion(bf16[8,16,512]{2,1,0:T(8,128)(2,1)} %shard_map.73), kind=kLoop, calls=%fused_computation.17 | loop fusion | flops 196480 | bytes 131584 | tf_op jit(solution)/shard_map/reduce_sum | solution.py:132
  13.5 0.1 broadcast_in_dim.30
  13.6 0.1 broadcast_in_dim.31
  13.7 0.9 %maximum_bitcast_fusion.x_ref = f32[16,8,1408]{2,1,0:T(8,128)} fusion(f32[128,128]{1,0:T(8,128)S(1)} %broadcast_in_dim.31, f32[128,1280]{1,0:T(8,128)S(1)} %fusion.34), kind=kLoop, calls=%fused_computation.10 | loop fusion | flops 180224 | bytes 1441792 | tf_op jit(solution)/shard_map/reshape | solution.py:139
  14.6 19.6 %shard_map.74 = f32[8,1408]{1,0:T(8,128)} custom-call(f32[16,8,1408]{2,1,0:T(8,128)} %maximum_bitcast_fusion.x_ref), custom_call_target="tpu_custom_call" | custom-call | tf_op jit(solution)/shard_map/pallas_call | solution.py:111
  34.2 0.0 copy-start.1
  34.2 0.9 %rsqrt_reduce_fusion = f32[8]{0:T(128)S(1)} fusion(f32[8,1408]{1,0:T(8,128)} %shard_map.74), kind=kLoop, calls=%fused_computation.43 | loop fusion | flops 16 | bytes 64 | tf_op jit(solution)/shard_map/rsqrt | solution.py:143
  35.2 1.0 %multiply_bitcast_fusion = f32[8,1,10,128]{3,0,2,1:T(8,128)S(1)} fusion(f32[8,1408]{1,0:T(8,128)} %shard_map.74, f32[8]{0:T(128)S(1)} %rsqrt_reduce_fusion), kind=kLoop, calls=%fused_computation.19 | loop fusion | flops 10240 | bytes 81952 | tf_op jit(solution)/shard_map/reshape | solution.py:144
  36.2 0.1 fusion.32
  36.3 1.0 %convert_element_type.63 = f32[8]{0:T(128)S(1)} convert(s32[8]{0:T(128)} %param.13) | non-fusion elementwise | flops 8 | bytes 64 | tf_op jit(solution)/shard_map/convert_element_type | solution.py:24
  37.3 0.1 multiply_cosine_fusion.1
  37.5 0.1 fusion.27
  37.6 0.1 maximum_bitcast_fusion.1
  37.7 0.2 fusion.21
  37.9 0.8 %iota_compare_fusion = pred[8,4096]{1,0:T(8,128)(4,1)S(1)} fusion(s32[8]{0:T(128)} %param.13), kind=kLoop, calls=%fused_computation.18 | loop fusion | flops 32768 | bytes 32800 | tf_op jit(solution)/shard_map/lt | solution.py:44
  38.6 5.8 %fusion.33 = (f32[8,8]{1,0:T(8,128)S(1)}, f32[8,8,4096]{2,1,0:T(8,128)S(1)}) fusion(bf16[8,4096,128]{2,1,0:T(8,128)(2,1)} %param.11, bf16[8,8,64]{2,1,0:T(8,128)(2,1)S(1)} %get-tuple-element.6, bf16[8,8,64]{2,1,0:T(8,128)(2,1)S(1)} %get-tuple-element.5, pred[8,4096]{1,0:T(8,128)(4,1)S(1)} %iota_compare_fusion), kind=kOutput, calls=%fused_computation.60 | convolution fusion | flops 67928000 | bytes 9486592 | tf_op jit(solution)/shard_map/rkgd,rpkd->rkgp/dot_general | solution.py:46
  44.4 0.4 fusion.5
  44.8 0.0 copy-done.1
  44.8 0.0 copy-start.2
  44.9 0.0 copy-start.3
  44.9 1.4 %fusion.2 = bf16[1,8,8,128]{3,2,1,0:T(8,128)(2,1)S(1)} fusion(bf16[8,4096,128]{2,1,0:T(8,128)(2,1)S(1)} %copy-done.1, f32[8,8,4096]{2,1,0:T(8,128)S(1)} %get-tuple-element.16, f32[8,8]{1,0:T(8,128)S(1)} %get-tuple-element.10, f32[8,8]{1,0:T(8,128)S(1)} %multiply_maximum_fusion, pred[8,4096]{1,0:T(8,128)(4,1)S(1)} %iota_compare_fusion, ...), kind=kOutput, calls=%fused_computation.4 | convolution fusion | flops 68182016 | bytes 9491200 | tf_op jit(solution)/shard_map/rkgp,rpkd->rkgd/dot_general | solution.py:57
  46.2 0.7 %broadcast_in_dim.60.x_ref = bf16[16,8,1024]{2,1,0:T(8,128)(2,1)} broadcast(bf16[8,1024]{1,0:T(8,128)(2,1)S(1)} %bitcast.47), dimensions={1,2} | broadcast | bytes 278528 | tf_op jit(solution)/shard_map/broadcast_in_dim | solution.py:156
  47.0 11.5 %shard_map.75 = bf16[16,8,1024]{2,1,0:T(8,128)(2,1)} custom-call(bf16[16,8,1024]{2,1,0:T(8,128)(2,1)} %broadcast_in_dim.60.x_ref), custom_call_target="tpu_custom_call" | custom-call | tf_op jit(solution)/shard_map/pallas_call | solution.py:111
  58.5 0.0 copy-done.2
  58.5 2.0 %fusion.3.x_ref = f32[8,16,512]{2,1,0:T(8,128)} fusion(bf16[8,16,1024]{2,1,0:T(8,128)(2,1)} %bitcast.46, bf16[1024,512]{1,0:T(8,128)(2,1)S(1)} %copy-done.2), kind=kOutput, calls=%fused_computation.5 | convolution fusion | flops 134217728 | bytes 1572864 | tf_op jit(solution)/shard_map/dot_general | solution.py:159
  60.4 8.1 %shard_map.76 = f32[16,512]{1,0:T(8,128)} custom-call(f32[8,16,512]{2,1,0:T(8,128)} %fusion.3.x_ref), custom_call_target="tpu_custom_call" | custom-call | tf_op jit(solution)/shard_map/pallas_call | solution.py:111
  68.5 0.0 copy-done.3
  68.5 1.4 %add_convert_fusion = bf16[16,512]{1,0:T(8,128)(2,1)} fusion(f32[16,512]{1,0:T(8,128)} %shard_map.76, bf16[16,512]{1,0:T(8,128)(2,1)S(1)} %copy-done.3), kind=kLoop, calls=%fused_computation.20 | loop fusion | flops 24576 | bytes 65536 | tf_op jit(solution)/shard_map/convert_element_type | solution.py:161
  (8 shorter events, 0.1 us)
Async XLA Ops:
  0.0 12.1 %copy-start = (bf16[512,1280]{1,0:T(8,128)(2,1)S(1)}, bf16[512,1280]{1,0:T(8,128)(2,1)}, u32[]{:S(2)}) copy-start(bf16[512,1280]{1,0:T(8,128)(2,1)} %param.9) | copy-start | bytes 3932164
  34.2 10.6 %copy-start.1 = (bf16[8,4096,128]{2,1,0:T(8,128)(2,1)S(1)}, bf16[8,4096,128]{2,1,0:T(8,128)(2,1)}, u32[]{:S(2)}) copy-start(bf16[8,4096,128]{2,1,0:T(8,128)(2,1)} %param.12) | copy-start | bytes 25165828
  44.8 13.6 %copy-start.2 = (bf16[1024,512]{1,0:T(8,128)(2,1)S(1)}, bf16[1024,512]{1,0:T(8,128)(2,1)}, u32[]{:S(2)}) copy-start(bf16[1024,512]{1,0:T(8,128)(2,1)} %param.10) | copy-start | bytes 3145732
  44.9 23.7 %copy-start.3 = (bf16[16,512]{1,0:T(8,128)(2,1)S(1)}, bf16[16,512]{1,0:T(8,128)(2,1)}, u32[]{:S(2)}) copy-start(bf16[16,512]{1,0:T(8,128)(2,1)} %param.7) | copy-start | bytes 49156

commit v3 on v2

--- a/solution.py
+++ b/solution.py
@@ -59,21 +59,24 @@
     return mixed.astype(jnp.bfloat16)
 
 
-def exchange_kernel(axis, n, reduce, x_ref, o_ref, buf, send_sems, recv_sems):
-    me = lax.axis_index(axis)
+def greet(peers):
     barrier = pltpu.get_barrier_semaphore()
-    for k in range(1, n):
-        pl.semaphore_signal(
-            barrier, inc=1, device_id={axis: lax.rem(me + k, n)},
-            device_id_type=pl.DeviceIdType.MESH,
-        )
-    pl.semaphore_wait(barrier, n - 1)
+    for axis, me, n in peers:
+        for k in range(1, n):
+            pl.semaphore_signal(
+                barrier, inc=1, device_id={axis: lax.rem(me + k, n)},
+                device_id_type=pl.DeviceIdType.MESH,
+            )
+    pl.semaphore_wait(barrier, sum(n - 1 for _, _, n in peers))
+
+
+def send_all(axis, me, n, block_of, dst, send_sems, recv_sems):
     sends = []
     for k in range(1, n):
         peer = lax.rem(me + k, n)
         copy = pltpu.make_async_remote_copy(
-            src_ref=x_ref.at[peer],
-            dst_ref=buf.at[me],
+            src_ref=block_of(peer),
+            dst_ref=dst.at[me],
             send_sem=send_sems.at[k],
             recv_sem=recv_sems.at[k],
             device_id={axis: peer},
@@ -81,11 +84,15 @@
         )
         copy.start()
         sends.append(copy)
+    return sends
+
+
+def receive_all(axis, me, n, block_of, dst, send_sems, recv_sems, sends):
     for k in range(1, n):
         source = lax.rem(me + n - k, n)
         arrival = pltpu.make_async_remote_copy(
-            src_ref=x_ref.at[source],
-            dst_ref=buf.at[source],
+            src_ref=block_of(source),
+            dst_ref=dst.at[source],
             send_sem=send_sems.at[k],
             recv_sem=recv_sems.at[k],
             device_id={axis: source},
@@ -94,49 +101,96 @@
         arrival.wait_recv()
     for copy in sends:
         copy.wait_send()
-    if reduce:
-        total = x_ref[me].astype(jnp.float32)
-        for k in range(1, n):
-            total = total + buf[lax.rem(me + n - k, n)].astype(jnp.float32)
-        o_ref[...] = total.astype(o_ref.dtype)
-    else:
-        for k in range(1, n):
-            source = lax.rem(me + n - k, n)
-            o_ref[source] = buf[source]
-        o_ref[me] = x_ref[me]
-
-
-def exchange(x, axis, n, reduce, collective_id):
-    out_shape = x.shape[1:] if reduce else x.shape
+
+
+def project_kernel(req_n, head_n, x_ref, gain_ref, w_ref, o_ref,
+                   rows_buf, part, sums_buf, sems):
+    me_head = lax.axis_index("head")
+    me_req = lax.axis_index("req")
+    greet((("head", me_head, head_n), ("req", me_req, req_n)))
+    own = lambda peer: x_ref
+    sends = send_all("head", me_head, head_n, own, rows_buf, sems.at[0], sems.at[1])
+    receive_all("head", me_head, head_n, own, rows_buf, sems.at[0], sems.at[1], sends)
+    rows_buf[me_head] = x_ref[...]
+    block_rows = x_ref.shape[0]
+    states = rows_buf[...].reshape(head_n * block_rows, x_ref.shape[1]).astype(jnp.float32)
+    scaled = (states * gain_ref[...].astype(jnp.float32)).astype(jnp.bfloat16)
+    columns = w_ref.shape[1]
+    part[:, :columns] = jnp.dot(scaled, w_ref[...], preferred_element_type=jnp.float32)
+    square = jnp.sum(states * states, axis=1, keepdims=True)
+    part[:, columns:] = jnp.broadcast_to(square, (square.shape[0], part.shape[1] - columns))
+    count = o_ref.shape[0]
+    chunk = lambda peer: part.at[pl.ds(pl.multiple_of(peer * count, count), count)]
+    sends = send_all("req", me_req, req_n, chunk, sums_buf, sems.at[2], sems.at[3])
+    receive_all("req", me_req, req_n, chunk, sums_buf, sems.at[2], sems.at[3], sends)
+    total = part[pl.ds(pl.multiple_of(me_req * count, count), count), :]
+    for k in range(1, req_n):
+        total = total + sums_buf[lax.rem(me_req + req_n - k, req_n)]
+    o_ref[...] = total
+
+
+def project(hidden_in, gain, w_qkv, req_n, head_n, count):
+    rows, width = hidden_in.shape
+    columns = w_qkv.shape[1] + 128
     return pl.pallas_call(
-        functools.partial(exchange_kernel, axis, n, reduce),
-        out_shape=jax.ShapeDtypeStruct(out_shape, x.dtype),
-        in_specs=[pl.BlockSpec(memory_space=pltpu.VMEM)],
+        functools.partial(project_kernel, req_n, head_n),
+        out_shape=jax.ShapeDtypeStruct((count, columns), jnp.float32),
+        in_specs=[pl.BlockSpec(memory_space=pltpu.VMEM)] * 3,
         out_specs=pl.BlockSpec(memory_space=pltpu.VMEM),
         scratch_shapes=[
-            pltpu.VMEM(x.shape, x.dtype),
-            pltpu.SemaphoreType.DMA((n,)),
-            pltpu.SemaphoreType.DMA((n,)),
+            pltpu.VMEM((head_n, rows, width), hidden_in.dtype),
+            pltpu.VMEM((req_n * count, columns), jnp.float32),
+            pltpu.VMEM((req_n, count, columns), jnp.float32),
+            pltpu.SemaphoreType.DMA((4, max(req_n, head_n))),
         ],
-        compiler_params=pltpu.CompilerParams(collective_id=collective_id, has_side_effects=True),
-    )(x)
+        compiler_params=pltpu.CompilerParams(collective_id=0, has_side_effects=True),
+    )(hidden_in, gain.reshape(1, width), w_qkv)
+
+
+def output_kernel(req_n, head_n, a_ref, w_ref, s_ref, o_ref, att_buf, part, sums_buf, sems):
+    me_head = lax.axis_index("head")
+    me_req = lax.axis_index("req")
+    greet((("req", me_req, req_n), ("head", me_head, head_n)))
+    own = lambda peer: a_ref
+    sends = send_all("req", me_req, req_n, own, att_buf, sems.at[0], sems.at[1])
+    receive_all("req", me_req, req_n, own, att_buf, sems.at[0], sems.at[1], sends)
+    att_buf[me_req] = a_ref[...]
+    every = jnp.concatenate(
+        [att_buf[s].astype(jnp.float32) for s in range(req_n)], axis=0
+    ).astype(jnp.bfloat16)
+    part[...] = jnp.dot(every, w_ref[...], preferred_element_type=jnp.float32)
+    rows = o_ref.shape[0]
+    chunk = lambda peer: part.at[pl.ds(pl.multiple_of(peer * rows, rows), rows)]
+    sends = send_all("head", me_head, head_n, chunk, sums_buf, sems.at[2], sems.at[3])
+    receive_all("head", me_head, head_n, chunk, sums_buf, sems.at[2], sems.at[3], sends)
+    total = part[pl.ds(pl.multiple_of(me_head * rows, rows), rows), :]
+    for k in range(1, head_n):
+        total = total + sums_buf[lax.rem(me_head + head_n - k, head_n)]
+    o_ref[...] = (s_ref[...].astype(jnp.float32) + total).astype(o_ref.dtype)
+
+
+def output_block(attended, w_out, hidden_in, req_n, head_n):
+    count, width = attended.shape
+    rows, columns = hidden_in.shape
+    return pl.pallas_call(
+        functools.partial(output_kernel, req_n, head_n),
+        out_shape=jax.ShapeDtypeStruct((rows, columns), hidden_in.dtype),
+        in_specs=[pl.BlockSpec(memory_space=pltpu.VMEM)] * 3,
+        out_specs=pl.BlockSpec(memory_space=pltpu.VMEM),
+        scratch_shapes=[
+            pltpu.VMEM((req_n, count, width), attended.dtype),
+            pltpu.VMEM((head_n * rows, columns), jnp.float32),
+            pltpu.VMEM((head_n, rows, columns), jnp.float32),
+            pltpu.SemaphoreType.DMA((4, max(req_n, head_n))),
+        ],
+        compiler_params=pltpu.CompilerParams(collective_id=1, has_side_effects=True),
+    )(attended, w_out, hidden_in)
 
 
 def local(req_n, head_n, hidden_in, attn_gain, w_qkv, w_out, k_cache, v_cache, lengths):
-    states = hidden_in.astype(jnp.float32)
-    rows = hidden_in.shape[0]
-    copies = jnp.broadcast_to(hidden_in[None], (head_n,) + hidden_in.shape)
-    every_row = exchange(copies, "head", head_n, False, 0)
-    every_row = every_row.reshape(head_n * rows, hidden_in.shape[1]).astype(jnp.float32)
-    scaled = (every_row * attn_gain.astype(jnp.float32)[None, :]).astype(jnp.bfloat16)
-    partial_square = jnp.sum(every_row * every_row, axis=1)
-    partial = jnp.dot(scaled, w_qkv, preferred_element_type=jnp.float32)
-    columns = partial.shape[1]
-    packed = jnp.concatenate(
-        [partial, jnp.broadcast_to(partial_square[:, None], (partial.shape[0], 128))], axis=1
-    )
     own_count = k_cache.shape[0]
-    summed = exchange(packed.reshape(req_n, own_count, columns + 128), "req", req_n, True, 1)
+    summed = project(hidden_in, attn_gain, w_qkv, req_n, head_n, own_count)
+    columns = w_qkv.shape[1]
     mean_square = summed[:, columns] / D
     slots = k_cache.shape[1]
     local_heads = k_cache.shape[2] // HD
@@ -152,13 +206,7 @@
         queries, new_keys, new_values, cached_keys, cached_values, lengths, factor
     )
     flat_rows = attended.reshape(own_count, local_heads * GROUP * HD)
-    gathered = exchange(
-        jnp.broadcast_to(flat_rows[None], (req_n,) + flat_rows.shape), "req", req_n, False, 2
-    )
-    gathered = gathered.reshape(req_n * own_count, flat_rows.shape[1])
-    product = jnp.dot(gathered, w_out, preferred_element_type=jnp.float32)
-    output = exchange(product.reshape(head_n, rows, product.shape[1]), "head", head_n, True, 3)
-    return (states + output).astype(jnp.bfloat16)
+    return output_block(flat_rows, w_out, hidden_in, req_n, head_n)
 
 
 def solution(mesh):

time: 70.3 us -> 57.5 us (0.82)
  Pallas kernels: 48.2 us -> 42.4 us
  other arithmetic: 9.41 us -> 4.17 us
  matrix products: 9.63 us -> 7.29 us
  local copies, waits for them, and re-layouts: 2.46 us -> 3.3 us
    pallas_call x4 -> x2, Pallas kernels: 48.2 us -> 42.4 us  [the longest x1 25.8 us: project(): pl.pallas_call(functools.partial(project_kernel, req_n, head_n), out_shap...]
    convert_element_type x3 -> x0, other arithmetic: 2.98 us -> none  [the longest x1 1.37 us: local(): return (states + output).astype(jnp.bfloat16)]
    broadcast_in_dim x4 -> x0, local copies, waits for them, and re-layouts: 2.35 us -> none  [the longest x1 1.47 us: local(): copies = jnp.broadcast_to(hidden_in[None], (head_n,) + hidden_in.shape)]
    dot_general x2 -> x0, matrix products: 2.31 us -> none  [the longest x1 1.96 us: local(): product = jnp.dot(gathered, w_out, preferred_element_type=jnp.float32)]
    unnamed x9 -> x4, local copies, waits for them, and re-layouts: 0.03 us -> 1.96 us
    reshape x0 -> x1, local copies, waits for them, and re-layouts: none -> 1.26 us  [project(): gain.reshape(1, width)]
    reduce_sum x1 -> x0, other arithmetic: 1.01 us -> none  [local(): partial_square = jnp.sum(every_row * every_row, axis=1)]
    reshape x1 -> x0, other arithmetic: 0.92 us -> none  [local(): packed.reshape(req_n, own_count, columns + 128)]
where the time goes in v3:
time: 57.5 us; the launch traced here: 57.2 us
  Pallas kernels  42.4 us (74%)
  matrix products  7.29 us (13%)
  other arithmetic  4.17 us (7%)
  local copies, waits for them, and re-layouts  3.3 us (6%)
    pallas_call x1, Pallas kernels, project(): pl.pallas_call(functools.partial(project_kernel, req_n, head_n), out_shap...  25.8 us
    pallas_call x1, Pallas kernels, output_block(): pl.pallas_call(functools.partial(output_kernel, req_n, head_n), out_shape...  16.6 us
    dot_general x1, matrix products, attend_padded(): jnp.einsum('rkgd,rpkd->rkgp', queries, cached_keys, preferred_element_typ...  5.77 us
    unnamed x4, local copies, waits for them, and re-layouts  1.96 us
    dot_general x1, matrix products, attend_padded(): jnp.einsum('rkgp,rpkd->rkgd', probs, cached_values, preferred_element_typ...  1.33 us
    reshape x1, local copies, waits for them, and re-layouts, project(): gain.reshape(1, width)  1.26 us

profile of v3, /device:TPU:1, one launch (start us, length us, event | category | flops | bytes accessed | tf_op | source)
XLA Modules:
  0.0 57.2 jit_solution(17919120050930426057)
XLA Ops:
  0.0 0.7 %convert_element_type.36 = f32[8]{0:T(128)S(1)} convert(s32[8]{0:T(128)} %param.13) | non-fusion elementwise | flops 8 | bytes 64 | tf_op jit(solution)/shard_map/convert_element_type | solution.py:24
  0.7 1.3 %reshape.248.gain_ref = bf16[1,512]{1,0:T(2,128)(2,1)} reshape(bf16[512]{0:T(512)(128)(2,1)} %param.8) | data formatting | bytes 2048 | tf_op jit(solution)/shard_map/reshape | solution.py:147
  1.9 0.1 multiply_cosine_fusion.1
  2.0 0.7 %iota_compare_fusion = pred[8,4096]{1,0:T(8,128)(4,1)S(1)} fusion(s32[8]{0:T(128)} %param.13), kind=kLoop, calls=%fused_computation.12 | loop fusion | flops 32768 | bytes 32800 | tf_op jit(solution)/shard_map/lt | solution.py:44
  2.8 25.8 %shard_map.73 = f32[8,1408]{1,0:T(8,128)} custom-call(bf16[16,512]{1,0:T(8,128)(2,1)} %s_ref.1, bf16[1,512]{1,0:T(2,128)(2,1)} %reshape.248.gain_ref, bf16[512,1280]{1,0:T(8,128)(2,1)} %w_ref.2), custom_call_target="tpu_custom_call" | custom-call | tf_op jit(solution)/shard_map/pallas_call | solution.py:135
  28.6 0.0 copy-start
  28.6 1.0 %rsqrt_reduce_fusion = f32[8]{0:T(128)S(1)} fusion(f32[8,1408]{1,0:T(8,128)} %shard_map.73), kind=kLoop, calls=%fused_computation.36 | loop fusion | flops 16 | bytes 64 | tf_op jit(solution)/shard_map/rsqrt | solution.py:197
  29.6 1.0 %multiply_bitcast_fusion = f32[8,1,10,128]{3,0,2,1:T(8,128)S(1)} fusion(f32[8,1408]{1,0:T(8,128)} %shard_map.73, f32[8]{0:T(128)S(1)} %rsqrt_reduce_fusion), kind=kLoop, calls=%fused_computation.13 | loop fusion | flops 10240 | bytes 81952 | tf_op jit(solution)/shard_map/reshape | solution.py:198
  30.6 0.1 fusion.24
  30.7 0.1 maximum_bitcast_fusion
  30.8 0.1 fusion.29
  30.9 0.2 fusion.18
  31.1 5.8 %fusion.30 = (f32[8,8]{1,0:T(8,128)S(1)}, f32[8,8,4096]{2,1,0:T(8,128)S(1)}) fusion(bf16[8,4096,128]{2,1,0:T(8,128)(2,1)} %param.11, bf16[8,8,64]{2,1,0:T(8,128)(2,1)S(1)} %get-tuple-element.6, bf16[8,8,64]{2,1,0:T(8,128)(2,1)S(1)} %get-tuple-element.5, pred[8,4096]{1,0:T(8,128)(4,1)S(1)} %iota_compare_fusion), kind=kOutput, calls=%fused_computation.53 | convolution fusion | flops 67928000 | bytes 9486592 | tf_op jit(solution)/shard_map/rkgd,rpkd->rkgp/dot_general | solution.py:46
  36.9 0.4 fusion.3
  37.3 0.0 copy-done
  37.3 1.3 %fusion.2 = bf16[1,8,8,128]{3,2,1,0:T(8,128)(2,1)S(1)} fusion(bf16[8,4096,128]{2,1,0:T(8,128)(2,1)S(1)} %copy-done, f32[8,8,4096]{2,1,0:T(8,128)S(1)} %get-tuple-element.16, f32[8,8]{1,0:T(8,128)S(1)} %get-tuple-element.10, f32[8,8]{1,0:T(8,128)S(1)} %multiply_maximum_fusion, pred[8,4096]{1,0:T(8,128)(4,1)S(1)} %iota_compare_fusion, ...), kind=kOutput, calls=%fused_computation.4 | convolution fusion | flops 68182016 | bytes 9491200 | tf_op jit(solution)/shard_map/rkgp,rpkd->rkgd/dot_general | solution.py:57
  38.7 0.6 %copy.32 = bf16[1,8,8,128]{3,1,2,0:T(8,128)(2,1)} copy(bf16[1,8,8,128]{3,2,1,0:T(8,128)(2,1)S(1)} %fusion.2) | data formatting | bytes 32768
  39.3 16.6 %shard_map.74 = bf16[16,512]{1,0:T(8,128)(2,1)} custom-call(bf16[8,1024]{1,0:T(8,128)(2,1)} %bitcast.33, bf16[1024,512]{1,0:T(8,128)(2,1)} %w_ref.3, bf16[16,512]{1,0:T(8,128)(2,1)} %s_ref.1), custom_call_target="tpu_custom_call" | custom-call | tf_op jit(solution)/shard_map/pallas_call | solution.py:175
  55.9 1.3 %copy.34 = bf16[16,512]{1,0:T(8,128)(2,1)} copy(bf16[16,512]{1,0:T(8,128)(2,1)} %shard_map.74) | data formatting | bytes 32768
  (7 shorter events, 0.1 us)
Async XLA Ops:
  28.6 8.7 %copy-start = (bf16[8,4096,128]{2,1,0:T(8,128)(2,1)S(1)}, bf16[8,4096,128]{2,1,0:T(8,128)(2,1)}, u32[]{:S(2)}) copy-start(bf16[8,4096,128]{2,1,0:T(8,128)(2,1)} %param.12) | copy-start | bytes 25165828

commit v4 on v3

--- a/solution.py
+++ b/solution.py
@@ -114,7 +114,7 @@
     rows_buf[me_head] = x_ref[...]
     block_rows = x_ref.shape[0]
     states = rows_buf[...].reshape(head_n * block_rows, x_ref.shape[1]).astype(jnp.float32)
-    scaled = (states * gain_ref[...].astype(jnp.float32)).astype(jnp.bfloat16)
+    scaled = (states * gain_ref[...].astype(jnp.float32)[None, :]).astype(jnp.bfloat16)
     columns = w_ref.shape[1]
     part[:, :columns] = jnp.dot(scaled, w_ref[...], preferred_element_type=jnp.float32)
     square = jnp.sum(states * states, axis=1, keepdims=True)
@@ -126,7 +126,8 @@
     total = part[pl.ds(pl.multiple_of(me_req * count, count), count), :]
     for k in range(1, req_n):
         total = total + sums_buf[lax.rem(me_req + req_n - k, req_n)]
-    o_ref[...] = total
+    mean_square = total[:, columns:columns + 1] / D
+    o_ref[...] = total[:, :columns] * lax.rsqrt(mean_square + epsilon)
 
 
 def project(hidden_in, gain, w_qkv, req_n, head_n, count):
@@ -134,7 +135,7 @@
     columns = w_qkv.shape[1] + 128
     return pl.pallas_call(
         functools.partial(project_kernel, req_n, head_n),
-        out_shape=jax.ShapeDtypeStruct((count, columns), jnp.float32),
+        out_shape=jax.ShapeDtypeStruct((count, w_qkv.shape[1]), jnp.float32),
         in_specs=[pl.BlockSpec(memory_space=pltpu.VMEM)] * 3,
         out_specs=pl.BlockSpec(memory_space=pltpu.VMEM),
         scratch_shapes=[
@@ -144,7 +145,7 @@
             pltpu.SemaphoreType.DMA((4, max(req_n, head_n))),
         ],
         compiler_params=pltpu.CompilerParams(collective_id=0, has_side_effects=True),
-    )(hidden_in, gain.reshape(1, width), w_qkv)
+    )(hidden_in, gain, w_qkv)
 
 
 def output_kernel(req_n, head_n, a_ref, w_ref, s_ref, o_ref, att_buf, part, sums_buf, sems):
@@ -189,12 +190,9 @@
 
 def local(req_n, head_n, hidden_in, attn_gain, w_qkv, w_out, k_cache, v_cache, lengths):
     own_count = k_cache.shape[0]
-    summed = project(hidden_in, attn_gain, w_qkv, req_n, head_n, own_count)
-    columns = w_qkv.shape[1]
-    mean_square = summed[:, columns] / D
+    projected = project(hidden_in, attn_gain, w_qkv, req_n, head_n, own_count)
     slots = k_cache.shape[1]
     local_heads = k_cache.shape[2] // HD
-    projected = summed[:, :columns] * lax.rsqrt(mean_square + epsilon)[:, None]
     projected = projected.reshape(own_count, local_heads, GROUP + 2, HD)
     queries = rotate(projected[:, :, :GROUP], lengths).astype(jnp.bfloat16)
     new_keys = rotate(projected[:, :, GROUP], lengths).astype(jnp.bfloat16)

time: 57.5 us -> 57 us (level)
  other arithmetic: 4.17 us -> 3.06 us
  local copies, waits for them, and re-layouts: 3.3 us -> 3.9 us
    reshape x1 -> x0, local copies, waits for them, and re-layouts: 1.26 us -> none  [project(): gain.reshape(1, width)]
    slice x1, local copies, waits for them, and re-layouts: 0.07 us -> 1.12 us  [rotate(): second = vectors[..., halfway:]]
    reshape x1 -> x0, other arithmetic: 1.05 us -> none  [local(): projected = projected.reshape(own_count, local_heads, GROUP + 2, HD)]
    rsqrt x1 -> x0, other arithmetic: 0.95 us -> none  [local(): projected = summed[:, :columns] * lax.rsqrt(mean_square + epsilon)[:, None]]
    mul x2, other arithmetic: 0.01 us -> 0.89 us  [own_part(): own_prob.astype(jnp.float32)[..., None]]
    squeeze x1, local copies, waits for them, and re-layouts: 0.01 us -> 0.83 us  [local(): new_keys = rotate(projected[:, :, GROUP], lengths).astype(jnp.bfloat16)]
where the time goes in v4:
time: 57 us; the launch traced here: 56.7 us
  Pallas kernels  42.4 us (74%)
  matrix products  7.29 us (13%)
  local copies, waits for them, and re-layouts  3.9 us (7%)
  other arithmetic  3.06 us (5%)
    pallas_call x1, Pallas kernels, project(): pl.pallas_call(functools.partial(project_kernel, req_n, head_n), out_shap...  25.9 us
    pallas_call x1, Pallas kernels, output_block(): pl.pallas_call(functools.partial(output_kernel, req_n, head_n), out_shape...  16.6 us
    dot_general x1, matrix products, attend_padded(): jnp.einsum('rkgd,rpkd->rkgp', queries, cached_keys, preferred_element_typ...  5.77 us
    unnamed x4, local copies, waits for them, and re-layouts  1.96 us
    dot_general x1, matrix products, attend_padded(): jnp.einsum('rkgp,rpkd->rkgd', probs, cached_values, preferred_element_typ...  1.33 us

profile of v4, /device:TPU:1, one launch (start us, length us, event | category | flops | bytes accessed | tf_op | source)
XLA Modules:
  0.0 56.7 jit_solution(10807399426266988457)
XLA Ops:
  0.0 0.7 %convert_element_type.36 = f32[8]{0:T(128)S(1)} convert(s32[8]{0:T(128)} %param.13) | non-fusion elementwise | flops 8 | bytes 64 | tf_op jit(solution)/shard_map/convert_element_type | solution.py:24
  0.7 0.1 multiply_cosine_fusion.1
  0.8 0.7 %iota_compare_fusion = pred[8,4096]{1,0:T(8,128)(4,1)S(1)} fusion(s32[8]{0:T(128)} %param.13), kind=kLoop, calls=%fused_computation.12 | loop fusion | flops 32768 | bytes 32800 | tf_op jit(solution)/shard_map/lt | solution.py:44
  1.5 25.9 %shard_map.73 = f32[8,1280]{1,0:T(8,128)} custom-call(bf16[16,512]{1,0:T(8,128)(2,1)} %s_ref.1, bf16[512]{0:T(512)(128)(2,1)} %gain_ref.1, bf16[512,1280]{1,0:T(8,128)(2,1)} %w_ref.2), custom_call_target="tpu_custom_call" | custom-call | tf_op jit(solution)/shard_map/pallas_call | solution.py:136
  27.4 0.0 copy-start
  27.4 0.8 %slice_bitcast_fusion = f32[8,1,128]{2,0,1:T(8,128)S(1)} fusion(f32[8,1,10,128]{3,0,2,1:T(8,128)} %bitcast.32), kind=kLoop, calls=%fused_computation.32 | loop fusion | bytes 8192 | tf_op jit(solution)/shard_map/squeeze | solution.py:198
  28.2 0.1 fusion.24
  28.3 0.1 maximum_bitcast_fusion
  28.4 0.9 %fusion.21 = f32[8,128]{1,0:T(8,128)S(1)} fusion(f32[8,1,10,128]{3,0,2,1:T(8,128)} %bitcast.33), kind=kLoop, calls=%fused_computation.39 | loop fusion | flops 1024 | bytes 6144 | tf_op jit(solution)/shard_map/mul | solution.py:39
  29.3 1.1 %fusion.29 = (f32[8,1,8,64]{3,0,2,1:T(8,128)S(1)}, f32[8,1,8,64]{3,0,2,1:T(8,128)S(1)}) fusion(f32[8,1,10,128]{3,0,2,1:T(8,128)} %bitcast.34), kind=kLoop, calls=%fused_computation.50 | loop fusion | bytes 65536 | tf_op jit(solution)/shard_map/slice | solution.py:29
  30.5 0.2 fusion.18
  30.7 5.8 %fusion.30 = (f32[8,8]{1,0:T(8,128)S(1)}, f32[8,8,4096]{2,1,0:T(8,128)S(1)}) fusion(bf16[8,4096,128]{2,1,0:T(8,128)(2,1)} %param.11, bf16[8,8,64]{2,1,0:T(8,128)(2,1)S(1)} %get-tuple-element.6, bf16[8,8,64]{2,1,0:T(8,128)(2,1)S(1)} %get-tuple-element.5, pred[8,4096]{1,0:T(8,128)(4,1)S(1)} %iota_compare_fusion), kind=kOutput, calls=%fused_computation.51 | convolution fusion | flops 67928000 | bytes 9486592 | tf_op jit(solution)/shard_map/rkgd,rpkd->rkgp/dot_general | solution.py:46
  36.4 0.4 fusion.3
  36.9 0.0 copy-done
  36.9 1.3 %fusion.2 = bf16[1,8,8,128]{3,2,1,0:T(8,128)(2,1)S(1)} fusion(bf16[8,4096,128]{2,1,0:T(8,128)(2,1)S(1)} %copy-done, f32[8,8,4096]{2,1,0:T(8,128)S(1)} %get-tuple-element.16, f32[8,8]{1,0:T(8,128)S(1)} %get-tuple-element.10, f32[8,8]{1,0:T(8,128)S(1)} %multiply_maximum_fusion, pred[8,4096]{1,0:T(8,128)(4,1)S(1)} %iota_compare_fusion, ...), kind=kOutput, calls=%fused_computation.4 | convolution fusion | flops 68182016 | bytes 9491200 | tf_op jit(solution)/shard_map/rkgp,rpkd->rkgd/dot_general | solution.py:57
  38.2 0.6 %copy.30 = bf16[1,8,8,128]{3,1,2,0:T(8,128)(2,1)} copy(bf16[1,8,8,128]{3,2,1,0:T(8,128)(2,1)S(1)} %fusion.2) | data formatting | bytes 32768
  38.8 16.6 %shard_map.74 = bf16[16,512]{1,0:T(8,128)(2,1)} custom-call(bf16[8,1024]{1,0:T(8,128)(2,1)} %bitcast.35, bf16[1024,512]{1,0:T(8,128)(2,1)} %w_ref.3, bf16[16,512]{1,0:T(8,128)(2,1)} %s_ref.1), custom_call_target="tpu_custom_call" | custom-call | tf_op jit(solution)/shard_map/pallas_call | solution.py:176
  55.4 1.3 %copy.32 = bf16[16,512]{1,0:T(8,128)(2,1)} copy(bf16[16,512]{1,0:T(8,128)(2,1)} %shard_map.74) | data formatting | bytes 32768
  (5 shorter events, 0.1 us)
Async XLA Ops:
  27.4 9.5 %copy-start = (bf16[8,4096,128]{2,1,0:T(8,128)(2,1)S(1)}, bf16[8,4096,128]{2,1,0:T(8,128)(2,1)}, u32[]{:S(2)}) copy-start(bf16[8,4096,128]{2,1,0:T(8,128)(2,1)} %param.12) | copy-start | bytes 25165828

commit v5 on v4

--- a/solution.py
+++ b/solution.py
@@ -104,10 +104,28 @@
 
 
 def project_kernel(req_n, head_n, x_ref, gain_ref, w_ref, o_ref,
-                   rows_buf, part, sums_buf, sems):
+                   rows_buf, part, pair_buf, mixed, sums_buf, sems):
     me_head = lax.axis_index("head")
     me_req = lax.axis_index("req")
-    greet((("head", me_head, head_n), ("req", me_req, req_n)))
+    chips = req_n // 2
+    me_core = lax.rem(me_req, 2)
+    me_chip = me_req // 2
+    partner = me_req + 1 - 2 * me_core
+    barrier = pltpu.get_barrier_semaphore()
+    for k in range(1, head_n):
+        pl.semaphore_signal(
+            barrier, inc=1, device_id={"head": lax.rem(me_head + k, head_n)},
+            device_id_type=pl.DeviceIdType.MESH,
+        )
+    pl.semaphore_signal(
+        barrier, inc=1, device_id={"req": partner}, device_id_type=pl.DeviceIdType.MESH
+    )
+    for k in range(1, chips):
+        pl.semaphore_signal(
+            barrier, inc=1, device_id={"req": lax.rem(me_chip + k, chips) * 2 + me_core},
+            device_id_type=pl.DeviceIdType.MESH,
+        )
+    pl.semaphore_wait(barrier, head_n - 1 + chips)
     own = lambda peer: x_ref
     sends = send_all("head", me_head, head_n, own, rows_buf, sems.at[0], sems.at[1])
     receive_all("head", me_head, head_n, own, rows_buf, sems.at[0], sems.at[1], sends)
@@ -116,16 +134,56 @@
     states = rows_buf[...].reshape(head_n * block_rows, x_ref.shape[1]).astype(jnp.float32)
     scaled = (states * gain_ref[...].astype(jnp.float32)[None, :]).astype(jnp.bfloat16)
     columns = w_ref.shape[1]
-    part[:, :columns] = jnp.dot(scaled, w_ref[...], preferred_element_type=jnp.float32)
     square = jnp.sum(states * states, axis=1, keepdims=True)
-    part[:, columns:] = jnp.broadcast_to(square, (square.shape[0], part.shape[1] - columns))
+    packed = jnp.concatenate(
+        [jnp.dot(scaled, w_ref[...], preferred_element_type=jnp.float32),
+         jnp.broadcast_to(square, (square.shape[0], part.shape[-1] - columns))],
+        axis=1,
+    )
     count = o_ref.shape[0]
-    chunk = lambda peer: part.at[pl.ds(pl.multiple_of(peer * count, count), count)]
-    sends = send_all("req", me_req, req_n, chunk, sums_buf, sems.at[2], sems.at[3])
-    receive_all("req", me_req, req_n, chunk, sums_buf, sems.at[2], sems.at[3], sends)
-    total = part[pl.ds(pl.multiple_of(me_req * count, count), count), :]
-    for k in range(1, req_n):
-        total = total + sums_buf[lax.rem(me_req + req_n - k, req_n)]
+    packed = packed.reshape(chips, 2, count, part.shape[-1])
+    part[0] = packed[:, 0]
+    part[1] = packed[:, 1]
+    pair = pltpu.make_async_remote_copy(
+        src_ref=part.at[1 - me_core],
+        dst_ref=pair_buf,
+        send_sem=sems.at[2, 0],
+        recv_sem=sems.at[3, 0],
+        device_id={"req": partner},
+        device_id_type=pl.DeviceIdType.MESH,
+    )
+    pair.start()
+    pair.wait()
+    mixed[...] = part[me_core] + pair_buf[...]
+    sends = []
+    for k in range(1, chips):
+        chip = lax.rem(me_chip + k, chips)
+        copy = pltpu.make_async_remote_copy(
+            src_ref=mixed.at[chip],
+            dst_ref=sums_buf.at[me_chip],
+            send_sem=sems.at[2, k],
+            recv_sem=sems.at[3, k],
+            device_id={"req": chip * 2 + me_core},
+            device_id_type=pl.DeviceIdType.MESH,
+        )
+        copy.start()
+        sends.append(copy)
+    for k in range(1, chips):
+        chip = lax.rem(me_chip + chips - k, chips)
+        arrival = pltpu.make_async_remote_copy(
+            src_ref=mixed.at[chip],
+            dst_ref=sums_buf.at[chip],
+            send_sem=sems.at[2, k],
+            recv_sem=sems.at[3, k],
+            device_id={"req": chip * 2 + me_core},
+            device_id_type=pl.DeviceIdType.MESH,
+        )
+        arrival.wait_recv()
+    for copy in sends:
+        copy.wait_send()
+    total = mixed[me_chip]
+    for k in range(1, chips):
+        total = total + sums_buf[lax.rem(me_chip + chips - k, chips)]
     mean_square = total[:, columns:columns + 1] / D
     o_ref[...] = total[:, :columns] * lax.rsqrt(mean_square + epsilon)
 
@@ -140,8 +198,10 @@
         out_specs=pl.BlockSpec(memory_space=pltpu.VMEM),
         scratch_shapes=[
             pltpu.VMEM((head_n, rows, width), hidden_in.dtype),
-            pltpu.VMEM((req_n * count, columns), jnp.float32),
-            pltpu.VMEM((req_n, count, columns), jnp.float32),
+            pltpu.VMEM((2, req_n // 2, count, columns), jnp.float32),
+            pltpu.VMEM((req_n // 2, count, columns), jnp.float32),
+            pltpu.VMEM((req_n // 2, count, columns), jnp.float32),
+            pltpu.VMEM((req_n // 2, count, columns), jnp.float32),
             pltpu.SemaphoreType.DMA((4, max(req_n, head_n))),
         ],
         compiler_params=pltpu.CompilerParams(collective_id=0, has_side_effects=True),

time: 57 us -> 55.4 us (0.972)
  Pallas kernels: 42.4 us -> 40.8 us
    pallas_call x1, Pallas kernels: 25.9 us -> 23.9 us  [project(): pl.pallas_call(functools.partial(project_kernel, req_n, head_n), out_shap...]
where the time goes in v5:
time: 55.4 us; the launch traced here: 55.1 us
  Pallas kernels  40.8 us (74%)
  matrix products  7.29 us (13%)
  local copies, waits for them, and re-layouts  3.9 us (7%)
  other arithmetic  3.06 us (6%)
    pallas_call x1, Pallas kernels, project(): pl.pallas_call(functools.partial(project_kernel, req_n, head_n), out_shap...  23.9 us
    pallas_call x1, Pallas kernels, output_block(): pl.pallas_call(functools.partial(output_kernel, req_n, head_n), out_shape...  16.9 us
    dot_general x1, matrix products, attend_padded(): jnp.einsum('rkgd,rpkd->rkgp', queries, cached_keys, preferred_element_typ...  5.77 us
    unnamed x4, local copies, waits for them, and re-layouts  1.96 us
    dot_general x1, matrix products, attend_padded(): jnp.einsum('rkgp,rpkd->rkgd', probs, cached_values, preferred_element_typ...  1.33 us
    slice x1, local copies, waits for them, and re-layouts, rotate(): second = vectors[..., halfway:]  1.12 us

profile of v5, /device:TPU:1, one launch (start us, length us, event | category | flops | bytes accessed | tf_op | source)
XLA Modules:
  0.0 55.1 jit_solution(1158381218812714577)
XLA Ops:
  0.0 0.7 %convert_element_type.36 = f32[8]{0:T(128)S(1)} convert(s32[8]{0:T(128)} %param.13) | non-fusion elementwise | flops 8 | bytes 64 | tf_op jit(solution)/shard_map/convert_element_type | solution.py:24
  0.7 0.1 multiply_cosine_fusion.1
  0.8 0.7 %iota_compare_fusion = pred[8,4096]{1,0:T(8,128)(4,1)S(1)} fusion(s32[8]{0:T(128)} %param.13), kind=kLoop, calls=%fused_computation.12 | loop fusion | flops 32768 | bytes 32800 | tf_op jit(solution)/shard_map/lt | solution.py:44
  1.5 23.9 %shard_map.73 = f32[8,1280]{1,0:T(8,128)} custom-call(bf16[16,512]{1,0:T(8,128)(2,1)} %s_ref.1, bf16[512]{0:T(512)(128)(2,1)} %gain_ref.1, bf16[512,1280]{1,0:T(8,128)(2,1)} %w_ref.2), custom_call_target="tpu_custom_call" | custom-call | tf_op jit(solution)/shard_map/pallas_call | solution.py:194
  25.4 0.0 copy-start
  25.5 0.8 %slice_bitcast_fusion = f32[8,1,128]{2,0,1:T(8,128)S(1)} fusion(f32[8,1,10,128]{3,0,2,1:T(8,128)} %bitcast.32), kind=kLoop, calls=%fused_computation.32 | loop fusion | bytes 8192 | tf_op jit(solution)/shard_map/squeeze | solution.py:258
  26.3 0.1 fusion.24
  26.4 0.1 maximum_bitcast_fusion
  26.5 0.9 %fusion.21 = f32[8,128]{1,0:T(8,128)S(1)} fusion(f32[8,1,10,128]{3,0,2,1:T(8,128)} %bitcast.33), kind=kLoop, calls=%fused_computation.39 | loop fusion | flops 1024 | bytes 6144 | tf_op jit(solution)/shard_map/mul | solution.py:39
  27.4 1.1 %fusion.29 = (f32[8,1,8,64]{3,0,2,1:T(8,128)S(1)}, f32[8,1,8,64]{3,0,2,1:T(8,128)S(1)}) fusion(f32[8,1,10,128]{3,0,2,1:T(8,128)} %bitcast.34), kind=kLoop, calls=%fused_computation.50 | loop fusion | bytes 65536 | tf_op jit(solution)/shard_map/slice | solution.py:29
  28.5 0.2 fusion.18
  28.7 5.8 %fusion.30 = (f32[8,8]{1,0:T(8,128)S(1)}, f32[8,8,4096]{2,1,0:T(8,128)S(1)}) fusion(bf16[8,4096,128]{2,1,0:T(8,128)(2,1)} %param.11, bf16[8,8,64]{2,1,0:T(8,128)(2,1)S(1)} %get-tuple-element.6, bf16[8,8,64]{2,1,0:T(8,128)(2,1)S(1)} %get-tuple-element.5, pred[8,4096]{1,0:T(8,128)(4,1)S(1)} %iota_compare_fusion), kind=kOutput, calls=%fused_computation.51 | convolution fusion | flops 67928000 | bytes 9486592 | tf_op jit(solution)/shard_map/rkgd,rpkd->rkgp/dot_general | solution.py:46
  34.5 0.4 fusion.3
  34.9 0.0 copy-done
  34.9 1.3 %fusion.2 = bf16[1,8,8,128]{3,2,1,0:T(8,128)(2,1)S(1)} fusion(bf16[8,4096,128]{2,1,0:T(8,128)(2,1)S(1)} %copy-done, f32[8,8,4096]{2,1,0:T(8,128)S(1)} %get-tuple-element.16, f32[8,8]{1,0:T(8,128)S(1)} %get-tuple-element.10, f32[8,8]{1,0:T(8,128)S(1)} %multiply_maximum_fusion, pred[8,4096]{1,0:T(8,128)(4,1)S(1)} %iota_compare_fusion, ...), kind=kOutput, calls=%fused_computation.4 | convolution fusion | flops 68182016 | bytes 9491200 | tf_op jit(solution)/shard_map/rkgp,rpkd->rkgd/dot_general | solution.py:57
  36.3 0.6 %copy.30 = bf16[1,8,8,128]{3,1,2,0:T(8,128)(2,1)} copy(bf16[1,8,8,128]{3,2,1,0:T(8,128)(2,1)S(1)} %fusion.2) | data formatting | bytes 32768
  36.9 16.9 %shard_map.74 = bf16[16,512]{1,0:T(8,128)(2,1)} custom-call(bf16[8,1024]{1,0:T(8,128)(2,1)} %bitcast.35, bf16[1024,512]{1,0:T(8,128)(2,1)} %w_ref.3, bf16[16,512]{1,0:T(8,128)(2,1)} %s_ref.1), custom_call_target="tpu_custom_call" | custom-call | tf_op jit(solution)/shard_map/pallas_call | solution.py:236
  53.8 1.3 %copy.32 = bf16[16,512]{1,0:T(8,128)(2,1)} copy(bf16[16,512]{1,0:T(8,128)(2,1)} %shard_map.74) | data formatting | bytes 32768
  (5 shorter events, 0.1 us)
Async XLA Ops:
  25.4 9.5 %copy-start = (bf16[8,4096,128]{2,1,0:T(8,128)(2,1)S(1)}, bf16[8,4096,128]{2,1,0:T(8,128)(2,1)}, u32[]{:S(2)}) copy-start(bf16[8,4096,128]{2,1,0:T(8,128)(2,1)} %param.12) | copy-start | bytes 25165828

commit v6 on v5

--- a/solution.py
+++ b/solution.py
@@ -111,21 +111,6 @@
     me_core = lax.rem(me_req, 2)
     me_chip = me_req // 2
     partner = me_req + 1 - 2 * me_core
-    barrier = pltpu.get_barrier_semaphore()
-    for k in range(1, head_n):
-        pl.semaphore_signal(
-            barrier, inc=1, device_id={"head": lax.rem(me_head + k, head_n)},
-            device_id_type=pl.DeviceIdType.MESH,
-        )
-    pl.semaphore_signal(
-        barrier, inc=1, device_id={"req": partner}, device_id_type=pl.DeviceIdType.MESH
-    )
-    for k in range(1, chips):
-        pl.semaphore_signal(
-            barrier, inc=1, device_id={"req": lax.rem(me_chip + k, chips) * 2 + me_core},
-            device_id_type=pl.DeviceIdType.MESH,
-        )
-    pl.semaphore_wait(barrier, head_n - 1 + chips)
     own = lambda peer: x_ref
     sends = send_all("head", me_head, head_n, own, rows_buf, sems.at[0], sems.at[1])
     receive_all("head", me_head, head_n, own, rows_buf, sems.at[0], sems.at[1], sends)
@@ -204,14 +189,13 @@
             pltpu.VMEM((req_n // 2, count, columns), jnp.float32),
             pltpu.SemaphoreType.DMA((4, max(req_n, head_n))),
         ],
-        compiler_params=pltpu.CompilerParams(collective_id=0, has_side_effects=True),
+        compiler_params=pltpu.CompilerParams(has_side_effects=True),
     )(hidden_in, gain, w_qkv)
 
 
 def output_kernel(req_n, head_n, a_ref, w_ref, s_ref, o_ref, att_buf, part, sums_buf, sems):
     me_head = lax.axis_index("head")
     me_req = lax.axis_index("req")
-    greet((("req", me_req, req_n), ("head", me_head, head_n)))
     own = lambda peer: a_ref
     sends = send_all("req", me_req, req_n, own, att_buf, sems.at[0], sems.at[1])
     receive_all("req", me_req, req_n, own, att_buf, sems.at[0], sems.at[1], sends)
@@ -244,7 +228,7 @@
             pltpu.VMEM((head_n, rows, columns), jnp.float32),
             pltpu.SemaphoreType.DMA((4, max(req_n, head_n))),
         ],
-        compiler_params=pltpu.CompilerParams(collective_id=1, has_side_effects=True),
+        compiler_params=pltpu.CompilerParams(has_side_effects=True),
     )(attended, w_out, hidden_in)
 
 

time: 55.4 us -> 67.5 us (1.22)
  Pallas kernels: 40.8 us -> 52.9 us
    pallas_call x1, Pallas kernels: 16.9 us -> 23.3 us  [output_block(): pl.pallas_call(functools.partial(output_kernel, req_n, head_n), out_shape...]
    pallas_call x1, Pallas kernels: 23.9 us -> 29.6 us  [project(): pl.pallas_call(functools.partial(project_kernel, req_n, head_n), out_shap...]
where the time goes in v6:
time: 67.5 us; the launch traced here: 67.2 us
  Pallas kernels  52.9 us (78%)
  matrix products  7.29 us (11%)
  local copies, waits for them, and re-layouts  3.9 us (6%)
  other arithmetic  3.06 us (5%)
    pallas_call x1, Pallas kernels, project(): pl.pallas_call(functools.partial(project_kernel, req_n, head_n), out_shap...  29.6 us
    pallas_call x1, Pallas kernels, output_block(): pl.pallas_call(functools.partial(output_kernel, req_n, head_n), out_shape...  23.3 us
    dot_general x1, matrix products, attend_padded(): jnp.einsum('rkgd,rpkd->rkgp', queries, cached_keys, preferred_element_typ...  5.77 us
    unnamed x4, local copies, waits for them, and re-layouts  1.96 us

profile of v6, /device:TPU:1, one launch (start us, length us, event | category | flops | bytes accessed | tf_op | source)
XLA Modules:
  0.0 67.2 jit_solution(16796799246089417796)
XLA Ops:
  0.0 0.7 convert_element_type.36
  0.7 0.1 multiply_cosine_fusion.1
  0.8 0.7 %iota_compare_fusion = pred[8,4096]{1,0:T(8,128)(4,1)S(1)} fusion(s32[8]{0:T(128)} %param.13), kind=kLoop, calls=%fused_computation.12 | loop fusion | flops 32768 | bytes 32800 | tf_op jit(solution)/shard_map/lt | solution.py:44
  1.5 29.6 %shard_map.73 = f32[8,1280]{1,0:T(8,128)} custom-call(bf16[16,512]{1,0:T(8,128)(2,1)} %s_ref.1, bf16[512]{0:T(512)(128)(2,1)} %gain_ref.1, bf16[512,1280]{1,0:T(8,128)(2,1)} %w_ref.2), custom_call_target="tpu_custom_call" | custom-call | tf_op jit(solution)/shard_map/pallas_call | solution.py:179
  31.2 0.0 copy-start
  31.2 0.8 %slice_bitcast_fusion = f32[8,1,128]{2,0,1:T(8,128)S(1)} fusion(f32[8,1,10,128]{3,0,2,1:T(8,128)} %bitcast.32), kind=kLoop, calls=%fused_computation.32 | loop fusion | bytes 8192 | tf_op jit(solution)/shard_map/squeeze | solution.py:242
  32.0 0.1 fusion.24
  32.1 0.1 maximum_bitcast_fusion
  32.2 0.9 %fusion.21 = f32[8,128]{1,0:T(8,128)S(1)} fusion(f32[8,1,10,128]{3,0,2,1:T(8,128)} %bitcast.33), kind=kLoop, calls=%fused_computation.39 | loop fusion | flops 1024 | bytes 6144 | tf_op jit(solution)/shard_map/mul | solution.py:39
  33.1 1.1 %fusion.29 = (f32[8,1,8,64]{3,0,2,1:T(8,128)S(1)}, f32[8,1,8,64]{3,0,2,1:T(8,128)S(1)}) fusion(f32[8,1,10,128]{3,0,2,1:T(8,128)} %bitcast.34), kind=kLoop, calls=%fused_computation.50 | loop fusion | bytes 65536 | tf_op jit(solution)/shard_map/slice | solution.py:29
  34.2 0.2 fusion.18
  34.4 5.8 %fusion.30 = (f32[8,8]{1,0:T(8,128)S(1)}, f32[8,8,4096]{2,1,0:T(8,128)S(1)}) fusion(bf16[8,4096,128]{2,1,0:T(8,128)(2,1)} %param.11, bf16[8,8,64]{2,1,0:T(8,128)(2,1)S(1)} %get-tuple-element.6, bf16[8,8,64]{2,1,0:T(8,128)(2,1)S(1)} %get-tuple-element.5, pred[8,4096]{1,0:T(8,128)(4,1)S(1)} %iota_compare_fusion), kind=kOutput, calls=%fused_computation.51 | convolution fusion | flops 67928000 | bytes 9486592 | tf_op jit(solution)/shard_map/rkgd,rpkd->rkgp/dot_general | solution.py:46
  40.2 0.4 fusion.3
  40.6 0.0 copy-done
  40.6 1.3 %fusion.2 = bf16[1,8,8,128]{3,2,1,0:T(8,128)(2,1)S(1)} fusion(bf16[8,4096,128]{2,1,0:T(8,128)(2,1)S(1)} %copy-done, f32[8,8,4096]{2,1,0:T(8,128)S(1)} %get-tuple-element.16, f32[8,8]{1,0:T(8,128)S(1)} %get-tuple-element.10, f32[8,8]{1,0:T(8,128)S(1)} %multiply_maximum_fusion, pred[8,4096]{1,0:T(8,128)(4,1)S(1)} %iota_compare_fusion, ...), kind=kOutput, calls=%fused_computation.4 | convolution fusion | flops 68182016 | bytes 9491200 | tf_op jit(solution)/shard_map/rkgp,rpkd->rkgd/dot_general | solution.py:57
  42.0 0.6 copy.30
  42.6 23.3 %shard_map.74 = bf16[16,512]{1,0:T(8,128)(2,1)} custom-call(bf16[8,1024]{1,0:T(8,128)(2,1)} %bitcast.35, bf16[1024,512]{1,0:T(8,128)(2,1)} %w_ref.3, bf16[16,512]{1,0:T(8,128)(2,1)} %s_ref.1), custom_call_target="tpu_custom_call" | custom-call | tf_op jit(solution)/shard_map/pallas_call | solution.py:220
  65.9 1.3 %copy.32 = bf16[16,512]{1,0:T(8,128)(2,1)} copy(bf16[16,512]{1,0:T(8,128)(2,1)} %shard_map.74) | data formatting | bytes 32768
  (5 shorter events, 0.1 us)
Async XLA Ops:
  31.2 9.5 %copy-start = (bf16[8,4096,128]{2,1,0:T(8,128)(2,1)S(1)}, bf16[8,4096,128]{2,1,0:T(8,128)(2,1)}, u32[]{:S(2)}) copy-start(bf16[8,4096,128]{2,1,0:T(8,128)(2,1)} %param.12) | copy-start | bytes 25165828

commit v7 on v5

--- a/solution.py
+++ b/solution.py
@@ -248,22 +248,100 @@
     )(attended, w_out, hidden_in)
 
 
+CHUNK = 512
+
+
+def attend_kernel(len_ref, q_ref, nk_ref, nv_ref, k_hbm, v_hbm, o_ref,
+                  keys, values, scores, rows, flat, sems):
+    count, slots = k_hbm.shape[0], k_hbm.shape[1]
+    chunks = slots // CHUNK
+    factor = HD ** (-0.5)
+
+    def chunk_copy(kind, b, c):
+        source = (k_hbm, v_hbm)[kind].at[b, pl.ds(c * CHUNK, CHUNK)]
+        target = (keys, values)[kind].at[b, pl.ds(c * CHUNK, CHUNK)]
+        return pltpu.make_async_copy(source, target, sems.at[kind, b, c])
+
+    for b in range(count):
+        live = (len_ref[b] + CHUNK - 1) // CHUNK
+        for kind in range(2):
+            for c in range(chunks):
+                @pl.when(c < live)
+                def _():
+                    chunk_copy(kind, b, c).start()
+    for b in range(count):
+        length = len_ref[b]
+        live = (length + CHUNK - 1) // CHUNK
+        q = q_ref[b]
+        for c in range(chunks):
+            @pl.when(c < live)
+            def _():
+                chunk_copy(0, b, c).wait()
+                scores[:, pl.ds(c * CHUNK, CHUNK)] = lax.dot_general(
+                    q, keys[b, pl.ds(c * CHUNK, CHUNK), :],
+                    (((1,), (1,)), ((), ())), preferred_element_type=jnp.float32,
+                ) * factor
+        inside = lax.broadcasted_iota(jnp.int32, scores.shape, 1) < length
+        masked = jnp.where(inside, scores[...], -1e30)
+        own = jnp.sum(
+            q.astype(jnp.float32) * nk_ref[pl.ds(b, 1), :].astype(jnp.float32),
+            axis=1, keepdims=True,
+        ) * factor
+        running = jnp.maximum(jnp.max(masked, axis=1, keepdims=True), own)
+        weights = jnp.where(inside, jnp.exp(masked - running), 0.0)
+        own_weight = jnp.exp(own - running)
+        totals = jnp.sum(weights, axis=1, keepdims=True) + own_weight
+        scores[...] = (weights / totals).astype(jnp.bfloat16).astype(jnp.float32)
+        own_prob = (own_weight / totals).astype(jnp.bfloat16).astype(jnp.float32)
+        rows[b] = own_prob * nv_ref[pl.ds(b, 1), :].astype(jnp.float32)
+        for c in range(chunks):
+            @pl.when(c < live)
+            def _():
+                chunk_copy(1, b, c).wait()
+                rows[b] += jnp.dot(
+                    scores[:, pl.ds(c * CHUNK, CHUNK)].astype(jnp.bfloat16),
+                    values[b, pl.ds(c * CHUNK, CHUNK), :],
+                    preferred_element_type=jnp.float32,
+                )
+    for b in range(count):
+        mixed = rows[b].astype(jnp.bfloat16).astype(jnp.float32)
+        for g in range(mixed.shape[0]):
+            flat[pl.ds(b, 1), pl.ds(g * HD, HD)] = mixed[g:g + 1, :]
+    o_ref[...] = flat[...].astype(o_ref.dtype)
+
+
+def attend(queries, new_keys, new_values, k_cache, v_cache, lengths):
+    count, slots, width = k_cache.shape
+    groups = queries.shape[1]
+    return pl.pallas_call(
+        attend_kernel,
+        out_shape=jax.ShapeDtypeStruct((count, groups * width), jnp.bfloat16),
+        in_specs=[pl.BlockSpec(memory_space=pltpu.SMEM)]
+        + [pl.BlockSpec(memory_space=pltpu.VMEM)] * 3
+        + [pl.BlockSpec(memory_space=pl.ANY)] * 2,
+        out_specs=pl.BlockSpec(memory_space=pltpu.VMEM),
+        scratch_shapes=[
+            pltpu.VMEM(k_cache.shape, k_cache.dtype),
+            pltpu.VMEM(v_cache.shape, v_cache.dtype),
+            pltpu.VMEM((groups, slots), jnp.float32),
+            pltpu.VMEM((count, groups, width), jnp.float32),
+            pltpu.VMEM((count, groups * width), jnp.float32),
+            pltpu.SemaphoreType.DMA((2, count, slots // CHUNK)),
+        ],
+        compiler_params=pltpu.CompilerParams(vmem_limit_bytes=48 * 1024 * 1024),
+    )(lengths, queries, new_keys, new_values, k_cache, v_cache)
+
+
 def local(req_n, head_n, hidden_in, attn_gain, w_qkv, w_out, k_cache, v_cache, lengths):
     own_count = k_cache.shape[0]
     projected = project(hidden_in, attn_gain, w_qkv, req_n, head_n, own_count)
     slots = k_cache.shape[1]
     local_heads = k_cache.shape[2] // HD
     projected = projected.reshape(own_count, local_heads, GROUP + 2, HD)
-    queries = rotate(projected[:, :, :GROUP], lengths).astype(jnp.bfloat16)
-    new_keys = rotate(projected[:, :, GROUP], lengths).astype(jnp.bfloat16)
-    new_values = projected[:, :, GROUP + 1].astype(jnp.bfloat16)
-    cached_keys = k_cache.reshape(own_count, slots, local_heads, HD)
-    cached_values = v_cache.reshape(own_count, slots, local_heads, HD)
-    factor = HD ** (-0.5)
-    attended = attend_padded(
-        queries, new_keys, new_values, cached_keys, cached_values, lengths, factor
-    )
-    flat_rows = attended.reshape(own_count, local_heads * GROUP * HD)
+    queries = rotate(projected[:, 0, :GROUP], lengths).astype(jnp.bfloat16)
+    new_keys = rotate(projected[:, 0, GROUP], lengths).astype(jnp.bfloat16)
+    new_values = projected[:, 0, GROUP + 1].astype(jnp.bfloat16)
+    flat_rows = attend(queries, new_keys, new_values, k_cache, v_cache, lengths)
     return output_block(flat_rows, w_out, hidden_in, req_n, head_n)
 
 

time: 55.4 us -> 62.4 us (1.13)
  Pallas kernels: 40.8 us -> 56.3 us
  matrix products: 7.29 us -> 0 us
  other arithmetic: 3.06 us -> 1.02 us
  local copies, waits for them, and re-layouts: 3.9 us -> 4.71 us
    pallas_call x0 -> x1, Pallas kernels: none -> 10.7 us  [attend(): pl.pallas_call(attend_kernel, out_shape=jax.ShapeDtypeStruct((count, grou...]
    dot_general x3 -> x0, matrix products: 7.29 us -> none  [the longest x1 5.77 us: attend_padded(): jnp.einsum('rkgd,rpkd->rkgp', queries, cached_keys, preferred_element_typ...]
    pallas_call x1, Pallas kernels: 16.9 us -> 21.8 us  [output_block(): pl.pallas_call(functools.partial(output_kernel, req_n, head_n), out_shape...]
    slice x1 -> x0, local copies, waits for them, and re-layouts: 1.12 us -> none  [rotate(): second = vectors[..., halfway:]]
    mul x2 -> x0, other arithmetic: 0.89 us -> none  [own_part(): own_prob.astype(jnp.float32)[..., None]]
    lt x1 -> x0, other arithmetic: 0.75 us -> none  [attend_padded(): inside = jnp.arange(slots, dtype=jnp.int32)[None, :] < lengths[:, None]]
    convert_element_type x0 -> x1, local copies, waits for them, and re-layouts: none -> 0.68 us  [local(): new_values = projected[:, 0, GROUP + 1].astype(jnp.bfloat16)]
    squeeze x1 -> x2, local copies, waits for them, and re-layouts: 0.83 us -> 1.44 us  [the longest x1 0.76 us: local(): queries = rotate(projected[:, 0, :GROUP], lengths).astype(jnp.bfloat16)]
where the time goes in v7:
time: 62.4 us; the launch traced here: 62.1 us
  Pallas kernels  56.3 us (90%)
  local copies, waits for them, and re-layouts  4.71 us (8%)
  other arithmetic  1.02 us (2%)
    pallas_call x1, Pallas kernels, project(): pl.pallas_call(functools.partial(project_kernel, req_n, head_n), out_shap...  23.8 us
    pallas_call x1, Pallas kernels, output_block(): pl.pallas_call(functools.partial(output_kernel, req_n, head_n), out_shape...  21.8 us
    pallas_call x1, Pallas kernels, attend(): pl.pallas_call(attend_kernel, out_shape=jax.ShapeDtypeStruct((count, grou...  10.7 us
    unnamed x5, local copies, waits for them, and re-layouts  2.57 us

profile of v7, /device:TPU:1, one launch (start us, length us, event | category | flops | bytes accessed | tf_op | source)
XLA Modules:
  0.0 62.1 jit_solution(12129607676891908680)
XLA Ops:
  0.0 0.7 %convert_element_type.4 = f32[8]{0:T(128)S(1)} convert(s32[8]{0:T(128)} %len_ref.1) | non-fusion elementwise | flops 8 | bytes 64 | tf_op jit(solution)/shard_map/convert_element_type | solution.py:24
  0.7 23.8 %shard_map.73 = f32[8,1280]{1,0:T(8,128)} custom-call(bf16[16,512]{1,0:T(8,128)(2,1)} %s_ref.1, bf16[512]{0:T(512)(128)(2,1)} %gain_ref.1, bf16[512,1280]{1,0:T(8,128)(2,1)} %w_ref.2), custom_call_target="tpu_custom_call" | custom-call | tf_op jit(solution)/shard_map/pallas_call | solution.py:194
  24.5 0.7 %fusion.nv_ref = bf16[8,128]{1,0:T(8,128)(2,1)S(1)} fusion(f32[8,1,10,128]{3,0,2,1:T(8,128)} %bitcast.7), kind=kLoop, calls=%fused_computation.10 | loop fusion | bytes 4096 | tf_op jit(solution)/shard_map/convert_element_type | solution.py:343
  25.2 0.7 %slice_bitcast_fusion.1 = f32[8,128]{1,0:T(8,128)S(1)} fusion(f32[8,1,10,128]{3,0,2,1:T(8,128)} %bitcast.8), kind=kLoop, calls=%fused_computation.7 | loop fusion | bytes 8192 | tf_op jit(solution)/shard_map/squeeze | solution.py:342
  25.9 0.8 %slice_bitcast_fusion = f32[8,8,128]{2,0,1:T(8,128)S(1)} fusion(f32[8,1,10,128]{3,0,2,1:T(8,128)} %bitcast.9), kind=kLoop, calls=%fused_computation | loop fusion | bytes 65536 | tf_op jit(solution)/shard_map/squeeze | solution.py:341
  26.6 0.1 subtract_convert_fusion.1
  26.7 0.1 pad_maximum_fusion.1.nk_ref
  26.8 0.1 subtract_convert_fusion
  26.9 0.1 pad_maximum_fusion
  27.0 0.0 copy-start.1
  27.0 0.6 %copy-done.1 = s32[8]{0:T(128)S(1)} copy-done((s32[8]{0:T(128)S(1)}, s32[8]{0:T(128)}, u32[]{:S(2)}) %copy-start.1) | copy-done | bytes 56
  27.7 10.7 %shard_map.74.a_ref = bf16[8,1024]{1,0:T(8,128)(2,1)S(1)} custom-call(s32[8]{0:T(128)S(1)} %copy-done.1, bf16[8,8,128]{2,1,0:T(8,128)(2,1)S(1)} %copy.8.q_ref, bf16[8,128]{1,0:T(8,128)(2,1)S(1)} %pad_maximum_fusion.1.nk_ref, bf16[8,128]{1,0:T(8,128)(2,1)S(1)} %fusion.nv_ref, bf16[8,4096,128]{2,1,0:T(8,128)(2,1)} %k_hbm.1, bf16[8,4096,128]{2,1,0:T(8,128)(2,1)} %v_hbm.1), custom_call_target="tpu_custom_call" | custom-call | tf_op jit(solution)/shard_map/pallas_call | solution.py:316
  38.3 0.0 copy-start
  38.3 0.6 copy-done
  38.9 21.8 %shard_map.75 = bf16[16,512]{1,0:T(8,128)(2,1)} custom-call(bf16[8,1024]{1,0:T(8,128)(2,1)} %copy-done, bf16[1024,512]{1,0:T(8,128)(2,1)} %w_ref.3, bf16[16,512]{1,0:T(8,128)(2,1)} %s_ref.1), custom_call_target="tpu_custom_call" | custom-call | tf_op jit(solution)/shard_map/pallas_call | solution.py:236
  60.8 1.3 %copy.10 = bf16[16,512]{1,0:T(8,128)(2,1)} copy(bf16[16,512]{1,0:T(8,128)(2,1)} %shard_map.75) | data formatting | bytes 32768
  (2 shorter events, 0.0 us)
Async XLA Ops:
  27.0 0.7 %copy-start.1 = (s32[8]{0:T(128)S(1)}, s32[8]{0:T(128)}, u32[]{:S(2)}) copy-start(s32[8]{0:T(128)} %len_ref.1) | copy-start | bytes 100
  38.3 0.6 copy-start

commit v8 on v5

--- a/solution.py
+++ b/solution.py
@@ -103,7 +103,7 @@
         copy.wait_send()
 
 
-def project_kernel(req_n, head_n, x_ref, gain_ref, w_ref, o_ref,
+def project_kernel(req_n, head_n, x_ref, gain_ref, w_ref, cos_ref, sin_ref, q_ref, k_ref, v_ref,
                    rows_buf, part, pair_buf, mixed, sums_buf, sems):
     me_head = lax.axis_index("head")
     me_req = lax.axis_index("req")
@@ -140,7 +140,7 @@
          jnp.broadcast_to(square, (square.shape[0], part.shape[-1] - columns))],
         axis=1,
     )
-    count = o_ref.shape[0]
+    count = k_ref.shape[0]
     packed = packed.reshape(chips, 2, count, part.shape[-1])
     part[0] = packed[:, 0]
     part[1] = packed[:, 1]
@@ -185,17 +185,34 @@
     for k in range(1, chips):
         total = total + sums_buf[lax.rem(me_chip + chips - k, chips)]
     mean_square = total[:, columns:columns + 1] / D
-    o_ref[...] = total[:, :columns] * lax.rsqrt(mean_square + epsilon)
-
-
-def project(hidden_in, gain, w_qkv, req_n, head_n, count):
+    projected = total[:, :columns] * lax.rsqrt(mean_square + epsilon)
+    cosine, sine = cos_ref[...], sin_ref[...]
+    rotated = lambda block: block * cosine + pltpu.roll(block, HD // 2, 1) * sine
+    for g in range(GROUP):
+        q_ref[g] = rotated(projected[:, g * HD:(g + 1) * HD]).astype(jnp.bfloat16).astype(jnp.float32)
+    k_ref[...] = rotated(projected[:, GROUP * HD:(GROUP + 1) * HD]).astype(k_ref.dtype)
+    v_ref[...] = projected[:, (GROUP + 1) * HD:].astype(v_ref.dtype)
+
+
+def project(hidden_in, gain, w_qkv, lengths, req_n, head_n, count):
     rows, width = hidden_in.shape
     columns = w_qkv.shape[1] + 128
+    halfway = HD // 2
+    frequency = jnp.exp(
+        -jnp.log(rope_base) * 2.0 * jnp.arange(halfway, dtype=jnp.float32) / HD
+    )
+    angles = lengths.astype(jnp.float32)[:, None] * frequency[None, :]
+    cosine = jnp.concatenate([jnp.cos(angles), jnp.cos(angles)], axis=1)
+    sine = jnp.concatenate([-jnp.sin(angles), jnp.sin(angles)], axis=1)
     return pl.pallas_call(
         functools.partial(project_kernel, req_n, head_n),
-        out_shape=jax.ShapeDtypeStruct((count, w_qkv.shape[1]), jnp.float32),
-        in_specs=[pl.BlockSpec(memory_space=pltpu.VMEM)] * 3,
-        out_specs=pl.BlockSpec(memory_space=pltpu.VMEM),
+        out_shape=(
+            jax.ShapeDtypeStruct((GROUP, count, HD), jnp.float32),
+            jax.ShapeDtypeStruct((count, HD), jnp.bfloat16),
+            jax.ShapeDtypeStruct((count, HD), jnp.bfloat16),
+        ),
+        in_specs=[pl.BlockSpec(memory_space=pltpu.VMEM)] * 5,
+        out_specs=(pl.BlockSpec(memory_space=pltpu.VMEM),) * 3,
         scratch_shapes=[
             pltpu.VMEM((head_n, rows, width), hidden_in.dtype),
             pltpu.VMEM((2, req_n // 2, count, columns), jnp.float32),
@@ -205,7 +222,7 @@
             pltpu.SemaphoreType.DMA((4, max(req_n, head_n))),
         ],
         compiler_params=pltpu.CompilerParams(collective_id=0, has_side_effects=True),
-    )(hidden_in, gain, w_qkv)
+    )(hidden_in, gain, w_qkv, cosine, sine)
 
 
 def output_kernel(req_n, head_n, a_ref, w_ref, s_ref, o_ref, att_buf, part, sums_buf, sems):
@@ -250,13 +267,14 @@
 
 def local(req_n, head_n, hidden_in, attn_gain, w_qkv, w_out, k_cache, v_cache, lengths):
     own_count = k_cache.shape[0]
-    projected = project(hidden_in, attn_gain, w_qkv, req_n, head_n, own_count)
+    queries, new_keys, new_values = project(
+        hidden_in, attn_gain, w_qkv, lengths, req_n, head_n, own_count
+    )
     slots = k_cache.shape[1]
     local_heads = k_cache.shape[2] // HD
-    projected = projected.reshape(own_count, local_heads, GROUP + 2, HD)
-    queries = rotate(projected[:, :, :GROUP], lengths).astype(jnp.bfloat16)
-    new_keys = rotate(projected[:, :, GROUP], lengths).astype(jnp.bfloat16)
-    new_values = projected[:, :, GROUP + 1].astype(jnp.bfloat16)
+    queries = jnp.transpose(queries.astype(jnp.bfloat16), (1, 0, 2))[:, None]
+    new_keys = new_keys[:, None]
+    new_values = new_values[:, None]
     cached_keys = k_cache.reshape(own_count, slots, local_heads, HD)
     cached_values = v_cache.reshape(own_count, slots, local_heads, HD)
     factor = HD ** (-0.5)

time: 55.4 us -> 55.6 us (level)
  local copies, waits for them, and re-layouts: 3.9 us -> 1.96 us
  other arithmetic: 3.06 us -> 4.53 us
  matrix products: 7.29 us -> 8.01 us
    slice x1 -> x0, local copies, waits for them, and re-layouts: 1.12 us -> none  [rotate(): second = vectors[..., halfway:]]
    convert_element_type x1 -> x2, other arithmetic: 0.66 us -> 1.65 us  [the longest x1 0.99 us: own_part(): new_values.astype(jnp.float32)[:, :, None, :]]
    transpose x0 -> x1, other arithmetic: none -> 0.91 us  [local(): queries = jnp.transpose(queries.astype(jnp.bfloat16), (1, 0, 2))[:, None]]
    mul x2 -> x1, other arithmetic: 0.89 us -> 0.01 us  [own_part(): own_prob.astype(jnp.float32)[..., None]]
    squeeze x1 -> x0, local copies, waits for them, and re-layouts: 0.83 us -> none  [local(): new_keys = rotate(projected[:, :, GROUP], lengths).astype(jnp.bfloat16)]
    dot_general x1, matrix products: 0.19 us -> 0.93 us  [attend_padded(): jnp.einsum('rkgd,rkd->rkg', queries, new_keys, preferred_element_type=jnp...]
where the time goes in v8:
time: 55.6 us; the launch traced here: 55.4 us
  Pallas kernels  40.8 us (73%)
  matrix products  8.01 us (14%)
  other arithmetic  4.53 us (8%)
  local copies, waits for them, and re-layouts  1.96 us (4%)
    pallas_call x1, Pallas kernels, project(): pl.pallas_call(functools.partial(project_kernel, req_n, head_n), out_shap...  23.9 us
    pallas_call x1, Pallas kernels, output_block(): pl.pallas_call(functools.partial(output_kernel, req_n, head_n), out_shape...  16.9 us
    dot_general x1, matrix products, attend_padded(): jnp.einsum('rkgd,rpkd->rkgp', queries, cached_keys, preferred_element_typ...  5.73 us
    unnamed x4, local copies, waits for them, and re-layouts  1.96 us
    dot_general x1, matrix products, attend_padded(): jnp.einsum('rkgp,rpkd->rkgd', probs, cached_values, preferred_element_typ...  1.35 us

profile of v8, /device:TPU:1, one launch (start us, length us, event | category | flops | bytes accessed | tf_op | source)
XLA Modules:
  0.0 55.4 jit_solution(4176806670703199526)
XLA Ops:
  0.0 0.7 %convert_element_type.25 = f32[8]{0:T(128)S(1)} convert(s32[8]{0:T(128)} %param.13) | non-fusion elementwise | flops 8 | bytes 64 | tf_op jit(solution)/shard_map/convert_element_type | solution.py:204
  0.7 0.1 fusion.14
  0.8 0.7 %pad_maximum_fusion = (f32[8,128]{1,0:T(8,128)}, f32[8,128]{1,0:T(8,128)}) fusion(f32[8,64]{1,0:T(8,128)S(1)} %get-tuple-element.15, f32[8,64]{1,0:T(8,128)S(1)} %get-tuple-element.14, f32[8,64]{1,0:T(8,128)S(1)} %get-tuple-element.13), kind=kLoop, calls=%fused_computation.20 | loop fusion | flops 2048 | bytes 14336 | tf_op jit(solution)/shard_map/concatenate | solution.py:205
  1.5 23.9 %shard_map.73 = (f32[8,8,128]{2,1,0:T(8,128)}, bf16[8,128]{1,0:T(8,128)(2,1)}, bf16[8,128]{1,0:T(8,128)(2,1)}) custom-call(bf16[16,512]{1,0:T(8,128)(2,1)} %s_ref.1, bf16[512]{0:T(512)(128)(2,1)} %gain_ref.1, bf16[512,1280]{1,0:T(8,128)(2,1)} %w_ref.2, f32[8,128]{1,0:T(8,128)} %get-tuple-element.18.cos_ref, f32[8,128]{1,0:T(8,128)} %get-tuple-element.19.sin_ref), custom_call_target="tpu_custom_call" | custom-call | tf_op jit(solution)/shard_map/pallas_call | solution.py:207
  25.4 0.0 copy-start
  25.4 0.9 %convert_bitcast_fusion = bf16[8,8,128]{2,0,1:T(8,128)(2,1)S(1)} fusion(f32[8,8,128]{2,1,0:T(8,128)} %get-tuple-element.8), kind=kLoop, calls=%fused_computation.14 | loop fusion | flops 8192 | bytes 49152 | tf_op jit(solution)/shard_map/transpose | solution.py:275
  26.3 0.9 %fusion.8 = f32[8,1,8]{2,1,0:T(1,128)S(1)} fusion(bf16[8,8,128]{2,0,1:T(8,128)(2,1)S(1)} %convert_bitcast_fusion, bf16[8,128,1]{1,0,2:T(8,128)(2,1)} %bitcast.20), kind=kOutput, calls=%fused_computation.15 | convolution fusion | flops 16384 | bytes 18688 | tf_op jit(solution)/shard_map/rkgd,rkd->rkg/dot_general | solution.py:51
  27.3 1.0 %convert_element_type.30 = f32[8,128]{1,0:T(8,128)S(1)} convert(bf16[8,128]{1,0:T(8,128)(2,1)} %get-tuple-element.10) | non-fusion elementwise | flops 1024 | bytes 6144 | tf_op jit(solution)/shard_map/convert_element_type | solution.py:39
  28.3 0.7 %iota_compare_fusion = pred[8,4096]{1,0:T(8,128)(4,1)S(1)} fusion(s32[8]{0:T(128)} %param.13), kind=kLoop, calls=%fused_computation.12 | loop fusion | flops 32768 | bytes 32800 | tf_op jit(solution)/shard_map/lt | solution.py:44
  29.0 5.7 %fusion.16 = (f32[8,8]{1,0:T(8,128)S(1)}, f32[8,8,4096]{2,1,0:T(8,128)S(1)}) fusion(bf16[8,4096,128]{2,1,0:T(8,128)(2,1)} %param.11, bf16[8,8,128]{2,0,1:T(8,128)(2,1)S(1)} %convert_bitcast_fusion, pred[8,4096]{1,0:T(8,128)(4,1)S(1)} %iota_compare_fusion), kind=kOutput, calls=%fused_computation.32 | convolution fusion | flops 67895232 | bytes 9486592 | tf_op jit(solution)/shard_map/rkgd,rpkd->rkgp/dot_general | solution.py:46
  34.7 0.4 fusion.3
  35.2 0.0 copy-done
  35.2 1.3 %fusion.2 = bf16[1,8,8,128]{3,2,1,0:T(8,128)(2,1)S(1)} fusion(bf16[8,4096,128]{2,1,0:T(8,128)(2,1)S(1)} %copy-done, f32[8,8,4096]{2,1,0:T(8,128)S(1)} %get-tuple-element.17, f32[8,8]{1,0:T(8,128)S(1)} %get-tuple-element.12, f32[8,8]{1,0:T(8,128)S(1)} %multiply_maximum_fusion, pred[8,4096]{1,0:T(8,128)(4,1)S(1)} %iota_compare_fusion, ...), kind=kOutput, calls=%fused_computation.4 | convolution fusion | flops 68182016 | bytes 9491200 | tf_op jit(solution)/shard_map/rkgp,rpkd->rkgd/dot_general | solution.py:57
  36.5 0.6 %copy.21 = bf16[1,8,8,128]{3,1,2,0:T(8,128)(2,1)} copy(bf16[1,8,8,128]{3,2,1,0:T(8,128)(2,1)S(1)} %fusion.2) | data formatting | bytes 32768
  37.1 16.9 %shard_map.74 = bf16[16,512]{1,0:T(8,128)(2,1)} custom-call(bf16[8,1024]{1,0:T(8,128)(2,1)} %bitcast.17, bf16[1024,512]{1,0:T(8,128)(2,1)} %w_ref.3, bf16[16,512]{1,0:T(8,128)(2,1)} %s_ref.1), custom_call_target="tpu_custom_call" | custom-call | tf_op jit(solution)/shard_map/pallas_call | solution.py:253
  54.1 1.3 %copy.23 = bf16[16,512]{1,0:T(8,128)(2,1)} copy(bf16[16,512]{1,0:T(8,128)(2,1)} %shard_map.74) | data formatting | bytes 32768
  (4 shorter events, 0.0 us)
Async XLA Ops:
  25.4 9.8 %copy-start = (bf16[8,4096,128]{2,1,0:T(8,128)(2,1)S(1)}, bf16[8,4096,128]{2,1,0:T(8,128)(2,1)}, u32[]{:S(2)}) copy-start(bf16[8,4096,128]{2,1,0:T(8,128)(2,1)} %param.12) | copy-start | bytes 25165828

commit v9 on v8

--- a/solution.py
+++ b/solution.py
@@ -103,14 +103,16 @@
         copy.wait_send()
 
 
-def project_kernel(req_n, head_n, x_ref, gain_ref, w_ref, cos_ref, sin_ref, q_ref, k_ref, v_ref,
-                   rows_buf, part, pair_buf, mixed, sums_buf, sems):
+def project_kernel(req_n, head_n, x_ref, gain_ref, w_hbm, cos_ref, sin_ref, q_ref, k_ref, v_ref,
+                   w_ref, rows_buf, part, pair_buf, mixed, sums_buf, sems, w_sem):
     me_head = lax.axis_index("head")
     me_req = lax.axis_index("req")
     chips = req_n // 2
     me_core = lax.rem(me_req, 2)
     me_chip = me_req // 2
     partner = me_req + 1 - 2 * me_core
+    w_copy = pltpu.make_async_copy(w_hbm, w_ref, w_sem)
+    w_copy.start()
     barrier = pltpu.get_barrier_semaphore()
     for k in range(1, head_n):
         pl.semaphore_signal(
@@ -135,6 +137,7 @@
     scaled = (states * gain_ref[...].astype(jnp.float32)[None, :]).astype(jnp.bfloat16)
     columns = w_ref.shape[1]
     square = jnp.sum(states * states, axis=1, keepdims=True)
+    w_copy.wait()
     packed = jnp.concatenate(
         [jnp.dot(scaled, w_ref[...], preferred_element_type=jnp.float32),
          jnp.broadcast_to(square, (square.shape[0], part.shape[-1] - columns))],
@@ -211,23 +214,30 @@
             jax.ShapeDtypeStruct((count, HD), jnp.bfloat16),
             jax.ShapeDtypeStruct((count, HD), jnp.bfloat16),
         ),
-        in_specs=[pl.BlockSpec(memory_space=pltpu.VMEM)] * 5,
+        in_specs=[pl.BlockSpec(memory_space=pltpu.VMEM)] * 2
+        + [pl.BlockSpec(memory_space=pl.ANY)]
+        + [pl.BlockSpec(memory_space=pltpu.VMEM)] * 2,
         out_specs=(pl.BlockSpec(memory_space=pltpu.VMEM),) * 3,
         scratch_shapes=[
+            pltpu.VMEM(w_qkv.shape, w_qkv.dtype),
             pltpu.VMEM((head_n, rows, width), hidden_in.dtype),
             pltpu.VMEM((2, req_n // 2, count, columns), jnp.float32),
             pltpu.VMEM((req_n // 2, count, columns), jnp.float32),
             pltpu.VMEM((req_n // 2, count, columns), jnp.float32),
             pltpu.VMEM((req_n // 2, count, columns), jnp.float32),
             pltpu.SemaphoreType.DMA((4, max(req_n, head_n))),
+            pltpu.SemaphoreType.DMA(()),
         ],
         compiler_params=pltpu.CompilerParams(collective_id=0, has_side_effects=True),
     )(hidden_in, gain, w_qkv, cosine, sine)
 
 
-def output_kernel(req_n, head_n, a_ref, w_ref, s_ref, o_ref, att_buf, part, sums_buf, sems):
+def output_kernel(req_n, head_n, a_ref, w_hbm, s_ref, o_ref, w_ref, att_buf, part, sums_buf,
+                  sems, w_sem):
     me_head = lax.axis_index("head")
     me_req = lax.axis_index("req")
+    w_copy = pltpu.make_async_copy(w_hbm, w_ref, w_sem)
+    w_copy.start()
     greet((("req", me_req, req_n), ("head", me_head, head_n)))
     own = lambda peer: a_ref
     sends = send_all("req", me_req, req_n, own, att_buf, sems.at[0], sems.at[1])
@@ -236,6 +246,7 @@
     every = jnp.concatenate(
         [att_buf[s].astype(jnp.float32) for s in range(req_n)], axis=0
     ).astype(jnp.bfloat16)
+    w_copy.wait()
     part[...] = jnp.dot(every, w_ref[...], preferred_element_type=jnp.float32)
     rows = o_ref.shape[0]
     chunk = lambda peer: part.at[pl.ds(pl.multiple_of(peer * rows, rows), rows)]
@@ -253,13 +264,19 @@
     return pl.pallas_call(
         functools.partial(output_kernel, req_n, head_n),
         out_shape=jax.ShapeDtypeStruct((rows, columns), hidden_in.dtype),
-        in_specs=[pl.BlockSpec(memory_space=pltpu.VMEM)] * 3,
+        in_specs=[
+            pl.BlockSpec(memory_space=pltpu.VMEM),
+            pl.BlockSpec(memory_space=pl.ANY),
+            pl.BlockSpec(memory_space=pltpu.VMEM),
+        ],
         out_specs=pl.BlockSpec(memory_space=pltpu.VMEM),
         scratch_shapes=[
+            pltpu.VMEM(w_out.shape, w_out.dtype),
             pltpu.VMEM((req_n, count, width), attended.dtype),
             pltpu.VMEM((head_n * rows, columns), jnp.float32),
             pltpu.VMEM((head_n, rows, columns), jnp.float32),
             pltpu.SemaphoreType.DMA((4, max(req_n, head_n))),
+            pltpu.SemaphoreType.DMA(()),
         ],
         compiler_params=pltpu.CompilerParams(collective_id=1, has_side_effects=True),
     )(attended, w_out, hidden_in)

time: 55.6 us -> 54.9 us (0.987)
  Pallas kernels: 40.8 us -> 39.9 us
where the time goes in v9:
time: 54.9 us; the launch traced here: 54.4 us
  Pallas kernels  39.9 us (73%)
  matrix products  8.01 us (15%)
  other arithmetic  4.53 us (8%)
  local copies, waits for them, and re-layouts  1.96 us (4%)
    pallas_call x1, Pallas kernels, project(): pl.pallas_call(functools.partial(project_kernel, req_n, head_n), out_shap...  23.4 us
    pallas_call x1, Pallas kernels, output_block(): pl.pallas_call(functools.partial(output_kernel, req_n, head_n), out_shape...  16.4 us
    dot_general x1, matrix products, attend_padded(): jnp.einsum('rkgd,rpkd->rkgp', queries, cached_keys, preferred_element_typ...  5.73 us
    unnamed x4, local copies, waits for them, and re-layouts  1.96 us
    dot_general x1, matrix products, attend_padded(): jnp.einsum('rkgp,rpkd->rkgd', probs, cached_values, preferred_element_typ...  1.35 us

profile of v9, /device:TPU:1, one launch (start us, length us, event | category | flops | bytes accessed | tf_op | source)
XLA Modules:
  0.0 54.4 jit_solution(17572043411309914335)
XLA Ops:
  0.0 0.7 %convert_element_type.25 = f32[8]{0:T(128)S(1)} convert(s32[8]{0:T(128)} %param.13) | non-fusion elementwise | flops 8 | bytes 64 | tf_op jit(solution)/shard_map/convert_element_type | solution.py:207
  0.7 0.1 fusion.14
  0.8 0.7 %pad_maximum_fusion = (f32[8,128]{1,0:T(8,128)}, f32[8,128]{1,0:T(8,128)}) fusion(f32[8,64]{1,0:T(8,128)S(1)} %get-tuple-element.15, f32[8,64]{1,0:T(8,128)S(1)} %get-tuple-element.14, f32[8,64]{1,0:T(8,128)S(1)} %get-tuple-element.13), kind=kLoop, calls=%fused_computation.20 | loop fusion | flops 2048 | bytes 14336 | tf_op jit(solution)/shard_map/concatenate | solution.py:208
  1.5 23.4 %shard_map.73 = (f32[8,8,128]{2,1,0:T(8,128)}, bf16[8,128]{1,0:T(8,128)(2,1)}, bf16[8,128]{1,0:T(8,128)(2,1)}) custom-call(bf16[16,512]{1,0:T(8,128)(2,1)} %s_ref.1, bf16[512]{0:T(512)(128)(2,1)} %gain_ref.1, bf16[512,1280]{1,0:T(8,128)(2,1)} %w_hbm.2, f32[8,128]{1,0:T(8,128)} %get-tuple-element.18.cos_ref, f32[8,128]{1,0:T(8,128)} %get-tuple-element.19.sin_ref), custom_call_target="tpu_custom_call" | custom-call | tf_op jit(solution)/shard_map/pallas_call | solution.py:210
  24.9 0.0 copy-start
  24.9 0.9 %convert_bitcast_fusion = bf16[8,8,128]{2,0,1:T(8,128)(2,1)S(1)} fusion(f32[8,8,128]{2,1,0:T(8,128)} %get-tuple-element.8), kind=kLoop, calls=%fused_computation.14 | loop fusion | flops 8192 | bytes 49152 | tf_op jit(solution)/shard_map/transpose | solution.py:292
  25.8 0.9 %fusion.8 = f32[8,1,8]{2,1,0:T(1,128)S(1)} fusion(bf16[8,8,128]{2,0,1:T(8,128)(2,1)S(1)} %convert_bitcast_fusion, bf16[8,128,1]{1,0,2:T(8,128)(2,1)} %bitcast.20), kind=kOutput, calls=%fused_computation.15 | convolution fusion | flops 16384 | bytes 18688 | tf_op jit(solution)/shard_map/rkgd,rkd->rkg/dot_general | solution.py:51
  26.8 1.0 %convert_element_type.30 = f32[8,128]{1,0:T(8,128)S(1)} convert(bf16[8,128]{1,0:T(8,128)(2,1)} %get-tuple-element.10) | non-fusion elementwise | flops 1024 | bytes 6144 | tf_op jit(solution)/shard_map/convert_element_type | solution.py:39
  27.8 0.7 %iota_compare_fusion = pred[8,4096]{1,0:T(8,128)(4,1)S(1)} fusion(s32[8]{0:T(128)} %param.13), kind=kLoop, calls=%fused_computation.12 | loop fusion | flops 32768 | bytes 32800 | tf_op jit(solution)/shard_map/lt | solution.py:44
  28.5 5.7 %fusion.16 = (f32[8,8]{1,0:T(8,128)S(1)}, f32[8,8,4096]{2,1,0:T(8,128)S(1)}) fusion(bf16[8,4096,128]{2,1,0:T(8,128)(2,1)} %param.11, bf16[8,8,128]{2,0,1:T(8,128)(2,1)S(1)} %convert_bitcast_fusion, pred[8,4096]{1,0:T(8,128)(4,1)S(1)} %iota_compare_fusion), kind=kOutput, calls=%fused_computation.32 | convolution fusion | flops 67895232 | bytes 9486592 | tf_op jit(solution)/shard_map/rkgd,rpkd->rkgp/dot_general | solution.py:46
  34.2 0.4 fusion.3
  34.7 0.0 copy-done
  34.7 1.3 %fusion.2 = bf16[1,8,8,128]{3,2,1,0:T(8,128)(2,1)S(1)} fusion(bf16[8,4096,128]{2,1,0:T(8,128)(2,1)S(1)} %copy-done, f32[8,8,4096]{2,1,0:T(8,128)S(1)} %get-tuple-element.17, f32[8,8]{1,0:T(8,128)S(1)} %get-tuple-element.12, f32[8,8]{1,0:T(8,128)S(1)} %multiply_maximum_fusion, pred[8,4096]{1,0:T(8,128)(4,1)S(1)} %iota_compare_fusion, ...), kind=kOutput, calls=%fused_computation.4 | convolution fusion | flops 68182016 | bytes 9491200 | tf_op jit(solution)/shard_map/rkgp,rpkd->rkgd/dot_general | solution.py:57
  36.0 0.6 %copy.21 = bf16[1,8,8,128]{3,1,2,0:T(8,128)(2,1)} copy(bf16[1,8,8,128]{3,2,1,0:T(8,128)(2,1)S(1)} %fusion.2) | data formatting | bytes 32768
  36.7 16.4 %shard_map.74 = bf16[16,512]{1,0:T(8,128)(2,1)} custom-call(bf16[8,1024]{1,0:T(8,128)(2,1)} %bitcast.17, bf16[1024,512]{1,0:T(8,128)(2,1)} %w_hbm.3, bf16[16,512]{1,0:T(8,128)(2,1)} %s_ref.1), custom_call_target="tpu_custom_call" | custom-call | tf_op jit(solution)/shard_map/pallas_call | solution.py:264
  53.1 1.3 %copy.23 = bf16[16,512]{1,0:T(8,128)(2,1)} copy(bf16[16,512]{1,0:T(8,128)(2,1)} %shard_map.74) | data formatting | bytes 32768
  (4 shorter events, 0.0 us)
Async XLA Ops:
  24.9 9.8 %copy-start = (bf16[8,4096,128]{2,1,0:T(8,128)(2,1)S(1)}, bf16[8,4096,128]{2,1,0:T(8,128)(2,1)}, u32[]{:S(2)}) copy-start(bf16[8,4096,128]{2,1,0:T(8,128)(2,1)} %param.12) | copy-start | bytes 25165828

commit v10 on v9

--- a/solution.py
+++ b/solution.py
@@ -228,7 +228,9 @@
             pltpu.SemaphoreType.DMA((4, max(req_n, head_n))),
             pltpu.SemaphoreType.DMA(()),
         ],
-        compiler_params=pltpu.CompilerParams(collective_id=0, has_side_effects=True),
+        compiler_params=pltpu.CompilerParams(
+            collective_id=0, has_side_effects=True, vmem_limit_bytes=12 * 1024 * 1024
+        ),
     )(hidden_in, gain, w_qkv, cosine, sine)
 
 
@@ -278,7 +280,9 @@
             pltpu.SemaphoreType.DMA((4, max(req_n, head_n))),
             pltpu.SemaphoreType.DMA(()),
         ],
-        compiler_params=pltpu.CompilerParams(collective_id=1, has_side_effects=True),
+        compiler_params=pltpu.CompilerParams(
+            collective_id=1, has_side_effects=True, vmem_limit_bytes=12 * 1024 * 1024
+        ),
     )(attended, w_out, hidden_in)
 
 

time: 54.9 us -> 50.5 us (0.920)
  other arithmetic: 4.53 us -> 2.03 us
  Pallas kernels: 39.9 us -> 37.6 us
  local copies, waits for them, and re-layouts: 1.96 us -> 3.35 us
  matrix products: 8.01 us -> 7.15 us
    unnamed x4 -> x14, local copies, waits for them, and re-layouts: 1.96 us -> 3.35 us
    pallas_call x1, Pallas kernels: 23.4 us -> 22.3 us  [project(): pl.pallas_call(functools.partial(project_kernel, req_n, head_n), out_shap...]
    pallas_call x1, Pallas kernels: 16.4 us -> 15.4 us  [output_block(): pl.pallas_call(functools.partial(output_kernel, req_n, head_n), out_shape...]
    convert_element_type x1, other arithmetic: 0.99 us -> 0.01 us  [own_part(): new_values.astype(jnp.float32)[:, :, None, :]]
    transpose x1, other arithmetic: 0.91 us -> 0.01 us  [local(): queries = jnp.transpose(queries.astype(jnp.bfloat16), (1, 0, 2))[:, None]]
    dot_general x1, matrix products: 0.93 us -> 0.12 us  [attend_padded(): jnp.einsum('rkgd,rkd->rkg', queries, new_keys, preferred_element_type=jnp...]
    concatenate x1, other arithmetic: 0.68 us -> 0.08 us  [project(): cosine = jnp.concatenate([jnp.cos(angles), jnp.cos(angles)], axis=1)]
where the time goes in v10:
time: 50.5 us; the launch traced here: 50.3 us
  Pallas kernels  37.6 us (74%)
  matrix products  7.15 us (14%)
  local copies, waits for them, and re-layouts  3.35 us (7%)
  other arithmetic  2.03 us (4%)
    pallas_call x1, Pallas kernels, project(): pl.pallas_call(functools.partial(project_kernel, req_n, head_n), out_shap...  22.3 us
    pallas_call x1, Pallas kernels, output_block(): pl.pallas_call(functools.partial(output_kernel, req_n, head_n), out_shape...  15.4 us
    dot_general x1, matrix products, attend_padded(): jnp.einsum('rkgd,rpkd->rkgp', queries, cached_keys, preferred_element_typ...  5.73 us
    unnamed x14, local copies, waits for them, and re-layouts  3.35 us
    dot_general x1, matrix products, attend_padded(): jnp.einsum('rkgp,rpkd->rkgd', probs, cached_values, preferred_element_typ...  1.3 us

profile of v10, /device:TPU:1, one launch (start us, length us, event | category | flops | bytes accessed | tf_op | source)
XLA Modules:
  0.0 50.3 jit_solution(4466931679884626349)
XLA Ops:
  0.0 0.7 %convert_element_type.25 = f32[8]{0:T(128)S(1)} convert(s32[8]{0:T(128)} %param.13) | non-fusion elementwise | flops 8 | bytes 64 | tf_op jit(solution)/shard_map/convert_element_type | solution.py:207
  0.7 0.1 fusion.14
  0.8 0.1 pad_maximum_fusion
  0.9 0.0 copy-start
  0.9 1.3 %copy-done = bf16[512,1280]{1,0:T(8,128)(2,1)S(1)} copy-done((bf16[512,1280]{1,0:T(8,128)(2,1)S(1)}, bf16[512,1280]{1,0:T(8,128)(2,1)}, u32[]{:S(2)}) %copy-start) | copy-done | bytes 1310744
  2.2 0.0 copy-start.2
  2.2 0.7 %copy-done.2 = bf16[16,512]{1,0:T(8,128)(2,1)S(1)} copy-done((bf16[16,512]{1,0:T(8,128)(2,1)S(1)}, bf16[16,512]{1,0:T(8,128)(2,1)}, u32[]{:S(2)}) %copy-start.2) | copy-done | bytes 16408
  2.9 0.0 copy-start.4
  2.9 0.7 %copy-done.4 = bf16[512]{0:T(512)(128)(2,1)S(1)} copy-done((bf16[512]{0:T(512)(128)(2,1)S(1)}, bf16[512]{0:T(512)(128)(2,1)}, u32[]{:S(2)}) %copy-start.4) | copy-done | bytes 1048
  3.6 0.0 copy-start.5
  3.6 22.3 %shard_map.73 = (f32[8,8,128]{2,1,0:T(8,128)S(1)}, bf16[8,128]{1,0:T(8,128)(2,1)S(1)}, bf16[8,128]{1,0:T(8,128)(2,1)S(1)}) custom-call(bf16[16,512]{1,0:T(8,128)(2,1)S(1)} %copy-done.2, bf16[512]{0:T(512)(128)(2,1)S(1)} %copy-done.4, bf16[512,1280]{1,0:T(8,128)(2,1)S(1)} %copy-done, f32[8,128]{1,0:T(8,128)S(1)} %get-tuple-element.18.cos_ref, ...), custom_call_target="tpu_custom_call" | custom-call | tf_op jit(solution)/shard_map/pallas_call | solution.py:210
  25.9 0.1 fusion.8
  26.0 0.7 %iota_compare_fusion = pred[8,4096]{1,0:T(8,128)(4,1)S(1)} fusion(s32[8]{0:T(128)} %param.13), kind=kLoop, calls=%fused_computation.12 | loop fusion | flops 32768 | bytes 32800 | tf_op jit(solution)/shard_map/lt | solution.py:44
  26.7 5.7 %fusion.16 = (f32[8,8]{1,0:T(8,128)S(1)}, f32[8,8,4096]{2,1,0:T(8,128)S(1)}) fusion(bf16[8,4096,128]{2,1,0:T(8,128)(2,1)} %param.11, bf16[8,8,128]{2,0,1:T(8,128)(2,1)S(1)} %convert_bitcast_fusion, pred[8,4096]{1,0:T(8,128)(4,1)S(1)} %iota_compare_fusion), kind=kOutput, calls=%fused_computation.32 | convolution fusion | flops 67895232 | bytes 9486592 | tf_op jit(solution)/shard_map/rkgd,rpkd->rkgp/dot_general | solution.py:46
  32.5 0.4 fusion.3
  32.9 0.0 copy-start.1
  32.9 0.0 copy-start.3
  32.9 0.0 copy-done.5
  33.0 1.3 %fusion.2 = bf16[1,8,8,128]{3,2,1,0:T(8,128)(2,1)S(1)} fusion(bf16[8,4096,128]{2,1,0:T(8,128)(2,1)S(1)} %copy-done.5, f32[8,8,4096]{2,1,0:T(8,128)S(1)} %get-tuple-element.17, f32[8,8]{1,0:T(8,128)S(1)} %get-tuple-element.12, f32[8,8]{1,0:T(8,128)S(1)} %multiply_maximum_fusion, pred[8,4096]{1,0:T(8,128)(4,1)S(1)} %iota_compare_fusion, ...), kind=kOutput, calls=%fused_computation.4 | convolution fusion | flops 68182016 | bytes 9491200 | tf_op jit(solution)/shard_map/rkgp,rpkd->rkgd/dot_general | solution.py:57
  34.3 0.0 copy-done.1
  34.3 0.0 copy-done.3
  34.3 15.4 %shard_map.74 = bf16[16,512]{1,0:T(8,128)(2,1)S(1)} custom-call(bf16[8,1024]{1,0:T(8,128)(2,1)S(1)} %bitcast.17, bf16[1024,512]{1,0:T(8,128)(2,1)S(1)} %copy-done.1, bf16[16,512]{1,0:T(8,128)(2,1)S(1)} %copy-done.3), custom_call_target="tpu_custom_call" | custom-call | tf_op jit(solution)/shard_map/pallas_call | solution.py:266
  49.7 0.6 %copy.23 = bf16[16,512]{1,0:T(8,128)(2,1)} copy(bf16[16,512]{1,0:T(8,128)(2,1)S(1)} %shard_map.74) | data formatting | bytes 32768
  (7 shorter events, 0.1 us)
Async XLA Ops:
  0.9 1.3 %copy-start = (bf16[512,1280]{1,0:T(8,128)(2,1)S(1)}, bf16[512,1280]{1,0:T(8,128)(2,1)}, u32[]{:S(2)}) copy-start(bf16[512,1280]{1,0:T(8,128)(2,1)} %w_hbm.2) | copy-start | bytes 3932164
  2.2 0.7 %copy-start.2 = (bf16[16,512]{1,0:T(8,128)(2,1)S(1)}, bf16[16,512]{1,0:T(8,128)(2,1)}, u32[]{:S(2)}) copy-start(bf16[16,512]{1,0:T(8,128)(2,1)} %s_ref.1) | copy-start | bytes 49156
  2.9 0.7 %copy-start.4 = (bf16[512]{0:T(512)(128)(2,1)S(1)}, bf16[512]{0:T(512)(128)(2,1)}, u32[]{:S(2)}) copy-start(bf16[512]{0:T(512)(128)(2,1)} %gain_ref.1) | copy-start | bytes 3076
  3.6 29.4 %copy-start.5 = (bf16[8,4096,128]{2,1,0:T(8,128)(2,1)S(1)}, bf16[8,4096,128]{2,1,0:T(8,128)(2,1)}, u32[]{:S(2)}) copy-start(bf16[8,4096,128]{2,1,0:T(8,128)(2,1)} %param.12) | copy-start | bytes 25165828
  32.9 1.4 %copy-start.1 = (bf16[1024,512]{1,0:T(8,128)(2,1)S(1)}, bf16[1024,512]{1,0:T(8,128)(2,1)}, u32[]{:S(2)}) copy-start(bf16[1024,512]{1,0:T(8,128)(2,1)} %w_hbm.3) | copy-start | bytes 3145732
  32.9 1.4 %copy-start.3 = (bf16[16,512]{1,0:T(8,128)(2,1)S(1)}, bf16[16,512]{1,0:T(8,128)(2,1)}, u32[]{:S(2)}) copy-start(bf16[16,512]{1,0:T(8,128)(2,1)} %s_ref.1) | copy-start | bytes 49156

commit v11 on v10

--- a/solution.py
+++ b/solution.py
@@ -103,8 +103,9 @@
         copy.wait_send()
 
 
-def project_kernel(req_n, head_n, x_ref, gain_ref, w_hbm, cos_ref, sin_ref, q_ref, k_ref, v_ref,
-                   w_ref, rows_buf, part, pair_buf, mixed, sums_buf, sems, w_sem):
+def project_kernel(req_n, head_n, x_ref, gain_ref, w_hbm, cos_ref, sin_ref, keys_hbm, values_hbm,
+                   q_ref, k_ref, v_ref, keys_ref, values_ref,
+                   w_ref, rows_buf, part, pair_buf, mixed, sums_buf, sems, w_sem, key_sem):
     me_head = lax.axis_index("head")
     me_req = lax.axis_index("req")
     chips = req_n // 2
@@ -113,6 +114,10 @@
     partner = me_req + 1 - 2 * me_core
     w_copy = pltpu.make_async_copy(w_hbm, w_ref, w_sem)
     w_copy.start()
+    key_copy = pltpu.make_async_copy(keys_hbm, keys_ref, key_sem.at[0])
+    key_copy.start()
+    value_copy = pltpu.make_async_copy(values_hbm, values_ref, key_sem.at[1])
+    value_copy.start()
     barrier = pltpu.get_barrier_semaphore()
     for k in range(1, head_n):
         pl.semaphore_signal(
@@ -195,9 +200,11 @@
         q_ref[g] = rotated(projected[:, g * HD:(g + 1) * HD]).astype(jnp.bfloat16).astype(jnp.float32)
     k_ref[...] = rotated(projected[:, GROUP * HD:(GROUP + 1) * HD]).astype(k_ref.dtype)
     v_ref[...] = projected[:, (GROUP + 1) * HD:].astype(v_ref.dtype)
-
-
-def project(hidden_in, gain, w_qkv, lengths, req_n, head_n, count):
+    key_copy.wait()
+    value_copy.wait()
+
+
+def project(hidden_in, gain, w_qkv, lengths, k_cache, v_cache, req_n, head_n, count):
     rows, width = hidden_in.shape
     columns = w_qkv.shape[1] + 128
     halfway = HD // 2
@@ -213,11 +220,14 @@
             jax.ShapeDtypeStruct((GROUP, count, HD), jnp.float32),
             jax.ShapeDtypeStruct((count, HD), jnp.bfloat16),
             jax.ShapeDtypeStruct((count, HD), jnp.bfloat16),
+            jax.ShapeDtypeStruct(k_cache.shape, k_cache.dtype),
+            jax.ShapeDtypeStruct(v_cache.shape, v_cache.dtype),
         ),
         in_specs=[pl.BlockSpec(memory_space=pltpu.VMEM)] * 2
         + [pl.BlockSpec(memory_space=pl.ANY)]
-        + [pl.BlockSpec(memory_space=pltpu.VMEM)] * 2,
-        out_specs=(pl.BlockSpec(memory_space=pltpu.VMEM),) * 3,
+        + [pl.BlockSpec(memory_space=pltpu.VMEM)] * 2
+        + [pl.BlockSpec(memory_space=pl.ANY)] * 2,
+        out_specs=(pl.BlockSpec(memory_space=pltpu.VMEM),) * 5,
         scratch_shapes=[
             pltpu.VMEM(w_qkv.shape, w_qkv.dtype),
             pltpu.VMEM((head_n, rows, width), hidden_in.dtype),
@@ -227,11 +237,12 @@
             pltpu.VMEM((req_n // 2, count, columns), jnp.float32),
             pltpu.SemaphoreType.DMA((4, max(req_n, head_n))),
             pltpu.SemaphoreType.DMA(()),
+            pltpu.SemaphoreType.DMA((2,)),
         ],
         compiler_params=pltpu.CompilerParams(
-            collective_id=0, has_side_effects=True, vmem_limit_bytes=12 * 1024 * 1024
+            collective_id=0, has_side_effects=True, vmem_limit_bytes=30 * 1024 * 1024
         ),
-    )(hidden_in, gain, w_qkv, cosine, sine)
+    )(hidden_in, gain, w_qkv, cosine, sine, k_cache, v_cache)
 
 
 def output_kernel(req_n, head_n, a_ref, w_hbm, s_ref, o_ref, w_ref, att_buf, part, sums_buf,
@@ -288,8 +299,8 @@
 
 def local(req_n, head_n, hidden_in, attn_gain, w_qkv, w_out, k_cache, v_cache, lengths):
     own_count = k_cache.shape[0]
-    queries, new_keys, new_values = project(
-        hidden_in, attn_gain, w_qkv, lengths, req_n, head_n, own_count
+    queries, new_keys, new_values, k_cache, v_cache = project(
+        hidden_in, attn_gain, w_qkv, lengths, k_cache, v_cache, req_n, head_n, own_count
     )
     slots = k_cache.shape[1]
     local_heads = k_cache.shape[2] // HD

time: 50.5 us -> 47.2 us (0.935)
  matrix products: 7.15 us -> 3.83 us
    dot_general x1, matrix products: 5.73 us -> 2.35 us  [attend_padded(): jnp.einsum('rkgd,rpkd->rkgp', queries, cached_keys, preferred_element_typ...]
    unnamed x14 -> x12, local copies, waits for them, and re-layouts: 3.35 us -> 3.34 us
where the time goes in v11:
time: 47.2 us; the launch traced here: 47 us
  Pallas kernels  37.7 us (80%)
  matrix products  3.83 us (8%)
  local copies, waits for them, and re-layouts  3.34 us (7%)
  other arithmetic  2.03 us (4%)
    pallas_call x1, Pallas kernels, project(): pl.pallas_call(functools.partial(project_kernel, req_n, head_n), out_shap...  22.3 us
    pallas_call x1, Pallas kernels, output_block(): pl.pallas_call(functools.partial(output_kernel, req_n, head_n), out_shape...  15.4 us
    unnamed x12, local copies, waits for them, and re-layouts  3.34 us
    dot_general x1, matrix products, attend_padded(): jnp.einsum('rkgd,rpkd->rkgp', queries, cached_keys, preferred_element_typ...  2.35 us
    dot_general x1, matrix products, attend_padded(): jnp.einsum('rkgp,rpkd->rkgd', probs, cached_values, preferred_element_typ...  1.36 us

profile of v11, /device:TPU:1, one launch (start us, length us, event | category | flops | bytes accessed | tf_op | source)
XLA Modules:
  0.0 47.0 jit_solution(16323122599811851371)
XLA Ops:
  0.0 0.7 %convert_element_type.25 = f32[8]{0:T(128)S(1)} convert(s32[8]{0:T(128)} %param.13) | non-fusion elementwise | flops 8 | bytes 64 | tf_op jit(solution)/shard_map/convert_element_type | solution.py:214
  0.7 0.1 fusion.14
  0.8 0.1 pad_maximum_fusion
  0.9 0.8 %iota_compare_fusion = pred[8,4096]{1,0:T(8,128)(4,1)S(1)} fusion(s32[8]{0:T(128)} %param.13), kind=kLoop, calls=%fused_computation.12 | loop fusion | flops 32768 | bytes 32800 | tf_op jit(solution)/shard_map/lt | solution.py:44
  1.6 0.0 copy-start
  1.6 1.3 %copy-done = bf16[512,1280]{1,0:T(8,128)(2,1)S(1)} copy-done((bf16[512,1280]{1,0:T(8,128)(2,1)S(1)}, bf16[512,1280]{1,0:T(8,128)(2,1)}, u32[]{:S(2)}) %copy-start) | copy-done | bytes 1310744
  2.9 0.0 copy-start.2
  2.9 0.7 %copy-done.2 = bf16[16,512]{1,0:T(8,128)(2,1)S(1)} copy-done((bf16[16,512]{1,0:T(8,128)(2,1)S(1)}, bf16[16,512]{1,0:T(8,128)(2,1)}, u32[]{:S(2)}) %copy-start.2) | copy-done | bytes 16408
  3.7 0.0 copy-start.4
  3.7 0.7 %copy-done.4 = bf16[512]{0:T(512)(128)(2,1)S(1)} copy-done((bf16[512]{0:T(512)(128)(2,1)S(1)}, bf16[512]{0:T(512)(128)(2,1)}, u32[]{:S(2)}) %copy-start.4) | copy-done | bytes 1048
  4.3 22.3 %shard_map.73 = (f32[8,8,128]{2,1,0:T(8,128)S(1)}, bf16[8,128]{1,0:T(8,128)(2,1)S(1)}, bf16[8,128]{1,0:T(8,128)(2,1)S(1)}, bf16[8,4096,128]{2,1,0:T(8,128)(2,1)S(1)}, bf16[8,4096,128]{2,1,0:T(8,128)(2,1)S(1)}) custom-call(bf16[16,512]{1,0:T(8,128)(2,1)S(1)} %copy-done.2, bf16[512]{0:T(512)(128)(2,1)S(1)} %copy-done.4, bf16[512,1280]{1,0:T(8,128)(2,1)S(1)} %copy-done, ...), custom_call_target="tpu_custom_call" | custom-call | tf_op jit(solution)/shard_map/pallas_call | solution.py:217
  26.6 2.3 %fusion.16 = (f32[8,8]{1,0:T(8,128)S(1)}, f32[8,8,4096]{2,1,0:T(8,128)S(1)}) fusion(bf16[8,4096,128]{2,1,0:T(8,128)(2,1)S(1)} %get-tuple-element.11, bf16[8,8,128]{2,0,1:T(8,128)(2,1)S(1)} %convert_bitcast_fusion, pred[8,4096]{1,0:T(8,128)(4,1)S(1)} %iota_compare_fusion), kind=kOutput, calls=%fused_computation.32 | convolution fusion | flops 67895232 | bytes 9486592 | tf_op jit(solution)/shard_map/rkgd,rpkd->rkgp/dot_general | solution.py:46
  29.0 0.1 fusion.8
  29.1 0.4 fusion.3
  29.5 0.0 copy-start.1
  29.6 0.0 copy-start.3
  29.6 1.4 %fusion.2 = bf16[1,8,8,128]{3,2,1,0:T(8,128)(2,1)S(1)} fusion(bf16[8,4096,128]{2,1,0:T(8,128)(2,1)S(1)} %get-tuple-element.13, f32[8,8,4096]{2,1,0:T(8,128)S(1)} %get-tuple-element.21, f32[8,8]{1,0:T(8,128)S(1)} %get-tuple-element.16, f32[8,8]{1,0:T(8,128)S(1)} %multiply_maximum_fusion, pred[8,4096]{1,0:T(8,128)(4,1)S(1)} %iota_compare_fusion, ...), kind=kOutput, calls=%fused_computation.4 | convolution fusion | flops 68182016 | bytes 9491200 | tf_op jit(solution)/shard_map/rkgp,rpkd->rkgd/dot_general | solution.py:57
  31.0 0.0 copy-done.1
  31.0 0.0 copy-done.3
  31.0 15.4 %shard_map.74 = bf16[16,512]{1,0:T(8,128)(2,1)S(1)} custom-call(bf16[8,1024]{1,0:T(8,128)(2,1)S(1)} %bitcast.17, bf16[1024,512]{1,0:T(8,128)(2,1)S(1)} %copy-done.1, bf16[16,512]{1,0:T(8,128)(2,1)S(1)} %copy-done.3), custom_call_target="tpu_custom_call" | custom-call | tf_op jit(solution)/shard_map/pallas_call | solution.py:277
  46.4 0.6 %copy.23 = bf16[16,512]{1,0:T(8,128)(2,1)} copy(bf16[16,512]{1,0:T(8,128)(2,1)S(1)} %shard_map.74) | data formatting | bytes 32768
  (7 shorter events, 0.1 us)
Async XLA Ops:
  1.6 1.3 %copy-start = (bf16[512,1280]{1,0:T(8,128)(2,1)S(1)}, bf16[512,1280]{1,0:T(8,128)(2,1)}, u32[]{:S(2)}) copy-start(bf16[512,1280]{1,0:T(8,128)(2,1)} %w_hbm.2) | copy-start | bytes 3932164
  2.9 0.7 %copy-start.2 = (bf16[16,512]{1,0:T(8,128)(2,1)S(1)}, bf16[16,512]{1,0:T(8,128)(2,1)}, u32[]{:S(2)}) copy-start(bf16[16,512]{1,0:T(8,128)(2,1)} %s_ref.1) | copy-start | bytes 49156
  3.7 0.7 %copy-start.4 = (bf16[512]{0:T(512)(128)(2,1)S(1)}, bf16[512]{0:T(512)(128)(2,1)}, u32[]{:S(2)}) copy-start(bf16[512]{0:T(512)(128)(2,1)} %gain_ref.1) | copy-start | bytes 3076
  29.5 1.4 %copy-start.1 = (bf16[1024,512]{1,0:T(8,128)(2,1)S(1)}, bf16[1024,512]{1,0:T(8,128)(2,1)}, u32[]{:S(2)}) copy-start(bf16[1024,512]{1,0:T(8,128)(2,1)} %w_hbm.3) | copy-start | bytes 3145732
  29.6 1.4 %copy-start.3 = (bf16[16,512]{1,0:T(8,128)(2,1)S(1)}, bf16[16,512]{1,0:T(8,128)(2,1)}, u32[]{:S(2)}) copy-start(bf16[16,512]{1,0:T(8,128)(2,1)} %s_ref.1) | copy-start | bytes 49156

commit v12 on v11

--- a/solution.py
+++ b/solution.py
@@ -103,17 +103,21 @@
         copy.wait_send()
 
 
-def project_kernel(req_n, head_n, x_ref, gain_ref, w_hbm, cos_ref, sin_ref, keys_hbm, values_hbm,
+def project_kernel(req_n, head_n, x_hbm, gain_hbm, w_hbm, cos_ref, sin_ref, keys_hbm, values_hbm,
                    q_ref, k_ref, v_ref, keys_ref, values_ref,
-                   w_ref, rows_buf, part, pair_buf, mixed, sums_buf, sems, w_sem, key_sem):
+                   w_ref, gain_ref, rows_buf, part, pair_buf, mixed, sums_buf, sems, w_sem, key_sem):
     me_head = lax.axis_index("head")
     me_req = lax.axis_index("req")
     chips = req_n // 2
     me_core = lax.rem(me_req, 2)
     me_chip = me_req // 2
     partner = me_req + 1 - 2 * me_core
-    w_copy = pltpu.make_async_copy(w_hbm, w_ref, w_sem)
+    w_copy = pltpu.make_async_copy(w_hbm, w_ref, w_sem.at[0])
     w_copy.start()
+    x_copy = pltpu.make_async_copy(x_hbm, rows_buf.at[me_head], w_sem.at[1])
+    x_copy.start()
+    gain_copy = pltpu.make_async_copy(gain_hbm, gain_ref, w_sem.at[2])
+    gain_copy.start()
     key_copy = pltpu.make_async_copy(keys_hbm, keys_ref, key_sem.at[0])
     key_copy.start()
     value_copy = pltpu.make_async_copy(values_hbm, values_ref, key_sem.at[1])
@@ -133,12 +137,13 @@
             device_id_type=pl.DeviceIdType.MESH,
         )
     pl.semaphore_wait(barrier, head_n - 1 + chips)
-    own = lambda peer: x_ref
+    own = lambda peer: x_hbm
     sends = send_all("head", me_head, head_n, own, rows_buf, sems.at[0], sems.at[1])
     receive_all("head", me_head, head_n, own, rows_buf, sems.at[0], sems.at[1], sends)
-    rows_buf[me_head] = x_ref[...]
-    block_rows = x_ref.shape[0]
-    states = rows_buf[...].reshape(head_n * block_rows, x_ref.shape[1]).astype(jnp.float32)
+    x_copy.wait()
+    gain_copy.wait()
+    block_rows = x_hbm.shape[0]
+    states = rows_buf[...].reshape(head_n * block_rows, x_hbm.shape[1]).astype(jnp.float32)
     scaled = (states * gain_ref[...].astype(jnp.float32)[None, :]).astype(jnp.bfloat16)
     columns = w_ref.shape[1]
     square = jnp.sum(states * states, axis=1, keepdims=True)
@@ -223,26 +228,31 @@
             jax.ShapeDtypeStruct(k_cache.shape, k_cache.dtype),
             jax.ShapeDtypeStruct(v_cache.shape, v_cache.dtype),
         ),
-        in_specs=[pl.BlockSpec(memory_space=pltpu.VMEM)] * 2
-        + [pl.BlockSpec(memory_space=pl.ANY)]
+        in_specs=[pl.BlockSpec(memory_space=pltpu.HBM)] * 3
         + [pl.BlockSpec(memory_space=pltpu.VMEM)] * 2
         + [pl.BlockSpec(memory_space=pl.ANY)] * 2,
         out_specs=(pl.BlockSpec(memory_space=pltpu.VMEM),) * 5,
         scratch_shapes=[
             pltpu.VMEM(w_qkv.shape, w_qkv.dtype),
+            pltpu.VMEM(gain.shape, gain.dtype),
             pltpu.VMEM((head_n, rows, width), hidden_in.dtype),
             pltpu.VMEM((2, req_n // 2, count, columns), jnp.float32),
             pltpu.VMEM((req_n // 2, count, columns), jnp.float32),
             pltpu.VMEM((req_n // 2, count, columns), jnp.float32),
             pltpu.VMEM((req_n // 2, count, columns), jnp.float32),
             pltpu.SemaphoreType.DMA((4, max(req_n, head_n))),
-            pltpu.SemaphoreType.DMA(()),
+            pltpu.SemaphoreType.DMA((3,)),
             pltpu.SemaphoreType.DMA((2,)),
         ],
         compiler_params=pltpu.CompilerParams(
             collective_id=0, has_side_effects=True, vmem_limit_bytes=30 * 1024 * 1024
         ),
-    )(hidden_in, gain, w_qkv, cosine, sine, k_cache, v_cache)
+    )(
+        pltpu.with_memory_space_constraint(hidden_in, pltpu.HBM),
+        pltpu.with_memory_space_constraint(gain, pltpu.HBM),
+        pltpu.with_memory_space_constraint(w_qkv, pltpu.HBM),
+        cosine, sine, k_cache, v_cache,
+    )
 
 
 def output_kernel(req_n, head_n, a_ref, w_hbm, s_ref, o_ref, w_ref, att_buf, part, sums_buf,

time: 47.2 us -> 44.8 us (0.949)
  local copies, waits for them, and re-layouts: 3.34 us -> 0.63 us
    unnamed x12 -> x6, local copies, waits for them, and re-layouts: 3.34 us -> 0.63 us
where the time goes in v12:
time: 44.8 us; the launch traced here: 44.7 us
  Pallas kernels  38.1 us (85%)
  matrix products  3.84 us (9%)
  other arithmetic  2.03 us (5%)
  local copies, waits for them, and re-layouts  0.63 us (1%)
    pallas_call x1, Pallas kernels, project(): pl.pallas_call(functools.partial(project_kernel, req_n, head_n), out_shap...  22.5 us
    pallas_call x1, Pallas kernels, output_block(): pl.pallas_call(functools.partial(output_kernel, req_n, head_n), out_shape...  15.6 us
    dot_general x1, matrix products, attend_padded(): jnp.einsum('rkgd,rpkd->rkgp', queries, cached_keys, preferred_element_typ...  2.35 us
    dot_general x1, matrix products, attend_padded(): jnp.einsum('rkgp,rpkd->rkgd', probs, cached_values, preferred_element_typ...  1.36 us

profile of v12, /device:TPU:1, one launch (start us, length us, event | category | flops | bytes accessed | tf_op | source)
XLA Modules:
  0.0 44.7 jit_solution(899692029199726300)
XLA Ops:
  0.0 0.7 %convert_element_type.25 = f32[8]{0:T(128)S(1)} convert(s32[8]{0:T(128)} %param.13) | non-fusion elementwise | flops 8 | bytes 64 | tf_op jit(solution)/shard_map/convert_element_type | solution.py:219
  0.7 0.1 fusion.14
  0.8 0.1 pad_maximum_fusion
  0.9 0.8 %iota_compare_fusion = pred[8,4096]{1,0:T(8,128)(4,1)S(1)} fusion(s32[8]{0:T(128)} %param.13), kind=kLoop, calls=%fused_computation.12 | loop fusion | flops 32768 | bytes 32800 | tf_op jit(solution)/shard_map/lt | solution.py:44
  1.6 22.5 %shard_map.73 = (f32[8,8,128]{2,1,0:T(8,128)S(1)}, bf16[8,128]{1,0:T(8,128)(2,1)S(1)}, bf16[8,128]{1,0:T(8,128)(2,1)S(1)}, bf16[8,4096,128]{2,1,0:T(8,128)(2,1)S(1)}, bf16[8,4096,128]{2,1,0:T(8,128)(2,1)S(1)}) custom-call(bf16[16,512]{1,0:T(8,128)(2,1)} %s_ref.1, bf16[512]{0:T(512)(128)(2,1)} %gain_hbm.1, bf16[512,1280]{1,0:T(8,128)(2,1)} %w_hbm.2, ...), custom_call_target="tpu_custom_call" | custom-call | tf_op jit(solution)/shard_map/pallas_call | solution.py:222
  24.2 2.4 %fusion.16 = (f32[8,8]{1,0:T(8,128)S(1)}, f32[8,8,4096]{2,1,0:T(8,128)S(1)}) fusion(bf16[8,4096,128]{2,1,0:T(8,128)(2,1)S(1)} %get-tuple-element.11, bf16[8,8,128]{2,0,1:T(8,128)(2,1)S(1)} %convert_bitcast_fusion, pred[8,4096]{1,0:T(8,128)(4,1)S(1)} %iota_compare_fusion), kind=kOutput, calls=%fused_computation.32 | convolution fusion | flops 67895232 | bytes 9486592 | tf_op jit(solution)/shard_map/rkgd,rpkd->rkgp/dot_general | solution.py:46
  26.5 0.1 fusion.8
  26.6 0.4 fusion.3
  27.1 0.0 copy-start
  27.1 0.0 copy-start.1
  27.1 1.4 %fusion.2 = bf16[1,8,8,128]{3,2,1,0:T(8,128)(2,1)S(1)} fusion(bf16[8,4096,128]{2,1,0:T(8,128)(2,1)S(1)} %get-tuple-element.13, f32[8,8,4096]{2,1,0:T(8,128)S(1)} %get-tuple-element.21, f32[8,8]{1,0:T(8,128)S(1)} %get-tuple-element.16, f32[8,8]{1,0:T(8,128)S(1)} %multiply_maximum_fusion, pred[8,4096]{1,0:T(8,128)(4,1)S(1)} %iota_compare_fusion, ...), kind=kOutput, calls=%fused_computation.4 | convolution fusion | flops 68182016 | bytes 9491200 | tf_op jit(solution)/shard_map/rkgp,rpkd->rkgd/dot_general | solution.py:57
  28.5 0.0 copy-done
  28.5 0.0 copy-done.1
  28.5 15.6 %shard_map.74 = bf16[16,512]{1,0:T(8,128)(2,1)S(1)} custom-call(bf16[8,1024]{1,0:T(8,128)(2,1)S(1)} %bitcast.17, bf16[1024,512]{1,0:T(8,128)(2,1)S(1)} %copy-done, bf16[16,512]{1,0:T(8,128)(2,1)S(1)} %copy-done.1), custom_call_target="tpu_custom_call" | custom-call | tf_op jit(solution)/shard_map/pallas_call | solution.py:287
  44.1 0.6 %copy.23 = bf16[16,512]{1,0:T(8,128)(2,1)} copy(bf16[16,512]{1,0:T(8,128)(2,1)S(1)} %shard_map.74) | data formatting | bytes 32768
  (7 shorter events, 0.1 us)
Async XLA Ops:
  27.1 1.4 %copy-start = (bf16[1024,512]{1,0:T(8,128)(2,1)S(1)}, bf16[1024,512]{1,0:T(8,128)(2,1)}, u32[]{:S(2)}) copy-start(bf16[1024,512]{1,0:T(8,128)(2,1)} %w_hbm.3) | copy-start | bytes 3145732
  27.1 1.4 %copy-start.1 = (bf16[16,512]{1,0:T(8,128)(2,1)S(1)}, bf16[16,512]{1,0:T(8,128)(2,1)}, u32[]{:S(2)}) copy-start(bf16[16,512]{1,0:T(8,128)(2,1)} %s_ref.1) | copy-start | bytes 49156

commit v13 on v12

--- a/solution.py
+++ b/solution.py
@@ -39,9 +39,7 @@
     return own_prob.astype(jnp.float32)[..., None] * new_values.astype(jnp.float32)[:, :, None, :]
 
 
-def attend_padded(queries, new_keys, new_values, cached_keys, cached_values, lengths, factor):
-    slots = cached_keys.shape[1]
-    inside = jnp.arange(slots, dtype=jnp.int32)[None, :] < lengths[:, None]
+def attend_padded(queries, new_keys, new_values, cached_keys, cached_values, inside, factor):
     scores = (
         jnp.einsum("rkgd,rpkd->rkgp", queries, cached_keys, preferred_element_type=jnp.float32)
         * factor
@@ -103,8 +101,8 @@
         copy.wait_send()
 
 
-def project_kernel(req_n, head_n, x_hbm, gain_hbm, w_hbm, cos_ref, sin_ref, keys_hbm, values_hbm,
-                   q_ref, k_ref, v_ref, keys_ref, values_ref,
+def project_kernel(req_n, head_n, x_hbm, gain_hbm, w_hbm, cos_ref, sin_ref, len_ref, keys_hbm,
+                   values_hbm, q_ref, k_ref, v_ref, inside_ref, keys_ref, values_ref,
                    w_ref, gain_ref, rows_buf, part, pair_buf, mixed, sums_buf, sems, w_sem, key_sem):
     me_head = lax.axis_index("head")
     me_req = lax.axis_index("req")
@@ -205,6 +203,9 @@
         q_ref[g] = rotated(projected[:, g * HD:(g + 1) * HD]).astype(jnp.bfloat16).astype(jnp.float32)
     k_ref[...] = rotated(projected[:, GROUP * HD:(GROUP + 1) * HD]).astype(k_ref.dtype)
     v_ref[...] = projected[:, (GROUP + 1) * HD:].astype(v_ref.dtype)
+    slot = lax.broadcasted_iota(jnp.int32, (1, inside_ref.shape[1]), 1)
+    for b in range(inside_ref.shape[0]):
+        inside_ref[pl.ds(b, 1), :] = (slot < len_ref[b]).astype(inside_ref.dtype)
     key_copy.wait()
     value_copy.wait()
 
@@ -225,13 +226,15 @@
             jax.ShapeDtypeStruct((GROUP, count, HD), jnp.float32),
             jax.ShapeDtypeStruct((count, HD), jnp.bfloat16),
             jax.ShapeDtypeStruct((count, HD), jnp.bfloat16),
+            jax.ShapeDtypeStruct((count, k_cache.shape[1]), jnp.int32),
             jax.ShapeDtypeStruct(k_cache.shape, k_cache.dtype),
             jax.ShapeDtypeStruct(v_cache.shape, v_cache.dtype),
         ),
         in_specs=[pl.BlockSpec(memory_space=pltpu.HBM)] * 3
         + [pl.BlockSpec(memory_space=pltpu.VMEM)] * 2
+        + [pl.BlockSpec(memory_space=pltpu.SMEM)]
         + [pl.BlockSpec(memory_space=pl.ANY)] * 2,
-        out_specs=(pl.BlockSpec(memory_space=pltpu.VMEM),) * 5,
+        out_specs=(pl.BlockSpec(memory_space=pltpu.VMEM),) * 6,
         scratch_shapes=[
             pltpu.VMEM(w_qkv.shape, w_qkv.dtype),
             pltpu.VMEM(gain.shape, gain.dtype),
@@ -251,7 +254,7 @@
         pltpu.with_memory_space_constraint(hidden_in, pltpu.HBM),
         pltpu.with_memory_space_constraint(gain, pltpu.HBM),
         pltpu.with_memory_space_constraint(w_qkv, pltpu.HBM),
-        cosine, sine, k_cache, v_cache,
+        cosine, sine, pltpu.with_memory_space_constraint(lengths, pltpu.HBM), k_cache, v_cache,
     )
 
 
@@ -309,7 +312,7 @@
 
 def local(req_n, head_n, hidden_in, attn_gain, w_qkv, w_out, k_cache, v_cache, lengths):
     own_count = k_cache.shape[0]
-    queries, new_keys, new_values, k_cache, v_cache = project(
+    queries, new_keys, new_values, inside, k_cache, v_cache = project(
         hidden_in, attn_gain, w_qkv, lengths, k_cache, v_cache, req_n, head_n, own_count
     )
     slots = k_cache.shape[1]
@@ -321,7 +324,7 @@
     cached_values = v_cache.reshape(own_count, slots, local_heads, HD)
     factor = HD ** (-0.5)
     attended = attend_padded(
-        queries, new_keys, new_values, cached_keys, cached_values, lengths, factor
+        queries, new_keys, new_values, cached_keys, cached_values, inside != 0, factor
     )
     flat_rows = attended.reshape(own_count, local_heads * GROUP * HD)
     return output_block(flat_rows, w_out, hidden_in, req_n, head_n)

time: 44.8 us -> 44.9 us (level)
  Pallas kernels: 38.1 us -> 38.9 us
  other arithmetic: 2.03 us -> 1.31 us
    pallas_call x1, Pallas kernels: 22.5 us -> 23.3 us  [project(): pl.pallas_call(functools.partial(project_kernel, req_n, head_n), out_shap...]
    lt x1 -> x0, other arithmetic: 0.75 us -> none  [attend_padded(): inside = jnp.arange(slots, dtype=jnp.int32)[None, :] < lengths[:, None]]
where the time goes in v13:
time: 44.9 us; the launch traced here: 44.7 us
  Pallas kernels  38.9 us (87%)
  matrix products  3.84 us (9%)
  other arithmetic  1.31 us (3%)
  local copies, waits for them, and re-layouts  0.63 us (1%)
    pallas_call x1, Pallas kernels, project(): pl.pallas_call(functools.partial(project_kernel, req_n, head_n), out_shap...  23.3 us
    pallas_call x1, Pallas kernels, output_block(): pl.pallas_call(functools.partial(output_kernel, req_n, head_n), out_shape...  15.6 us
    dot_general x1, matrix products, attend_padded(): jnp.einsum('rkgd,rpkd->rkgp', queries, cached_keys, preferred_element_typ...  2.35 us
    dot_general x1, matrix products, attend_padded(): jnp.einsum('rkgp,rpkd->rkgd', probs, cached_values, preferred_element_typ...  1.36 us

profile of v13, /device:TPU:1, one launch (start us, length us, event | category | flops | bytes accessed | tf_op | source)
XLA Modules:
  0.0 44.7 jit_solution(4869547679400930542)
XLA Ops:
  0.0 0.7 %convert_element_type.25 = f32[8]{0:T(128)S(1)} convert(s32[8]{0:T(128)} %len_ref.1) | non-fusion elementwise | flops 8 | bytes 64 | tf_op jit(solution)/shard_map/convert_element_type | solution.py:220
  0.7 0.1 fusion.14
  0.8 0.1 pad_maximum_fusion
  0.9 23.3 %shard_map.73 = (f32[8,8,128]{2,1,0:T(8,128)S(1)}, bf16[8,128]{1,0:T(8,128)(2,1)S(1)}, bf16[8,128]{1,0:T(8,128)(2,1)S(1)}, s32[8,4096]{1,0:T(8,128)S(1)}, bf16[8...) custom-call(bf16[16,512]{1,0:T(8,128)(2,1)} %s_ref.1, bf16[512]{0:T(512)(128)(2,1)} %gain_hbm.1, ...), custom_call_target="tpu_custom_call" | custom-call | tf_op jit(solution)/shard_map/pallas_call | solution.py:223
  24.2 2.4 %fusion.16 = (f32[8,8]{1,0:T(8,128)S(1)}, f32[8,8,4096]{2,1,0:T(8,128)S(1)}) fusion(bf16[8,4096,128]{2,1,0:T(8,128)(2,1)S(1)} %get-tuple-element.13, bf16[8,8,128]{2,0,1:T(8,128)(2,1)S(1)} %convert_bitcast_fusion, pred[8,4096]{1,0:T(8,128)(4,1)S(1)} %broadcast_compare_fusion), kind=kOutput, calls=%fused_computation.32 | convolution fusion | flops 67895232 | bytes 9486592 | tf_op jit(solution)/shard_map/rkgd,rpkd->rkgp/dot_general | solution.py:44
  26.6 0.1 fusion.8
  26.7 0.4 fusion.3
  27.1 0.0 copy-start
  27.2 0.0 copy-start.1
  27.2 1.4 %fusion.2 = bf16[1,8,8,128]{3,2,1,0:T(8,128)(2,1)S(1)} fusion(bf16[8,4096,128]{2,1,0:T(8,128)(2,1)S(1)} %get-tuple-element.15, f32[8,8,4096]{2,1,0:T(8,128)S(1)} %get-tuple-element.23, f32[8,8]{1,0:T(8,128)S(1)} %get-tuple-element.18, f32[8,8]{1,0:T(8,128)S(1)} %multiply_maximum_fusion, pred[8,4096]{1,0:T(8,128)(4,1)S(1)} %broadcast_compare_fusion, ...), kind=kOutput, calls=%fused_computation.4 | convolution fusion | flops 68182016 | bytes 9491200 | tf_op jit(solution)/shard_map/rkgp,rpkd->rkgd/dot_general | solution.py:55
  28.6 0.0 copy-done
  28.6 0.0 copy-done.1
  28.6 15.6 %shard_map.74 = bf16[16,512]{1,0:T(8,128)(2,1)S(1)} custom-call(bf16[8,1024]{1,0:T(8,128)(2,1)S(1)} %bitcast.17, bf16[1024,512]{1,0:T(8,128)(2,1)S(1)} %copy-done, bf16[16,512]{1,0:T(8,128)(2,1)S(1)} %copy-done.1), custom_call_target="tpu_custom_call" | custom-call | tf_op jit(solution)/shard_map/pallas_call | solution.py:290
  44.1 0.6 %copy.23 = bf16[16,512]{1,0:T(8,128)(2,1)} copy(bf16[16,512]{1,0:T(8,128)(2,1)S(1)} %shard_map.74) | data formatting | bytes 32768
  (8 shorter events, 0.1 us)
Async XLA Ops:
  27.1 1.4 %copy-start = (bf16[1024,512]{1,0:T(8,128)(2,1)S(1)}, bf16[1024,512]{1,0:T(8,128)(2,1)}, u32[]{:S(2)}) copy-start(bf16[1024,512]{1,0:T(8,128)(2,1)} %w_hbm.3) | copy-start | bytes 3145732
  27.2 1.4 %copy-start.1 = (bf16[16,512]{1,0:T(8,128)(2,1)S(1)}, bf16[16,512]{1,0:T(8,128)(2,1)}, u32[]{:S(2)}) copy-start(bf16[16,512]{1,0:T(8,128)(2,1)} %s_ref.1) | copy-start | bytes 49156

commit v14 on v13

--- a/solution.py
+++ b/solution.py
@@ -135,10 +135,10 @@
             device_id_type=pl.DeviceIdType.MESH,
         )
     pl.semaphore_wait(barrier, head_n - 1 + chips)
-    own = lambda peer: x_hbm
+    x_copy.wait()
+    own = lambda peer: rows_buf.at[me_head]
     sends = send_all("head", me_head, head_n, own, rows_buf, sems.at[0], sems.at[1])
     receive_all("head", me_head, head_n, own, rows_buf, sems.at[0], sems.at[1], sends)
-    x_copy.wait()
     gain_copy.wait()
     block_rows = x_hbm.shape[0]
     states = rows_buf[...].reshape(head_n * block_rows, x_hbm.shape[1]).astype(jnp.float32)

time: 44.9 us -> 47.5 us (1.058)
  Pallas kernels: 38.9 us -> 41.5 us
    pallas_call x1, Pallas kernels: 23.3 us -> 25.4 us  [project(): pl.pallas_call(functools.partial(project_kernel, req_n, head_n), out_shap...]
    pallas_call x1, Pallas kernels: 15.6 us -> 16 us  [output_block(): pl.pallas_call(functools.partial(output_kernel, req_n, head_n), out_shape...]
where the time goes in v14:
time: 47.5 us; the launch traced here: 47.3 us
  Pallas kernels  41.5 us (87%)
  matrix products  3.84 us (8%)
  other arithmetic  1.31 us (3%)
  local copies, waits for them, and re-layouts  0.63 us (1%)
    pallas_call x1, Pallas kernels, project(): pl.pallas_call(functools.partial(project_kernel, req_n, head_n), out_shap...  25.4 us
    pallas_call x1, Pallas kernels, output_block(): pl.pallas_call(functools.partial(output_kernel, req_n, head_n), out_shape...  16 us
    dot_general x1, matrix products, attend_padded(): jnp.einsum('rkgd,rpkd->rkgp', queries, cached_keys, preferred_element_typ...  2.35 us
    dot_general x1, matrix products, attend_padded(): jnp.einsum('rkgp,rpkd->rkgd', probs, cached_values, preferred_element_typ...  1.36 us

profile of v14, /device:TPU:1, one launch (start us, length us, event | category | flops | bytes accessed | tf_op | source)
XLA Modules:
  0.0 47.3 jit_solution(4116724575305928638)
XLA Ops:
  0.0 0.7 %convert_element_type.25 = f32[8]{0:T(128)S(1)} convert(s32[8]{0:T(128)} %len_ref.1) | non-fusion elementwise | flops 8 | bytes 64 | tf_op jit(solution)/shard_map/convert_element_type | solution.py:220
  0.7 0.1 fusion.14
  0.8 0.1 pad_maximum_fusion
  0.9 25.4 %shard_map.73 = (f32[8,8,128]{2,1,0:T(8,128)S(1)}, bf16[8,128]{1,0:T(8,128)(2,1)S(1)}, bf16[8,128]{1,0:T(8,128)(2,1)S(1)}, s32[8,4096]{1,0:T(8,128)S(1)}, bf16[8...) custom-call(bf16[16,512]{1,0:T(8,128)(2,1)} %s_ref.1, bf16[512]{0:T(512)(128)(2,1)} %gain_hbm.1, ...), custom_call_target="tpu_custom_call" | custom-call | tf_op jit(solution)/shard_map/pallas_call | solution.py:223
  26.3 2.4 %fusion.16 = (f32[8,8]{1,0:T(8,128)S(1)}, f32[8,8,4096]{2,1,0:T(8,128)S(1)}) fusion(bf16[8,4096,128]{2,1,0:T(8,128)(2,1)S(1)} %get-tuple-element.13, bf16[8,8,128]{2,0,1:T(8,128)(2,1)S(1)} %convert_bitcast_fusion, pred[8,4096]{1,0:T(8,128)(4,1)S(1)} %broadcast_compare_fusion), kind=kOutput, calls=%fused_computation.32 | convolution fusion | flops 67895232 | bytes 9486592 | tf_op jit(solution)/shard_map/rkgd,rpkd->rkgp/dot_general | solution.py:44
  28.7 0.1 fusion.8
  28.8 0.4 fusion.3
  29.2 0.0 copy-start
  29.2 0.0 copy-start.1
  29.3 1.4 %fusion.2 = bf16[1,8,8,128]{3,2,1,0:T(8,128)(2,1)S(1)} fusion(bf16[8,4096,128]{2,1,0:T(8,128)(2,1)S(1)} %get-tuple-element.15, f32[8,8,4096]{2,1,0:T(8,128)S(1)} %get-tuple-element.23, f32[8,8]{1,0:T(8,128)S(1)} %get-tuple-element.18, f32[8,8]{1,0:T(8,128)S(1)} %multiply_maximum_fusion, pred[8,4096]{1,0:T(8,128)(4,1)S(1)} %broadcast_compare_fusion, ...), kind=kOutput, calls=%fused_computation.4 | convolution fusion | flops 68182016 | bytes 9491200 | tf_op jit(solution)/shard_map/rkgp,rpkd->rkgd/dot_general | solution.py:55
  30.6 0.0 copy-done
  30.7 0.0 copy-done.1
  30.7 16.0 %shard_map.74 = bf16[16,512]{1,0:T(8,128)(2,1)S(1)} custom-call(bf16[8,1024]{1,0:T(8,128)(2,1)S(1)} %bitcast.17, bf16[1024,512]{1,0:T(8,128)(2,1)S(1)} %copy-done, bf16[16,512]{1,0:T(8,128)(2,1)S(1)} %copy-done.1), custom_call_target="tpu_custom_call" | custom-call | tf_op jit(solution)/shard_map/pallas_call | solution.py:290
  46.7 0.6 %copy.23 = bf16[16,512]{1,0:T(8,128)(2,1)} copy(bf16[16,512]{1,0:T(8,128)(2,1)S(1)} %shard_map.74) | data formatting | bytes 32768
  (8 shorter events, 0.1 us)
Async XLA Ops:
  29.2 1.4 %copy-start = (bf16[1024,512]{1,0:T(8,128)(2,1)S(1)}, bf16[1024,512]{1,0:T(8,128)(2,1)}, u32[]{:S(2)}) copy-start(bf16[1024,512]{1,0:T(8,128)(2,1)} %w_hbm.3) | copy-start | bytes 3145732
  29.2 1.4 %copy-start.1 = (bf16[16,512]{1,0:T(8,128)(2,1)S(1)}, bf16[16,512]{1,0:T(8,128)(2,1)}, u32[]{:S(2)}) copy-start(bf16[16,512]{1,0:T(8,128)(2,1)} %s_ref.1) | copy-start | bytes 49156

commit v15 on v13

--- a/solution.py
+++ b/solution.py
@@ -166,9 +166,15 @@
     pair.start()
     pair.wait()
     mixed[...] = part[me_core] + pair_buf[...]
+    z_n = chips // 2
+    me_z, me_x = me_chip // 2, lax.rem(me_chip, 2)
+    offsets = sorted(
+        [(dz, dx) for dz in range(z_n) for dx in range(2) if dz or dx],
+        key=lambda o: -(min(o[0], z_n - o[0]) + 2 * o[1]),
+    )
     sends = []
-    for k in range(1, chips):
-        chip = lax.rem(me_chip + k, chips)
+    for k, (dz, dx) in enumerate(offsets, start=1):
+        chip = lax.rem(me_z + dz, z_n) * 2 + lax.rem(me_x + dx, 2)
         copy = pltpu.make_async_remote_copy(
             src_ref=mixed.at[chip],
             dst_ref=sums_buf.at[me_chip],
@@ -179,8 +185,8 @@
         )
         copy.start()
         sends.append(copy)
-    for k in range(1, chips):
-        chip = lax.rem(me_chip + chips - k, chips)
+    for k, (dz, dx) in enumerate(offsets, start=1):
+        chip = lax.rem(me_z + z_n - dz, z_n) * 2 + lax.rem(me_x + 2 - dx, 2)
         arrival = pltpu.make_async_remote_copy(
             src_ref=mixed.at[chip],
             dst_ref=sums_buf.at[chip],

time: 44.9 us -> 44.6 us (level)
  no operation moved by 1% of the time
where the time goes in v15:
time: 44.6 us; the launch traced here: 44.5 us
  Pallas kernels  38.6 us (87%)
  matrix products  3.84 us (9%)
  other arithmetic  1.31 us (3%)
  local copies, waits for them, and re-layouts  0.63 us (1%)
    pallas_call x1, Pallas kernels, project(): pl.pallas_call(functools.partial(project_kernel, req_n, head_n), out_shap...  23.3 us
    pallas_call x1, Pallas kernels, output_block(): pl.pallas_call(functools.partial(output_kernel, req_n, head_n), out_shape...  15.3 us
    dot_general x1, matrix products, attend_padded(): jnp.einsum('rkgd,rpkd->rkgp', queries, cached_keys, preferred_element_typ...  2.35 us
    dot_general x1, matrix products, attend_padded(): jnp.einsum('rkgp,rpkd->rkgd', probs, cached_values, preferred_element_typ...  1.36 us

profile of v15, /device:TPU:1, one launch (start us, length us, event | category | flops | bytes accessed | tf_op | source)
XLA Modules:
  0.0 44.5 jit_solution(9807032749692685835)
XLA Ops:
  0.0 0.7 %convert_element_type.25 = f32[8]{0:T(128)S(1)} convert(s32[8]{0:T(128)} %len_ref.1) | non-fusion elementwise | flops 8 | bytes 64 | tf_op jit(solution)/shard_map/convert_element_type | solution.py:226
  0.7 0.1 fusion.14
  0.8 0.1 pad_maximum_fusion
  0.9 23.3 %shard_map.73 = (f32[8,8,128]{2,1,0:T(8,128)S(1)}, bf16[8,128]{1,0:T(8,128)(2,1)S(1)}, bf16[8,128]{1,0:T(8,128)(2,1)S(1)}, s32[8,4096]{1,0:T(8,128)S(1)}, bf16[8...) custom-call(bf16[16,512]{1,0:T(8,128)(2,1)} %s_ref.1, bf16[512]{0:T(512)(128)(2,1)} %gain_hbm.1, ...), custom_call_target="tpu_custom_call" | custom-call | tf_op jit(solution)/shard_map/pallas_call | solution.py:229
  24.2 2.4 %fusion.16 = (f32[8,8]{1,0:T(8,128)S(1)}, f32[8,8,4096]{2,1,0:T(8,128)S(1)}) fusion(bf16[8,4096,128]{2,1,0:T(8,128)(2,1)S(1)} %get-tuple-element.13, bf16[8,8,128]{2,0,1:T(8,128)(2,1)S(1)} %convert_bitcast_fusion, pred[8,4096]{1,0:T(8,128)(4,1)S(1)} %broadcast_compare_fusion), kind=kOutput, calls=%fused_computation.32 | convolution fusion | flops 67895232 | bytes 9486592 | tf_op jit(solution)/shard_map/rkgd,rpkd->rkgp/dot_general | solution.py:44
  26.6 0.1 fusion.8
  26.7 0.4 fusion.3
  27.2 0.0 copy-start
  27.2 0.0 copy-start.1
  27.2 1.4 %fusion.2 = bf16[1,8,8,128]{3,2,1,0:T(8,128)(2,1)S(1)} fusion(bf16[8,4096,128]{2,1,0:T(8,128)(2,1)S(1)} %get-tuple-element.15, f32[8,8,4096]{2,1,0:T(8,128)S(1)} %get-tuple-element.23, f32[8,8]{1,0:T(8,128)S(1)} %get-tuple-element.18, f32[8,8]{1,0:T(8,128)S(1)} %multiply_maximum_fusion, pred[8,4096]{1,0:T(8,128)(4,1)S(1)} %broadcast_compare_fusion, ...), kind=kOutput, calls=%fused_computation.4 | convolution fusion | flops 68182016 | bytes 9491200 | tf_op jit(solution)/shard_map/rkgp,rpkd->rkgd/dot_general | solution.py:55
  28.6 0.0 copy-done
  28.6 0.0 copy-done.1
  28.6 15.3 %shard_map.74 = bf16[16,512]{1,0:T(8,128)(2,1)S(1)} custom-call(bf16[8,1024]{1,0:T(8,128)(2,1)S(1)} %bitcast.17, bf16[1024,512]{1,0:T(8,128)(2,1)S(1)} %copy-done, bf16[16,512]{1,0:T(8,128)(2,1)S(1)} %copy-done.1), custom_call_target="tpu_custom_call" | custom-call | tf_op jit(solution)/shard_map/pallas_call | solution.py:296
  43.9 0.6 %copy.23 = bf16[16,512]{1,0:T(8,128)(2,1)} copy(bf16[16,512]{1,0:T(8,128)(2,1)S(1)} %shard_map.74) | data formatting | bytes 32768
  (8 shorter events, 0.1 us)
Async XLA Ops:
  27.2 1.4 %copy-start = (bf16[1024,512]{1,0:T(8,128)(2,1)S(1)}, bf16[1024,512]{1,0:T(8,128)(2,1)}, u32[]{:S(2)}) copy-start(bf16[1024,512]{1,0:T(8,128)(2,1)} %w_hbm.3) | copy-start | bytes 3145732
  27.2 1.4 %copy-start.1 = (bf16[16,512]{1,0:T(8,128)(2,1)S(1)}, bf16[16,512]{1,0:T(8,128)(2,1)}, u32[]{:S(2)}) copy-start(bf16[16,512]{1,0:T(8,128)(2,1)} %s_ref.1) | copy-start | bytes 49156

commit v16 on v15

--- a/solution.py
+++ b/solution.py
@@ -1,4 +1,5 @@
 import functools
+import itertools
 
 import jax
 import jax.numpy as jnp
@@ -68,10 +69,28 @@
     pl.semaphore_wait(barrier, sum(n - 1 for _, _, n in peers))
 
 
-def send_all(axis, me, n, block_of, dst, send_sems, recv_sems):
+def ordered_peers(me, digits):
+    sizes = [size for size, _ in digits]
+    mine, rest = [], me
+    for size in reversed(sizes):
+        mine.append(lax.rem(rest, size))
+        rest = rest // size
+    mine = mine[::-1]
+    offsets = [o for o in itertools.product(*[range(s) for s in sizes]) if any(o)]
+    offsets.sort(key=lambda o: -sum(w * min(d, s - d) for d, (s, w) in zip(o, digits)))
+
+    def compose(o, forward):
+        index = 0
+        for d, m, s in zip(o, mine, sizes):
+            index = index * s + lax.rem(m + (d if forward else s - d), s)
+        return index
+
+    return [(compose(o, True), compose(o, False)) for o in offsets]
+
+
+def send_all(axis, peers, block_of, dst, send_sems, recv_sems, me):
     sends = []
-    for k in range(1, n):
-        peer = lax.rem(me + k, n)
+    for k, (peer, _) in enumerate(peers, start=1):
         copy = pltpu.make_async_remote_copy(
             src_ref=block_of(peer),
             dst_ref=dst.at[me],
@@ -85,9 +104,8 @@
     return sends
 
 
-def receive_all(axis, me, n, block_of, dst, send_sems, recv_sems, sends):
-    for k in range(1, n):
-        source = lax.rem(me + n - k, n)
+def receive_all(axis, peers, block_of, dst, send_sems, recv_sems, sends):
+    for k, (_, source) in enumerate(peers, start=1):
         arrival = pltpu.make_async_remote_copy(
             src_ref=block_of(source),
             dst_ref=dst.at[source],
@@ -136,8 +154,9 @@
         )
     pl.semaphore_wait(barrier, head_n - 1 + chips)
     own = lambda peer: x_hbm
-    sends = send_all("head", me_head, head_n, own, rows_buf, sems.at[0], sems.at[1])
-    receive_all("head", me_head, head_n, own, rows_buf, sems.at[0], sems.at[1], sends)
+    head_peers = ordered_peers(me_head, ((head_n // 2, 1), (2, 1)))
+    sends = send_all("head", head_peers, own, rows_buf, sems.at[0], sems.at[1], me_head)
+    receive_all("head", head_peers, own, rows_buf, sems.at[0], sems.at[1], sends)
     x_copy.wait()
     gain_copy.wait()
     block_rows = x_hbm.shape[0]
@@ -272,8 +291,9 @@
     w_copy.start()
     greet((("req", me_req, req_n), ("head", me_head, head_n)))
     own = lambda peer: a_ref
-    sends = send_all("req", me_req, req_n, own, att_buf, sems.at[0], sems.at[1])
-    receive_all("req", me_req, req_n, own, att_buf, sems.at[0], sems.at[1], sends)
+    req_peers = ordered_peers(me_req, ((req_n // 4, 1), (2, 2), (2, 0.5)))
+    sends = send_all("req", req_peers, own, att_buf, sems.at[0], sems.at[1], me_req)
+    receive_all("req", req_peers, own, att_buf, sems.at[0], sems.at[1], sends)
     att_buf[me_req] = a_ref[...]
     every = jnp.concatenate(
         [att_buf[s].astype(jnp.float32) for s in range(req_n)], axis=0
@@ -282,8 +302,9 @@
     part[...] = jnp.dot(every, w_ref[...], preferred_element_type=jnp.float32)
     rows = o_ref.shape[0]
     chunk = lambda peer: part.at[pl.ds(pl.multiple_of(peer * rows, rows), rows)]
-    sends = send_all("head", me_head, head_n, chunk, sums_buf, sems.at[2], sems.at[3])
-    receive_all("head", me_head, head_n, chunk, sums_buf, sems.at[2], sems.at[3], sends)
+    head_peers = ordered_peers(me_head, ((head_n // 2, 1), (2, 1)))
+    sends = send_all("head", head_peers, chunk, sums_buf, sems.at[2], sems.at[3], me_head)
+    receive_all("head", head_peers, chunk, sums_buf, sems.at[2], sems.at[3], sends)
     total = part[pl.ds(pl.multiple_of(me_head * rows, rows), rows), :]
     for k in range(1, head_n):
         total = total + sums_buf[lax.rem(me_head + head_n - k, head_n)]

time: 44.6 us -> 43.3 us (0.971)
  Pallas kernels: 38.6 us -> 37 us
    pallas_call x1, Pallas kernels: 15.3 us -> 13.6 us  [output_block(): pl.pallas_call(functools.partial(output_kernel, req_n, head_n), out_shape...]
where the time goes in v16:
time: 43.3 us; the launch traced here: 42.8 us
  Pallas kernels  37 us (85%)
  matrix products  3.84 us (9%)
  other arithmetic  1.31 us (3%)
  local copies, waits for them, and re-layouts  0.63 us (1%)
    pallas_call x1, Pallas kernels, project(): pl.pallas_call(functools.partial(project_kernel, req_n, head_n), out_shap...  23.3 us
    pallas_call x1, Pallas kernels, output_block(): pl.pallas_call(functools.partial(output_kernel, req_n, head_n), out_shape...  13.6 us
    dot_general x1, matrix products, attend_padded(): jnp.einsum('rkgd,rpkd->rkgp', queries, cached_keys, preferred_element_typ...  2.35 us
    dot_general x1, matrix products, attend_padded(): jnp.einsum('rkgp,rpkd->rkgd', probs, cached_values, preferred_element_typ...  1.36 us

profile of v16, /device:TPU:1, one launch (start us, length us, event | category | flops | bytes accessed | tf_op | source)
XLA Modules:
  0.0 42.8 jit_solution(1145045874052780754)
XLA Ops:
  0.0 0.7 %convert_element_type.25 = f32[8]{0:T(128)S(1)} convert(s32[8]{0:T(128)} %len_ref.1) | non-fusion elementwise | flops 8 | bytes 64 | tf_op jit(solution)/shard_map/convert_element_type | solution.py:245
  0.7 0.1 fusion.14
  0.8 0.1 pad_maximum_fusion
  0.9 23.3 %shard_map.73 = (f32[8,8,128]{2,1,0:T(8,128)S(1)}, bf16[8,128]{1,0:T(8,128)(2,1)S(1)}, bf16[8,128]{1,0:T(8,128)(2,1)S(1)}, s32[8,4096]{1,0:T(8,128)S(1)}, bf16[8...) custom-call(bf16[16,512]{1,0:T(8,128)(2,1)} %s_ref.1, bf16[512]{0:T(512)(128)(2,1)} %gain_hbm.1, ...), custom_call_target="tpu_custom_call" | custom-call | tf_op jit(solution)/shard_map/pallas_call | solution.py:248
  24.2 2.4 %fusion.16 = (f32[8,8]{1,0:T(8,128)S(1)}, f32[8,8,4096]{2,1,0:T(8,128)S(1)}) fusion(bf16[8,4096,128]{2,1,0:T(8,128)(2,1)S(1)} %get-tuple-element.13, bf16[8,8,128]{2,0,1:T(8,128)(2,1)S(1)} %convert_bitcast_fusion, pred[8,4096]{1,0:T(8,128)(4,1)S(1)} %broadcast_compare_fusion), kind=kOutput, calls=%fused_computation.32 | convolution fusion | flops 67895232 | bytes 9486592 | tf_op jit(solution)/shard_map/rkgd,rpkd->rkgp/dot_general | solution.py:45
  26.6 0.1 fusion.8
  26.7 0.4 fusion.3
  27.1 0.0 copy-start
  27.2 0.0 copy-start.1
  27.2 1.4 %fusion.2 = bf16[1,8,8,128]{3,2,1,0:T(8,128)(2,1)S(1)} fusion(bf16[8,4096,128]{2,1,0:T(8,128)(2,1)S(1)} %get-tuple-element.15, f32[8,8,4096]{2,1,0:T(8,128)S(1)} %get-tuple-element.23, f32[8,8]{1,0:T(8,128)S(1)} %get-tuple-element.18, f32[8,8]{1,0:T(8,128)S(1)} %multiply_maximum_fusion, pred[8,4096]{1,0:T(8,128)(4,1)S(1)} %broadcast_compare_fusion, ...), kind=kOutput, calls=%fused_computation.4 | convolution fusion | flops 68182016 | bytes 9491200 | tf_op jit(solution)/shard_map/rkgp,rpkd->rkgd/dot_general | solution.py:56
  28.6 0.0 copy-done
  28.6 0.0 copy-done.1
  28.6 13.6 %shard_map.74 = bf16[16,512]{1,0:T(8,128)(2,1)S(1)} custom-call(bf16[8,1024]{1,0:T(8,128)(2,1)S(1)} %bitcast.17, bf16[1024,512]{1,0:T(8,128)(2,1)S(1)} %copy-done, bf16[16,512]{1,0:T(8,128)(2,1)S(1)} %copy-done.1), custom_call_target="tpu_custom_call" | custom-call | tf_op jit(solution)/shard_map/pallas_call | solution.py:317
  42.2 0.6 %copy.23 = bf16[16,512]{1,0:T(8,128)(2,1)} copy(bf16[16,512]{1,0:T(8,128)(2,1)S(1)} %shard_map.74) | data formatting | bytes 32768
  (8 shorter events, 0.1 us)
Async XLA Ops:
  27.1 1.4 %copy-start = (bf16[1024,512]{1,0:T(8,128)(2,1)S(1)}, bf16[1024,512]{1,0:T(8,128)(2,1)}, u32[]{:S(2)}) copy-start(bf16[1024,512]{1,0:T(8,128)(2,1)} %w_hbm.3) | copy-start | bytes 3145732
  27.2 1.4 %copy-start.1 = (bf16[16,512]{1,0:T(8,128)(2,1)S(1)}, bf16[16,512]{1,0:T(8,128)(2,1)}, u32[]{:S(2)}) copy-start(bf16[16,512]{1,0:T(8,128)(2,1)} %s_ref.1) | copy-start | bytes 49156

commit v17 on v16

--- a/solution.py
+++ b/solution.py
@@ -60,13 +60,12 @@
 
 def greet(peers):
     barrier = pltpu.get_barrier_semaphore()
-    for axis, me, n in peers:
-        for k in range(1, n):
+    for axis, ordered in peers:
+        for peer, _ in ordered:
             pl.semaphore_signal(
-                barrier, inc=1, device_id={axis: lax.rem(me + k, n)},
-                device_id_type=pl.DeviceIdType.MESH,
+                barrier, inc=1, device_id={axis: peer}, device_id_type=pl.DeviceIdType.MESH
             )
-    pl.semaphore_wait(barrier, sum(n - 1 for _, _, n in peers))
+    pl.semaphore_wait(barrier, sum(len(ordered) for _, ordered in peers))
 
 
 def ordered_peers(me, digits):
@@ -138,23 +137,13 @@
     key_copy.start()
     value_copy = pltpu.make_async_copy(values_hbm, values_ref, key_sem.at[1])
     value_copy.start()
-    barrier = pltpu.get_barrier_semaphore()
-    for k in range(1, head_n):
-        pl.semaphore_signal(
-            barrier, inc=1, device_id={"head": lax.rem(me_head + k, head_n)},
-            device_id_type=pl.DeviceIdType.MESH,
-        )
-    pl.semaphore_signal(
-        barrier, inc=1, device_id={"req": partner}, device_id_type=pl.DeviceIdType.MESH
-    )
-    for k in range(1, chips):
-        pl.semaphore_signal(
-            barrier, inc=1, device_id={"req": lax.rem(me_chip + k, chips) * 2 + me_core},
-            device_id_type=pl.DeviceIdType.MESH,
-        )
-    pl.semaphore_wait(barrier, head_n - 1 + chips)
+    chip_peers = [
+        (chip * 2 + me_core, None)
+        for chip, _ in ordered_peers(me_chip, ((chips // 2, 1), (2, 2)))
+    ]
+    head_peers = ordered_peers(me_head, ((head_n // 2, 1), (2, 1)))
+    greet((("req", chip_peers), ("head", head_peers), ("req", [(partner, None)])))
     own = lambda peer: x_hbm
-    head_peers = ordered_peers(me_head, ((head_n // 2, 1), (2, 1)))
     sends = send_all("head", head_peers, own, rows_buf, sems.at[0], sems.at[1], me_head)
     receive_all("head", head_peers, own, rows_buf, sems.at[0], sems.at[1], sends)
     x_copy.wait()
@@ -289,9 +278,10 @@
     me_req = lax.axis_index("req")
     w_copy = pltpu.make_async_copy(w_hbm, w_ref, w_sem)
     w_copy.start()
-    greet((("req", me_req, req_n), ("head", me_head, head_n)))
+    req_peers = ordered_peers(me_req, ((req_n // 4, 1), (2, 2), (2, 0.5)))
+    head_peers = ordered_peers(me_head, ((head_n // 2, 1), (2, 1)))
+    greet((("req", req_peers), ("head", head_peers)))
     own = lambda peer: a_ref
-    req_peers = ordered_peers(me_req, ((req_n // 4, 1), (2, 2), (2, 0.5)))
     sends = send_all("req", req_peers, own, att_buf, sems.at[0], sems.at[1], me_req)
     receive_all("req", req_peers, own, att_buf, sems.at[0], sems.at[1], sends)
     att_buf[me_req] = a_ref[...]

time: 43.3 us -> 43.3 us (level)
  no operation moved by 1% of the time
where the time goes in v17:
time: 43.3 us; the launch traced here: 42.9 us
  Pallas kernels  37.1 us (86%)
  matrix products  3.84 us (9%)
  other arithmetic  1.31 us (3%)
  local copies, waits for them, and re-layouts  0.63 us (1%)
    pallas_call x1, Pallas kernels, project(): pl.pallas_call(functools.partial(project_kernel, req_n, head_n), out_shap...  23.3 us
    pallas_call x1, Pallas kernels, output_block(): pl.pallas_call(functools.partial(output_kernel, req_n, head_n), out_shape...  13.8 us
    dot_general x1, matrix products, attend_padded(): jnp.einsum('rkgd,rpkd->rkgp', queries, cached_keys, preferred_element_typ...  2.35 us
    dot_general x1, matrix products, attend_padded(): jnp.einsum('rkgp,rpkd->rkgd', probs, cached_values, preferred_element_typ...  1.36 us

profile of v17, /device:TPU:1, one launch (start us, length us, event | category | flops | bytes accessed | tf_op | source)
XLA Modules:
  0.0 42.9 jit_solution(7121273031929618315)
XLA Ops:
  0.0 0.7 %convert_element_type.25 = f32[8]{0:T(128)S(1)} convert(s32[8]{0:T(128)} %len_ref.1) | non-fusion elementwise | flops 8 | bytes 64 | tf_op jit(solution)/shard_map/convert_element_type | solution.py:234
  0.7 0.1 fusion.14
  0.8 0.1 pad_maximum_fusion
  0.9 23.3 %shard_map.73 = (f32[8,8,128]{2,1,0:T(8,128)S(1)}, bf16[8,128]{1,0:T(8,128)(2,1)S(1)}, bf16[8,128]{1,0:T(8,128)(2,1)S(1)}, s32[8,4096]{1,0:T(8,128)S(1)}, bf16[8...) custom-call(bf16[16,512]{1,0:T(8,128)(2,1)} %s_ref.1, bf16[512]{0:T(512)(128)(2,1)} %gain_hbm.1, ...), custom_call_target="tpu_custom_call" | custom-call | tf_op jit(solution)/shard_map/pallas_call | solution.py:237
  24.2 2.4 %fusion.16 = (f32[8,8]{1,0:T(8,128)S(1)}, f32[8,8,4096]{2,1,0:T(8,128)S(1)}) fusion(bf16[8,4096,128]{2,1,0:T(8,128)(2,1)S(1)} %get-tuple-element.13, bf16[8,8,128]{2,0,1:T(8,128)(2,1)S(1)} %convert_bitcast_fusion, pred[8,4096]{1,0:T(8,128)(4,1)S(1)} %broadcast_compare_fusion), kind=kOutput, calls=%fused_computation.32 | convolution fusion | flops 67895232 | bytes 9486592 | tf_op jit(solution)/shard_map/rkgd,rpkd->rkgp/dot_general | solution.py:45
  26.5 0.1 fusion.8
  26.7 0.4 fusion.3
  27.1 0.0 copy-start
  27.1 0.0 copy-start.1
  27.1 1.4 %fusion.2 = bf16[1,8,8,128]{3,2,1,0:T(8,128)(2,1)S(1)} fusion(bf16[8,4096,128]{2,1,0:T(8,128)(2,1)S(1)} %get-tuple-element.15, f32[8,8,4096]{2,1,0:T(8,128)S(1)} %get-tuple-element.23, f32[8,8]{1,0:T(8,128)S(1)} %get-tuple-element.18, f32[8,8]{1,0:T(8,128)S(1)} %multiply_maximum_fusion, pred[8,4096]{1,0:T(8,128)(4,1)S(1)} %broadcast_compare_fusion, ...), kind=kOutput, calls=%fused_computation.4 | convolution fusion | flops 68182016 | bytes 9491200 | tf_op jit(solution)/shard_map/rkgp,rpkd->rkgd/dot_general | solution.py:56
  28.5 0.0 copy-done
  28.5 0.0 copy-done.1
  28.5 13.8 %shard_map.74 = bf16[16,512]{1,0:T(8,128)(2,1)S(1)} custom-call(bf16[8,1024]{1,0:T(8,128)(2,1)S(1)} %bitcast.17, bf16[1024,512]{1,0:T(8,128)(2,1)S(1)} %copy-done, bf16[16,512]{1,0:T(8,128)(2,1)S(1)} %copy-done.1), custom_call_target="tpu_custom_call" | custom-call | tf_op jit(solution)/shard_map/pallas_call | solution.py:307
  42.3 0.6 %copy.23 = bf16[16,512]{1,0:T(8,128)(2,1)} copy(bf16[16,512]{1,0:T(8,128)(2,1)S(1)} %shard_map.74) | data formatting | bytes 32768
  (8 shorter events, 0.1 us)
Async XLA Ops:
  27.1 1.4 %copy-start = (bf16[1024,512]{1,0:T(8,128)(2,1)S(1)}, bf16[1024,512]{1,0:T(8,128)(2,1)}, u32[]{:S(2)}) copy-start(bf16[1024,512]{1,0:T(8,128)(2,1)} %w_hbm.3) | copy-start | bytes 3145732
  27.1 1.4 %copy-start.1 = (bf16[16,512]{1,0:T(8,128)(2,1)S(1)}, bf16[16,512]{1,0:T(8,128)(2,1)}, u32[]{:S(2)}) copy-start(bf16[16,512]{1,0:T(8,128)(2,1)} %s_ref.1) | copy-start | bytes 49156

commit v18 on v17

--- a/solution.py
+++ b/solution.py
@@ -163,17 +163,21 @@
     packed = packed.reshape(chips, 2, count, part.shape[-1])
     part[0] = packed[:, 0]
     part[1] = packed[:, 1]
-    pair = pltpu.make_async_remote_copy(
-        src_ref=part.at[1 - me_core],
-        dst_ref=pair_buf,
-        send_sem=sems.at[2, 0],
-        recv_sem=sems.at[3, 0],
-        device_id={"req": partner},
-        device_id_type=pl.DeviceIdType.MESH,
-    )
-    pair.start()
-    pair.wait()
-    mixed[...] = part[me_core] + pair_buf[...]
+    width = part.shape[-1]
+    split = (width // 2 + 127) // 128 * 128
+    parts = ((0, split), (split, width - split))
+    pairs = []
+    for h, (lo, size) in enumerate(parts):
+        pair = pltpu.make_async_remote_copy(
+            src_ref=part.at[1 - me_core, :, :, pl.ds(lo, size)],
+            dst_ref=pair_buf.at[:, :, pl.ds(lo, size)],
+            send_sem=sems.at[2 * h, 0],
+            recv_sem=sems.at[2 * h + 1, 0],
+            device_id={"req": partner},
+            device_id_type=pl.DeviceIdType.MESH,
+        )
+        pair.start()
+        pairs.append(pair)
     z_n = chips // 2
     me_z, me_x = me_chip // 2, lax.rem(me_chip, 2)
     offsets = sorted(
@@ -181,29 +185,34 @@
         key=lambda o: -(min(o[0], z_n - o[0]) + 2 * o[1]),
     )
     sends = []
-    for k, (dz, dx) in enumerate(offsets, start=1):
-        chip = lax.rem(me_z + dz, z_n) * 2 + lax.rem(me_x + dx, 2)
-        copy = pltpu.make_async_remote_copy(
-            src_ref=mixed.at[chip],
-            dst_ref=sums_buf.at[me_chip],
-            send_sem=sems.at[2, k],
-            recv_sem=sems.at[3, k],
-            device_id={"req": chip * 2 + me_core},
-            device_id_type=pl.DeviceIdType.MESH,
-        )
-        copy.start()
-        sends.append(copy)
-    for k, (dz, dx) in enumerate(offsets, start=1):
-        chip = lax.rem(me_z + z_n - dz, z_n) * 2 + lax.rem(me_x + 2 - dx, 2)
-        arrival = pltpu.make_async_remote_copy(
-            src_ref=mixed.at[chip],
-            dst_ref=sums_buf.at[chip],
-            send_sem=sems.at[2, k],
-            recv_sem=sems.at[3, k],
-            device_id={"req": chip * 2 + me_core},
-            device_id_type=pl.DeviceIdType.MESH,
-        )
-        arrival.wait_recv()
+    for h, (lo, size) in enumerate(parts):
+        pairs[h].wait()
+        columns_h = pl.ds(lo, size)
+        mixed[:, :, columns_h] = part[me_core, :, :, columns_h] + pair_buf[:, :, columns_h]
+        for k, (dz, dx) in enumerate(offsets, start=1):
+            chip = lax.rem(me_z + dz, z_n) * 2 + lax.rem(me_x + dx, 2)
+            copy = pltpu.make_async_remote_copy(
+                src_ref=mixed.at[chip, :, columns_h],
+                dst_ref=sums_buf.at[me_chip, :, columns_h],
+                send_sem=sems.at[2, h * chips + k],
+                recv_sem=sems.at[3, h * chips + k],
+                device_id={"req": chip * 2 + me_core},
+                device_id_type=pl.DeviceIdType.MESH,
+            )
+            copy.start()
+            sends.append(copy)
+    for h, (lo, size) in enumerate(parts):
+        for k, (dz, dx) in enumerate(offsets, start=1):
+            chip = lax.rem(me_z + z_n - dz, z_n) * 2 + lax.rem(me_x + 2 - dx, 2)
+            arrival = pltpu.make_async_remote_copy(
+                src_ref=mixed.at[chip, :, pl.ds(lo, size)],
+                dst_ref=sums_buf.at[chip, :, pl.ds(lo, size)],
+                send_sem=sems.at[2, h * chips + k],
+                recv_sem=sems.at[3, h * chips + k],
+                device_id={"req": chip * 2 + me_core},
+                device_id_type=pl.DeviceIdType.MESH,
+            )
+            arrival.wait_recv()
     for copy in sends:
         copy.wait_send()
     total = mixed[me_chip]

time: 43.3 us -> 44.4 us (1.025)
  Pallas kernels: 37.1 us -> 38.5 us
    pallas_call x1, Pallas kernels: 13.8 us -> 15.4 us  [output_block(): pl.pallas_call(functools.partial(output_kernel, req_n, head_n), out_shape...]
where the time goes in v18:
time: 44.4 us; the launch traced here: 44.3 us
  Pallas kernels  38.5 us (87%)
  matrix products  3.84 us (9%)
  other arithmetic  1.31 us (3%)
  local copies, waits for them, and re-layouts  0.63 us (1%)
    pallas_call x1, Pallas kernels, project(): pl.pallas_call(functools.partial(project_kernel, req_n, head_n), out_shap...  23 us
    pallas_call x1, Pallas kernels, output_block(): pl.pallas_call(functools.partial(output_kernel, req_n, head_n), out_shape...  15.4 us
    dot_general x1, matrix products, attend_padded(): jnp.einsum('rkgd,rpkd->rkgp', queries, cached_keys, preferred_element_typ...  2.35 us
    dot_general x1, matrix products, attend_padded(): jnp.einsum('rkgp,rpkd->rkgd', probs, cached_values, preferred_element_typ...  1.36 us

profile of v18, /device:TPU:1, one launch (start us, length us, event | category | flops | bytes accessed | tf_op | source)
XLA Modules:
  0.0 44.3 jit_solution(12364606927808217376)
XLA Ops:
  0.0 0.7 %convert_element_type.25 = f32[8]{0:T(128)S(1)} convert(s32[8]{0:T(128)} %len_ref.1) | non-fusion elementwise | flops 8 | bytes 64 | tf_op jit(solution)/shard_map/convert_element_type | solution.py:243
  0.7 0.1 fusion.14
  0.8 0.1 pad_maximum_fusion
  0.9 23.0 %shard_map.73 = (f32[8,8,128]{2,1,0:T(8,128)S(1)}, bf16[8,128]{1,0:T(8,128)(2,1)S(1)}, bf16[8,128]{1,0:T(8,128)(2,1)S(1)}, s32[8,4096]{1,0:T(8,128)S(1)}, bf16[8...) custom-call(bf16[16,512]{1,0:T(8,128)(2,1)} %s_ref.1, bf16[512]{0:T(512)(128)(2,1)} %gain_hbm.1, ...), custom_call_target="tpu_custom_call" | custom-call | tf_op jit(solution)/shard_map/pallas_call | solution.py:246
  23.9 2.4 %fusion.16 = (f32[8,8]{1,0:T(8,128)S(1)}, f32[8,8,4096]{2,1,0:T(8,128)S(1)}) fusion(bf16[8,4096,128]{2,1,0:T(8,128)(2,1)S(1)} %get-tuple-element.13, bf16[8,8,128]{2,0,1:T(8,128)(2,1)S(1)} %convert_bitcast_fusion, pred[8,4096]{1,0:T(8,128)(4,1)S(1)} %broadcast_compare_fusion), kind=kOutput, calls=%fused_computation.32 | convolution fusion | flops 67895232 | bytes 9486592 | tf_op jit(solution)/shard_map/rkgd,rpkd->rkgp/dot_general | solution.py:45
  26.3 0.1 fusion.8
  26.4 0.4 fusion.3
  26.9 0.0 copy-start
  26.9 0.0 copy-start.1
  26.9 1.4 %fusion.2 = bf16[1,8,8,128]{3,2,1,0:T(8,128)(2,1)S(1)} fusion(bf16[8,4096,128]{2,1,0:T(8,128)(2,1)S(1)} %get-tuple-element.15, f32[8,8,4096]{2,1,0:T(8,128)S(1)} %get-tuple-element.23, f32[8,8]{1,0:T(8,128)S(1)} %get-tuple-element.18, f32[8,8]{1,0:T(8,128)S(1)} %multiply_maximum_fusion, pred[8,4096]{1,0:T(8,128)(4,1)S(1)} %broadcast_compare_fusion, ...), kind=kOutput, calls=%fused_computation.4 | convolution fusion | flops 68182016 | bytes 9491200 | tf_op jit(solution)/shard_map/rkgp,rpkd->rkgd/dot_general | solution.py:56
  28.3 0.0 copy-done
  28.3 0.0 copy-done.1
  28.3 15.4 %shard_map.74 = bf16[16,512]{1,0:T(8,128)(2,1)S(1)} custom-call(bf16[8,1024]{1,0:T(8,128)(2,1)S(1)} %bitcast.17, bf16[1024,512]{1,0:T(8,128)(2,1)S(1)} %copy-done, bf16[16,512]{1,0:T(8,128)(2,1)S(1)} %copy-done.1), custom_call_target="tpu_custom_call" | custom-call | tf_op jit(solution)/shard_map/pallas_call | solution.py:316
  43.7 0.6 %copy.23 = bf16[16,512]{1,0:T(8,128)(2,1)} copy(bf16[16,512]{1,0:T(8,128)(2,1)S(1)} %shard_map.74) | data formatting | bytes 32768
  (8 shorter events, 0.1 us)
Async XLA Ops:
  26.9 1.4 %copy-start = (bf16[1024,512]{1,0:T(8,128)(2,1)S(1)}, bf16[1024,512]{1,0:T(8,128)(2,1)}, u32[]{:S(2)}) copy-start(bf16[1024,512]{1,0:T(8,128)(2,1)} %w_hbm.3) | copy-start | bytes 3145732
  26.9 1.4 %copy-start.1 = (bf16[16,512]{1,0:T(8,128)(2,1)S(1)}, bf16[16,512]{1,0:T(8,128)(2,1)}, u32[]{:S(2)}) copy-start(bf16[16,512]{1,0:T(8,128)(2,1)} %s_ref.1) | copy-start | bytes 49156

commit v19 on v17

--- a/solution.py
+++ b/solution.py
@@ -272,12 +272,9 @@
     )
 
 
-def output_kernel(req_n, head_n, a_ref, w_hbm, s_ref, o_ref, w_ref, att_buf, part, sums_buf,
-                  sems, w_sem):
+def output_kernel(req_n, head_n, a_ref, w_ref, s_ref, o_ref, att_buf, part, sums_buf, sems):
     me_head = lax.axis_index("head")
     me_req = lax.axis_index("req")
-    w_copy = pltpu.make_async_copy(w_hbm, w_ref, w_sem)
-    w_copy.start()
     req_peers = ordered_peers(me_req, ((req_n // 4, 1), (2, 2), (2, 0.5)))
     head_peers = ordered_peers(me_head, ((head_n // 2, 1), (2, 1)))
     greet((("req", req_peers), ("head", head_peers)))
@@ -288,7 +285,6 @@
     every = jnp.concatenate(
         [att_buf[s].astype(jnp.float32) for s in range(req_n)], axis=0
     ).astype(jnp.bfloat16)
-    w_copy.wait()
     part[...] = jnp.dot(every, w_ref[...], preferred_element_type=jnp.float32)
     rows = o_ref.shape[0]
     chunk = lambda peer: part.at[pl.ds(pl.multiple_of(peer * rows, rows), rows)]
@@ -307,19 +303,14 @@
     return pl.pallas_call(
         functools.partial(output_kernel, req_n, head_n),
         out_shape=jax.ShapeDtypeStruct((rows, columns), hidden_in.dtype),
-        in_specs=[
-            pl.BlockSpec(memory_space=pltpu.VMEM),
-            pl.BlockSpec(memory_space=pl.ANY),
-            pl.BlockSpec(memory_space=pltpu.VMEM),
-        ],
+        in_specs=[pl.BlockSpec(memory_space=pltpu.VMEM)] * 3,
         out_specs=pl.BlockSpec(memory_space=pltpu.VMEM),
         scratch_shapes=[
-            pltpu.VMEM(w_out.shape, w_out.dtype),
             pltpu.VMEM((req_n, count, width), attended.dtype),
             pltpu.VMEM((head_n * rows, columns), jnp.float32),
             pltpu.VMEM((head_n, rows, columns), jnp.float32),
             pltpu.SemaphoreType.DMA((4, max(req_n, head_n))),
-            pltpu.SemaphoreType.DMA(()),
+
         ],
         compiler_params=pltpu.CompilerParams(
             collective_id=1, has_side_effects=True, vmem_limit_bytes=12 * 1024 * 1024

time: 43.3 us -> 43.3 us (level)
  no operation moved by 1% of the time
where the time goes in v19:
time: 43.3 us; the launch traced here: 42.8 us
  Pallas kernels  37 us (85%)
  matrix products  3.84 us (9%)
  other arithmetic  1.31 us (3%)
  local copies, waits for them, and re-layouts  0.63 us (1%)
    pallas_call x1, Pallas kernels, project(): pl.pallas_call(functools.partial(project_kernel, req_n, head_n), out_shap...  23.3 us
    pallas_call x1, Pallas kernels, output_block(): pl.pallas_call(functools.partial(output_kernel, req_n, head_n), out_shape...  13.7 us
    dot_general x1, matrix products, attend_padded(): jnp.einsum('rkgd,rpkd->rkgp', queries, cached_keys, preferred_element_typ...  2.35 us
    dot_general x1, matrix products, attend_padded(): jnp.einsum('rkgp,rpkd->rkgd', probs, cached_values, preferred_element_typ...  1.36 us

profile of v19, /device:TPU:1, one launch (start us, length us, event | category | flops | bytes accessed | tf_op | source)
XLA Modules:
  0.0 42.8 jit_solution(4312649244028583797)
XLA Ops:
  0.0 0.7 %convert_element_type.25 = f32[8]{0:T(128)S(1)} convert(s32[8]{0:T(128)} %len_ref.1) | non-fusion elementwise | flops 8 | bytes 64 | tf_op jit(solution)/shard_map/convert_element_type | solution.py:234
  0.7 0.1 fusion.14
  0.8 0.1 pad_maximum_fusion
  0.9 23.3 %shard_map.73 = (f32[8,8,128]{2,1,0:T(8,128)S(1)}, bf16[8,128]{1,0:T(8,128)(2,1)S(1)}, bf16[8,128]{1,0:T(8,128)(2,1)S(1)}, s32[8,4096]{1,0:T(8,128)S(1)}, bf16[8...) custom-call(bf16[16,512]{1,0:T(8,128)(2,1)} %s_ref.1, bf16[512]{0:T(512)(128)(2,1)} %gain_hbm.1, ...), custom_call_target="tpu_custom_call" | custom-call | tf_op jit(solution)/shard_map/pallas_call | solution.py:237
  24.2 2.4 %fusion.16 = (f32[8,8]{1,0:T(8,128)S(1)}, f32[8,8,4096]{2,1,0:T(8,128)S(1)}) fusion(bf16[8,4096,128]{2,1,0:T(8,128)(2,1)S(1)} %get-tuple-element.13, bf16[8,8,128]{2,0,1:T(8,128)(2,1)S(1)} %convert_bitcast_fusion, pred[8,4096]{1,0:T(8,128)(4,1)S(1)} %broadcast_compare_fusion), kind=kOutput, calls=%fused_computation.32 | convolution fusion | flops 67895232 | bytes 9486592 | tf_op jit(solution)/shard_map/rkgd,rpkd->rkgp/dot_general | solution.py:45
  26.5 0.1 fusion.8
  26.7 0.4 fusion.3
  27.1 0.0 copy-start
  27.1 0.0 copy-start.1
  27.1 1.4 %fusion.2 = bf16[1,8,8,128]{3,2,1,0:T(8,128)(2,1)S(1)} fusion(bf16[8,4096,128]{2,1,0:T(8,128)(2,1)S(1)} %get-tuple-element.15, f32[8,8,4096]{2,1,0:T(8,128)S(1)} %get-tuple-element.23, f32[8,8]{1,0:T(8,128)S(1)} %get-tuple-element.18, f32[8,8]{1,0:T(8,128)S(1)} %multiply_maximum_fusion, pred[8,4096]{1,0:T(8,128)(4,1)S(1)} %broadcast_compare_fusion, ...), kind=kOutput, calls=%fused_computation.4 | convolution fusion | flops 68182016 | bytes 9491200 | tf_op jit(solution)/shard_map/rkgp,rpkd->rkgd/dot_general | solution.py:56
  28.5 0.0 copy-done
  28.5 0.0 copy-done.1
  28.5 13.7 %shard_map.74 = bf16[16,512]{1,0:T(8,128)(2,1)S(1)} custom-call(bf16[8,1024]{1,0:T(8,128)(2,1)S(1)} %bitcast.17, bf16[1024,512]{1,0:T(8,128)(2,1)S(1)} %copy-done, bf16[16,512]{1,0:T(8,128)(2,1)S(1)} %copy-done.1), custom_call_target="tpu_custom_call" | custom-call | tf_op jit(solution)/shard_map/pallas_call | solution.py:303
  42.2 0.6 %copy.23 = bf16[16,512]{1,0:T(8,128)(2,1)} copy(bf16[16,512]{1,0:T(8,128)(2,1)S(1)} %shard_map.74) | data formatting | bytes 32768
  (8 shorter events, 0.1 us)
Async XLA Ops:
  27.1 1.4 %copy-start = (bf16[1024,512]{1,0:T(8,128)(2,1)S(1)}, bf16[1024,512]{1,0:T(8,128)(2,1)}, u32[]{:S(2)}) copy-start(bf16[1024,512]{1,0:T(8,128)(2,1)} %w_ref.1) | copy-start | bytes 3145732
  27.1 1.4 %copy-start.1 = (bf16[16,512]{1,0:T(8,128)(2,1)S(1)}, bf16[16,512]{1,0:T(8,128)(2,1)}, u32[]{:S(2)}) copy-start(bf16[16,512]{1,0:T(8,128)(2,1)} %s_ref.1) | copy-start | bytes 49156

commit v20 on v17

--- a/solution.py
+++ b/solution.py
@@ -173,7 +173,6 @@
     )
     pair.start()
     pair.wait()
-    mixed[...] = part[me_core] + pair_buf[...]
     z_n = chips // 2
     me_z, me_x = me_chip // 2, lax.rem(me_chip, 2)
     offsets = sorted(
@@ -183,6 +182,7 @@
     sends = []
     for k, (dz, dx) in enumerate(offsets, start=1):
         chip = lax.rem(me_z + dz, z_n) * 2 + lax.rem(me_x + dx, 2)
+        mixed[chip] = part[me_core, chip] + pair_buf[chip]
         copy = pltpu.make_async_remote_copy(
             src_ref=mixed.at[chip],
             dst_ref=sums_buf.at[me_chip],
@@ -206,7 +206,7 @@
         arrival.wait_recv()
     for copy in sends:
         copy.wait_send()
-    total = mixed[me_chip]
+    total = part[me_core, me_chip] + pair_buf[me_chip]
     for k in range(1, chips):
         total = total + sums_buf[lax.rem(me_chip + chips - k, chips)]
     mean_square = total[:, columns:columns + 1] / D

time: 43.3 us -> 43.3 us (level)
  no operation moved by 1% of the time
where the time goes in v20:
time: 43.3 us; the launch traced here: 43 us
  Pallas kernels  37.1 us (86%)
  matrix products  3.84 us (9%)
  other arithmetic  1.31 us (3%)
  local copies, waits for them, and re-layouts  0.63 us (1%)
    pallas_call x1, Pallas kernels, project(): pl.pallas_call(functools.partial(project_kernel, req_n, head_n), out_shap...  23.2 us
    pallas_call x1, Pallas kernels, output_block(): pl.pallas_call(functools.partial(output_kernel, req_n, head_n), out_shape...  13.9 us
    dot_general x1, matrix products, attend_padded(): jnp.einsum('rkgd,rpkd->rkgp', queries, cached_keys, preferred_element_typ...  2.35 us
    dot_general x1, matrix products, attend_padded(): jnp.einsum('rkgp,rpkd->rkgd', probs, cached_values, preferred_element_typ...  1.36 us

profile of v20, /device:TPU:1, one launch (start us, length us, event | category | flops | bytes accessed | tf_op | source)
XLA Modules:
  0.0 43.0 jit_solution(16879107224439473349)
XLA Ops:
  0.0 0.7 %convert_element_type.25 = f32[8]{0:T(128)S(1)} convert(s32[8]{0:T(128)} %len_ref.1) | non-fusion elementwise | flops 8 | bytes 64 | tf_op jit(solution)/shard_map/convert_element_type | solution.py:234
  0.7 0.1 fusion.14
  0.8 0.1 pad_maximum_fusion
  0.9 23.2 %shard_map.73 = (f32[8,8,128]{2,1,0:T(8,128)S(1)}, bf16[8,128]{1,0:T(8,128)(2,1)S(1)}, bf16[8,128]{1,0:T(8,128)(2,1)S(1)}, s32[8,4096]{1,0:T(8,128)S(1)}, bf16[8...) custom-call(bf16[16,512]{1,0:T(8,128)(2,1)} %s_ref.1, bf16[512]{0:T(512)(128)(2,1)} %gain_hbm.1, ...), custom_call_target="tpu_custom_call" | custom-call | tf_op jit(solution)/shard_map/pallas_call | solution.py:237
  24.2 2.4 %fusion.16 = (f32[8,8]{1,0:T(8,128)S(1)}, f32[8,8,4096]{2,1,0:T(8,128)S(1)}) fusion(bf16[8,4096,128]{2,1,0:T(8,128)(2,1)S(1)} %get-tuple-element.13, bf16[8,8,128]{2,0,1:T(8,128)(2,1)S(1)} %convert_bitcast_fusion, pred[8,4096]{1,0:T(8,128)(4,1)S(1)} %broadcast_compare_fusion), kind=kOutput, calls=%fused_computation.32 | convolution fusion | flops 67895232 | bytes 9486592 | tf_op jit(solution)/shard_map/rkgd,rpkd->rkgp/dot_general | solution.py:45
  26.5 0.1 fusion.8
  26.6 0.4 fusion.3
  27.1 0.0 copy-start
  27.1 0.0 copy-start.1
  27.1 1.4 %fusion.2 = bf16[1,8,8,128]{3,2,1,0:T(8,128)(2,1)S(1)} fusion(bf16[8,4096,128]{2,1,0:T(8,128)(2,1)S(1)} %get-tuple-element.15, f32[8,8,4096]{2,1,0:T(8,128)S(1)} %get-tuple-element.23, f32[8,8]{1,0:T(8,128)S(1)} %get-tuple-element.18, f32[8,8]{1,0:T(8,128)S(1)} %multiply_maximum_fusion, pred[8,4096]{1,0:T(8,128)(4,1)S(1)} %broadcast_compare_fusion, ...), kind=kOutput, calls=%fused_computation.4 | convolution fusion | flops 68182016 | bytes 9491200 | tf_op jit(solution)/shard_map/rkgp,rpkd->rkgd/dot_general | solution.py:56
  28.5 0.0 copy-done
  28.5 0.0 copy-done.1
  28.5 13.9 %shard_map.74 = bf16[16,512]{1,0:T(8,128)(2,1)S(1)} custom-call(bf16[8,1024]{1,0:T(8,128)(2,1)S(1)} %bitcast.17, bf16[1024,512]{1,0:T(8,128)(2,1)S(1)} %copy-done, bf16[16,512]{1,0:T(8,128)(2,1)S(1)} %copy-done.1), custom_call_target="tpu_custom_call" | custom-call | tf_op jit(solution)/shard_map/pallas_call | solution.py:307
  42.4 0.6 %copy.23 = bf16[16,512]{1,0:T(8,128)(2,1)} copy(bf16[16,512]{1,0:T(8,128)(2,1)S(1)} %shard_map.74) | data formatting | bytes 32768
  (8 shorter events, 0.1 us)
Async XLA Ops:
  27.1 1.4 %copy-start = (bf16[1024,512]{1,0:T(8,128)(2,1)S(1)}, bf16[1024,512]{1,0:T(8,128)(2,1)}, u32[]{:S(2)}) copy-start(bf16[1024,512]{1,0:T(8,128)(2,1)} %w_hbm.3) | copy-start | bytes 3145732
  27.1 1.4 %copy-start.1 = (bf16[16,512]{1,0:T(8,128)(2,1)S(1)}, bf16[16,512]{1,0:T(8,128)(2,1)}, u32[]{:S(2)}) copy-start(bf16[16,512]{1,0:T(8,128)(2,1)} %s_ref.1) | copy-start | bytes 49156

commit v21 on v17

--- a/solution.py
+++ b/solution.py
@@ -154,15 +154,21 @@
     columns = w_ref.shape[1]
     square = jnp.sum(states * states, axis=1, keepdims=True)
     w_copy.wait()
-    packed = jnp.concatenate(
-        [jnp.dot(scaled, w_ref[...], preferred_element_type=jnp.float32),
-         jnp.broadcast_to(square, (square.shape[0], part.shape[-1] - columns))],
-        axis=1,
-    )
     count = k_ref.shape[0]
-    packed = packed.reshape(chips, 2, count, part.shape[-1])
-    part[0] = packed[:, 0]
-    part[1] = packed[:, 1]
+    scaled = scaled.reshape(chips, 2, count, scaled.shape[-1])
+    square = square.reshape(chips, 2, count, 1)
+
+    def half_rows(core):
+        pick = lambda x: jnp.where(core == 0, x[:, 0], x[:, 1]).reshape(chips * count, x.shape[-1])
+        squares = pick(square)
+        packed = jnp.concatenate(
+            [jnp.dot(pick(scaled), w_ref[...], preferred_element_type=jnp.float32),
+             jnp.broadcast_to(squares, (squares.shape[0], part.shape[-1] - columns))],
+            axis=1,
+        )
+        part[core] = packed.reshape(chips, count, part.shape[-1])
+
+    half_rows(1 - me_core)
     pair = pltpu.make_async_remote_copy(
         src_ref=part.at[1 - me_core],
         dst_ref=pair_buf,
@@ -172,6 +178,7 @@
         device_id_type=pl.DeviceIdType.MESH,
     )
     pair.start()
+    half_rows(me_core)
     pair.wait()
     mixed[...] = part[me_core] + pair_buf[...]
     z_n = chips // 2

time: 43.3 us -> 43.4 us (level)
  no operation moved by 1% of the time
where the time goes in v21:
time: 43.4 us; the launch traced here: 42.9 us
  Pallas kernels  37.1 us (85%)
  matrix products  3.84 us (9%)
  other arithmetic  1.31 us (3%)
  local copies, waits for them, and re-layouts  0.63 us (1%)
    pallas_call x1, Pallas kernels, project(): pl.pallas_call(functools.partial(project_kernel, req_n, head_n), out_shap...  23.3 us
    pallas_call x1, Pallas kernels, output_block(): pl.pallas_call(functools.partial(output_kernel, req_n, head_n), out_shape...  13.8 us
    dot_general x1, matrix products, attend_padded(): jnp.einsum('rkgd,rpkd->rkgp', queries, cached_keys, preferred_element_typ...  2.35 us
    dot_general x1, matrix products, attend_padded(): jnp.einsum('rkgp,rpkd->rkgd', probs, cached_values, preferred_element_typ...  1.36 us

profile of v21, /device:TPU:1, one launch (start us, length us, event | category | flops | bytes accessed | tf_op | source)
XLA Modules:
  0.0 42.9 jit_solution(4081275896812359408)
XLA Ops:
  0.0 0.7 %convert_element_type.25 = f32[8]{0:T(128)S(1)} convert(s32[8]{0:T(128)} %len_ref.1) | non-fusion elementwise | flops 8 | bytes 64 | tf_op jit(solution)/shard_map/convert_element_type | solution.py:241
  0.7 0.1 fusion.14
  0.8 0.1 pad_maximum_fusion
  0.9 23.3 %shard_map.73 = (f32[8,8,128]{2,1,0:T(8,128)S(1)}, bf16[8,128]{1,0:T(8,128)(2,1)S(1)}, bf16[8,128]{1,0:T(8,128)(2,1)S(1)}, s32[8,4096]{1,0:T(8,128)S(1)}, bf16[8...) custom-call(bf16[16,512]{1,0:T(8,128)(2,1)} %s_ref.1, bf16[512]{0:T(512)(128)(2,1)} %gain_hbm.1, ...), custom_call_target="tpu_custom_call" | custom-call | tf_op jit(solution)/shard_map/pallas_call | solution.py:244
  24.2 2.4 %fusion.16 = (f32[8,8]{1,0:T(8,128)S(1)}, f32[8,8,4096]{2,1,0:T(8,128)S(1)}) fusion(bf16[8,4096,128]{2,1,0:T(8,128)(2,1)S(1)} %get-tuple-element.13, bf16[8,8,128]{2,0,1:T(8,128)(2,1)S(1)} %convert_bitcast_fusion, pred[8,4096]{1,0:T(8,128)(4,1)S(1)} %broadcast_compare_fusion), kind=kOutput, calls=%fused_computation.32 | convolution fusion | flops 67895232 | bytes 9486592 | tf_op jit(solution)/shard_map/rkgd,rpkd->rkgp/dot_general | solution.py:45
  26.6 0.1 fusion.8
  26.7 0.4 fusion.3
  27.1 0.0 copy-start
  27.1 0.0 copy-start.1
  27.1 1.4 %fusion.2 = bf16[1,8,8,128]{3,2,1,0:T(8,128)(2,1)S(1)} fusion(bf16[8,4096,128]{2,1,0:T(8,128)(2,1)S(1)} %get-tuple-element.15, f32[8,8,4096]{2,1,0:T(8,128)S(1)} %get-tuple-element.23, f32[8,8]{1,0:T(8,128)S(1)} %get-tuple-element.18, f32[8,8]{1,0:T(8,128)S(1)} %multiply_maximum_fusion, pred[8,4096]{1,0:T(8,128)(4,1)S(1)} %broadcast_compare_fusion, ...), kind=kOutput, calls=%fused_computation.4 | convolution fusion | flops 68182016 | bytes 9491200 | tf_op jit(solution)/shard_map/rkgp,rpkd->rkgd/dot_general | solution.py:56
  28.5 0.0 copy-done
  28.5 0.0 copy-done.1
  28.5 13.8 %shard_map.74 = bf16[16,512]{1,0:T(8,128)(2,1)S(1)} custom-call(bf16[8,1024]{1,0:T(8,128)(2,1)S(1)} %bitcast.17, bf16[1024,512]{1,0:T(8,128)(2,1)S(1)} %copy-done, bf16[16,512]{1,0:T(8,128)(2,1)S(1)} %copy-done.1), custom_call_target="tpu_custom_call" | custom-call | tf_op jit(solution)/shard_map/pallas_call | solution.py:314
  42.3 0.6 %copy.23 = bf16[16,512]{1,0:T(8,128)(2,1)} copy(bf16[16,512]{1,0:T(8,128)(2,1)S(1)} %shard_map.74) | data formatting | bytes 32768
  (8 shorter events, 0.1 us)
Async XLA Ops:
  27.1 1.4 %copy-start = (bf16[1024,512]{1,0:T(8,128)(2,1)S(1)}, bf16[1024,512]{1,0:T(8,128)(2,1)}, u32[]{:S(2)}) copy-start(bf16[1024,512]{1,0:T(8,128)(2,1)} %w_hbm.3) | copy-start | bytes 3145732
  27.1 1.4 %copy-start.1 = (bf16[16,512]{1,0:T(8,128)(2,1)S(1)}, bf16[16,512]{1,0:T(8,128)(2,1)}, u32[]{:S(2)}) copy-start(bf16[16,512]{1,0:T(8,128)(2,1)} %s_ref.1) | copy-start | bytes 49156

commit v22 on v17

--- a/solution.py
+++ b/solution.py
@@ -298,7 +298,7 @@
     total = part[pl.ds(pl.multiple_of(me_head * rows, rows), rows), :]
     for k in range(1, head_n):
         total = total + sums_buf[lax.rem(me_head + head_n - k, head_n)]
-    o_ref[...] = (s_ref[...].astype(jnp.float32) + total).astype(o_ref.dtype)
+    o_ref[...] = total
 
 
 def output_block(attended, w_out, hidden_in, req_n, head_n):
@@ -306,7 +306,7 @@
     rows, columns = hidden_in.shape
     return pl.pallas_call(
         functools.partial(output_kernel, req_n, head_n),
-        out_shape=jax.ShapeDtypeStruct((rows, columns), hidden_in.dtype),
+        out_shape=jax.ShapeDtypeStruct((rows, columns), jnp.float32),
         in_specs=[
             pl.BlockSpec(memory_space=pltpu.VMEM),
             pl.BlockSpec(memory_space=pl.ANY),
@@ -344,7 +344,8 @@
         queries, new_keys, new_values, cached_keys, cached_values, inside != 0, factor
     )
     flat_rows = attended.reshape(own_count, local_heads * GROUP * HD)
-    return output_block(flat_rows, w_out, hidden_in, req_n, head_n)
+    output = output_block(flat_rows, w_out, hidden_in, req_n, head_n)
+    return (hidden_in.astype(jnp.float32) + output).astype(jnp.bfloat16)
 
 
 def solution(mesh):

time: 43.3 us -> 43.3 us (level)
  local copies, waits for them, and re-layouts: 0.63 us -> 0.02 us
  other arithmetic: 1.31 us -> 1.92 us
    convert_element_type x0 -> x1, other arithmetic: none -> 0.61 us  [local(): return (hidden_in.astype(jnp.float32) + output).astype(jnp.bfloat16)]
    unnamed x6 -> x5, local copies, waits for them, and re-layouts: 0.63 us -> 0.02 us
where the time goes in v22:
time: 43.3 us; the launch traced here: 42.9 us
  Pallas kernels  37 us (85%)
  matrix products  3.84 us (9%)
  other arithmetic  1.92 us (4%)
    pallas_call x1, Pallas kernels, project(): pl.pallas_call(functools.partial(project_kernel, req_n, head_n), out_shap...  23.3 us
    pallas_call x1, Pallas kernels, output_block(): pl.pallas_call(functools.partial(output_kernel, req_n, head_n), out_shape...  13.8 us
    dot_general x1, matrix products, attend_padded(): jnp.einsum('rkgd,rpkd->rkgp', queries, cached_keys, preferred_element_typ...  2.35 us
    dot_general x1, matrix products, attend_padded(): jnp.einsum('rkgp,rpkd->rkgd', probs, cached_values, preferred_element_typ...  1.36 us

profile of v22, /device:TPU:1, one launch (start us, length us, event | category | flops | bytes accessed | tf_op | source)
XLA Modules:
  0.0 42.9 jit_solution(6424737765596196173)
XLA Ops:
  0.0 0.7 %convert_element_type.32 = f32[8]{0:T(128)S(1)} convert(s32[8]{0:T(128)} %len_ref.1) | non-fusion elementwise | flops 8 | bytes 64 | tf_op jit(solution)/shard_map/convert_element_type | solution.py:234
  0.7 0.1 fusion.14
  0.8 0.1 pad_maximum_fusion
  0.9 23.3 %shard_map.73 = (f32[8,8,128]{2,1,0:T(8,128)S(1)}, bf16[8,128]{1,0:T(8,128)(2,1)S(1)}, bf16[8,128]{1,0:T(8,128)(2,1)S(1)}, s32[8,4096]{1,0:T(8,128)S(1)}, bf16[8...) custom-call(bf16[16,512]{1,0:T(8,128)(2,1)} %s_ref.1, bf16[512]{0:T(512)(128)(2,1)} %gain_hbm.1, ...), custom_call_target="tpu_custom_call" | custom-call | tf_op jit(solution)/shard_map/pallas_call | solution.py:237
  24.2 2.4 %fusion.16 = (f32[8,8]{1,0:T(8,128)S(1)}, f32[8,8,4096]{2,1,0:T(8,128)S(1)}) fusion(bf16[8,4096,128]{2,1,0:T(8,128)(2,1)S(1)} %get-tuple-element.13, bf16[8,8,128]{2,0,1:T(8,128)(2,1)S(1)} %convert_bitcast_fusion, pred[8,4096]{1,0:T(8,128)(4,1)S(1)} %broadcast_compare_fusion), kind=kOutput, calls=%fused_computation.33 | convolution fusion | flops 67895232 | bytes 9486592 | tf_op jit(solution)/shard_map/rkgd,rpkd->rkgp/dot_general | solution.py:45
  26.5 0.1 fusion.8
  26.7 0.4 fusion.3
  27.1 0.0 copy-start
  27.1 0.0 copy-start.1
  27.1 1.4 %fusion.2 = bf16[1,8,8,128]{3,2,1,0:T(8,128)(2,1)S(1)} fusion(bf16[8,4096,128]{2,1,0:T(8,128)(2,1)S(1)} %get-tuple-element.15, f32[8,8,4096]{2,1,0:T(8,128)S(1)} %get-tuple-element.23, f32[8,8]{1,0:T(8,128)S(1)} %get-tuple-element.18, f32[8,8]{1,0:T(8,128)S(1)} %multiply_maximum_fusion, pred[8,4096]{1,0:T(8,128)(4,1)S(1)} %broadcast_compare_fusion, ...), kind=kOutput, calls=%fused_computation.4 | convolution fusion | flops 68182016 | bytes 9491200 | tf_op jit(solution)/shard_map/rkgp,rpkd->rkgd/dot_general | solution.py:56
  28.5 0.0 copy-done
  28.5 0.0 copy-done.1
  28.5 13.8 %shard_map.74 = f32[16,512]{1,0:T(8,128)S(1)} custom-call(bf16[8,1024]{1,0:T(8,128)(2,1)S(1)} %bitcast.17, bf16[1024,512]{1,0:T(8,128)(2,1)S(1)} %copy-done, bf16[16,512]{1,0:T(8,128)(2,1)S(1)} %copy-done.1), custom_call_target="tpu_custom_call" | custom-call | tf_op jit(solution)/shard_map/pallas_call | solution.py:307
  42.3 0.6 %add_convert_fusion = bf16[16,512]{1,0:T(8,128)(2,1)} fusion(f32[16,512]{1,0:T(8,128)S(1)} %shard_map.74, bf16[16,512]{1,0:T(8,128)(2,1)S(1)} %copy-done.1), kind=kLoop, calls=%fused_computation.13 | loop fusion | flops 24576 | bytes 65536 | tf_op jit(solution)/shard_map/convert_element_type | solution.py:348
  (8 shorter events, 0.1 us)
Async XLA Ops:
  27.1 1.4 %copy-start = (bf16[1024,512]{1,0:T(8,128)(2,1)S(1)}, bf16[1024,512]{1,0:T(8,128)(2,1)}, u32[]{:S(2)}) copy-start(bf16[1024,512]{1,0:T(8,128)(2,1)} %w_hbm.3) | copy-start | bytes 3145732
  27.1 1.4 %copy-start.1 = (bf16[16,512]{1,0:T(8,128)(2,1)S(1)}, bf16[16,512]{1,0:T(8,128)(2,1)}, u32[]{:S(2)}) copy-start(bf16[16,512]{1,0:T(8,128)(2,1)} %s_ref.1) | copy-start | bytes 49156
